TPU v7x, 32 devices: a whole 2x2x4 slice. The times are simulated.
32 devices in a mesh: rep: 8 (over z, core), fsdp: 4 (over y, x).
Axes of the slice: x: 2, y: 2, z: 4, core: 2. Of those that a mesh axis runs over, the one named last changes fastest.
Arguments:
- hidden_in: bfloat16 [10240, 1536], P(('rep', 'fsdp')), may hold values from -6 to 6
- out_grad: bfloat16 [10240, 1536], P(('rep', 'fsdp')), may hold values from -6 to 6
- doc_lengths: int32 [8, 8], P('rep'), may hold values from 1 to 1024, 1280 in all within a row
- piece_starts: int32 [8, 2], P('rep'), may hold values from 0 to 1024, as said below
- w_query: bfloat16 [1536, 1536], P('fsdp'), may hold values from -0.15625 to 0.15625
- b_query: bfloat16 [1536], P('fsdp'), may hold values from -3 to 3
- w_key: bfloat16 [1536, 256], P('fsdp'), may hold values from -0.15625 to 0.15625
- b_key: bfloat16 [256], P('fsdp'), may hold values from -3 to 3
- w_value: bfloat16 [1536, 256], P('fsdp'), may hold values from -0.15625 to 0.15625
- b_value: bfloat16 [256], P('fsdp'), may hold values from -3 to 3
- w_output: bfloat16 [1536, 1536], P('fsdp'), may hold values from -0.625 to 0.625
- gain_attn: bfloat16 [1536], P('fsdp'), may hold values from 0.5 to 1.5
- w_gate: bfloat16 [1536, 8960], P('fsdp'), may hold values from -0.15625 to 0.15625
- w_up: bfloat16 [1536, 8960], P('fsdp'), may hold values from -0.15625 to 0.15625
- w_down: bfloat16 [8960, 1536], P('fsdp'), may hold values from -0.0625 to 0.0625
- gain_mlp: bfloat16 [1536], P('fsdp'), may hold values from 0.5 to 1.5
Outputs:
- output: float32 [10240, 1536], P(('rep', 'fsdp'))
- grad_input: float32 [10240, 1536], P(('rep', 'fsdp'))
- grad_w_query: float32 [1536, 1536], P('fsdp')
- grad_b_query: float32 [1536], P('fsdp')
- grad_w_key: float32 [1536, 256], P('fsdp')
- grad_b_key: float32 [256], P('fsdp')
- grad_w_value: float32 [1536, 256], P('fsdp')
- grad_b_value: float32 [256], P('fsdp')
- grad_w_output: float32 [1536, 1536], P('fsdp')
- grad_gain_attn: float32 [1536], P('fsdp')
- grad_w_gate: float32 [1536, 8960], P('fsdp')
- grad_w_up: float32 [1536, 8960], P('fsdp')
- grad_w_down: float32 [8960, 1536], P('fsdp')
- grad_gain_mlp: float32 [1536], P('fsdp')
Inputs may be any that keep to these rules, and one draw needn't show every extreme that they name: `doc_lengths`: each row's 8 lengths sum to 1280, and the longest is exactly 1024. `piece_starts`: in each row the starts rise by 256 or more from piece to piece, so pieces never intersect; a piece may run over a document's end.
All inputs are finite; a program needn't handle non-finite values.
Results may differ from a plain program's by a relative error of at most 0.028.
Values may be sent and summed in bfloat16 or wider, within the bound.
A program may use at most 576 MiB of HBM per device.

v0:
```python
import jax
import jax.numpy as jnp
from jax import lax
from jax.sharding import PartitionSpec as P

HEADS = 12
KVH = 2
HDIM = 128
PIECE = 256


epsilon = 1e-06
rope_base = 1000000.0


def row_layout(positions, lengths, starts, piece_len):
    doc_ends = jnp.cumsum(lengths)
    passed = positions[:, None] >= doc_ends[None, :]
    doc_ids = jnp.sum(passed.astype(jnp.int32), axis=1, dtype=jnp.int32)
    offsets = jnp.sum(jnp.where(passed, lengths[None, :], 0), axis=1, dtype=jnp.int32)
    inside = (positions[:, None] >= starts[None, :]) & (
        positions[:, None] < starts[None, :] + piece_len
    )
    labels = jnp.arange(1, starts.shape[0] + 1, dtype=jnp.int32)
    piece_ids = jnp.sum(jnp.where(inside, labels[None, :], 0), axis=1, dtype=jnp.int32)
    return (doc_ids, positions - offsets, piece_ids)


def visible_pairs(query_doc, query_pos, query_piece, key_doc, key_pos, key_piece):
    same_doc = query_doc[:, None] == key_doc[None, :]
    causal = key_pos[None, :] <= query_pos[:, None]
    same_piece = (query_piece[:, None] == key_piece[None, :]) & (query_piece[:, None] > 0)
    return same_doc & (causal | same_piece)


def rope_tables(relative, head_dim):
    halves = jnp.arange(0, head_dim, 2).astype(jnp.float32) / head_dim
    inverse = rope_base ** (-halves)
    angles = relative.astype(jnp.float32)[:, None] * inverse[None, :]
    angles = jnp.concatenate([angles, angles], axis=1)
    return (jnp.cos(angles), jnp.sin(angles))


def rotate(values, cosine, sine):
    half_dim = values.shape[-1] // 2
    turned = jnp.concatenate([-values[..., half_dim:], values[..., :half_dim]], axis=-1)
    return values * cosine[:, None, :] + turned * sine[:, None, :]


def unrotate(grads, cosine, sine):
    half_dim = grads.shape[-1] // 2
    spun = grads * sine[:, None, :]
    turned_back = jnp.concatenate([spun[..., half_dim:], -spun[..., :half_dim]], axis=-1)
    return grads * cosine[:, None, :] + turned_back


def mat_dot(left, right):
    return jnp.dot(left, right, preferred_element_type=jnp.float32)


def dot_right_t(left, right):
    return lax.dot_general(
        left, right, (((1,), (1,)), ((), ())), preferred_element_type=jnp.float32
    )


def dot_left_t(left, right):
    return lax.dot_general(
        left, right, (((0,), (0,)), ((), ())), preferred_element_type=jnp.float32
    )


def local(
    hidden_in,
    out_grad,
    doc_lengths,
    piece_starts,
    w_query,
    b_query,
    w_key,
    b_key,
    w_value,
    b_value,
    w_output,
    gain_attn,
    w_gate,
    w_up,
    w_down,
    gain_mlp,
):
    tok_rows = hidden_in.shape[0]
    model_width = hidden_in.shape[1]
    shard_count = lax.axis_size("fsdp")
    row_len = tok_rows * shard_count
    group_size = HEADS // KVH
    kv_width = KVH * HDIM
    ff_width = w_gate.shape[1]
    score_scale = 1.0 / HDIM**0.5
    local_pos = lax.axis_index("fsdp") * tok_rows + jnp.arange(tok_rows, dtype=jnp.int32)
    row_pos = jnp.arange(row_len, dtype=jnp.int32)
    lengths = doc_lengths[0]
    starts = piece_starts[0]
    query_doc, query_rel, query_piece = row_layout(local_pos, lengths, starts, PIECE)
    key_doc, unused_rel, key_piece = row_layout(row_pos, lengths, starts, PIECE)
    allowed = visible_pairs(query_doc, local_pos, query_piece, key_doc, row_pos, key_piece)
    cosine, sine = rope_tables(query_rel, HDIM)
    (
        query_full,
        key_full,
        value_full,
        output_full,
        query_bias,
        key_bias,
        value_bias,
        attn_gain,
        mlp_gain,
    ) = (
        lax.all_gather(w_query, "fsdp", axis=0, tiled=True),
        lax.all_gather(w_key, "fsdp", axis=0, tiled=True),
        lax.all_gather(w_value, "fsdp", axis=0, tiled=True),
        lax.all_gather(w_output, "fsdp", axis=0, tiled=True),
        lax.all_gather(b_query, "fsdp", axis=0, tiled=True),
        lax.all_gather(b_key, "fsdp", axis=0, tiled=True),
        lax.all_gather(b_value, "fsdp", axis=0, tiled=True),
        lax.all_gather(gain_attn, "fsdp", axis=0, tiled=True),
        lax.all_gather(gain_mlp, "fsdp", axis=0, tiled=True),
    )
    x_float = hidden_in.astype(jnp.float32)
    inv_first = lax.rsqrt(jnp.mean(x_float * x_float, axis=1, keepdims=True) + epsilon)
    unit_first = x_float * inv_first
    gain_first = attn_gain.astype(jnp.float32)
    normed_first = (unit_first * gain_first).astype(jnp.bfloat16)
    query_pre = mat_dot(normed_first, query_full) + query_bias.astype(jnp.float32)
    key_pre = mat_dot(normed_first, key_full) + key_bias.astype(jnp.float32)
    value_pre = mat_dot(normed_first, value_full) + value_bias.astype(jnp.float32)
    query_rot = rotate(query_pre.reshape(tok_rows, HEADS, HDIM), cosine, sine).astype(jnp.bfloat16)
    key_rot = (
        rotate(key_pre.reshape(tok_rows, KVH, HDIM), cosine, sine)
        .astype(jnp.bfloat16)
        .reshape(tok_rows, kv_width)
    )
    value_low = value_pre.astype(jnp.bfloat16)
    keys_row, values_row = (
        lax.all_gather(key_rot, "fsdp", axis=0, tiled=True),
        lax.all_gather(value_low, "fsdp", axis=0, tiled=True),
    )
    query_grouped = query_rot.reshape(tok_rows, KVH, group_size, HDIM)
    keys_grouped = keys_row.reshape(row_len, KVH, HDIM)
    values_grouped = values_row.reshape(row_len, KVH, HDIM)

    def masked_scores():
        raw_scores = (
            jnp.einsum(
                "tgjd,rgd->gjtr", query_grouped, keys_grouped, preferred_element_type=jnp.float32
            )
            * score_scale
        )
        return jnp.where(allowed[None, None], raw_scores, -1e30)

    scores = masked_scores()
    row_peak = jnp.max(scores, axis=3, keepdims=True)
    expo_vals = jnp.exp(scores - row_peak)
    row_total = jnp.sum(expo_vals, axis=3, keepdims=True)
    soft_probs = expo_vals / row_total
    log_total = row_peak + jnp.log(row_total)
    attn_heads = jnp.einsum(
        "gjtr,rgd->tgjd",
        soft_probs.astype(jnp.bfloat16),
        values_grouped,
        preferred_element_type=jnp.float32,
    )
    attn_low = attn_heads.reshape(tok_rows, model_width).astype(jnp.bfloat16)
    mid_state = x_float + mat_dot(attn_low, output_full)
    inv_second = lax.rsqrt(jnp.mean(mid_state * mid_state, axis=1, keepdims=True) + epsilon)
    unit_second = mid_state * inv_second
    gain_second = mlp_gain.astype(jnp.float32)
    normed_second = (unit_second * gain_second).astype(jnp.bfloat16)
    cot_float = out_grad.astype(jnp.float32)
    pieces = (
        lax.all_gather(w_gate, "fsdp", axis=0, tiled=True),
        lax.all_gather(w_up, "fsdp", axis=0, tiled=True),
    )
    columns = normed_second
    gate_val = mat_dot(columns, pieces[0])
    up_val = mat_dot(columns, pieces[1])
    sig_gate = jax.nn.sigmoid(gate_val)
    silu_gate = gate_val * sig_gate
    act_low = (silu_gate * up_val).astype(jnp.bfloat16)
    columns = act_low
    mlp_out = mat_dot(columns, lax.all_gather(w_down, "fsdp", axis=0, tiled=True))
    d_act = dot_right_t(out_grad, lax.all_gather(w_down, "fsdp", axis=0, tiled=True))
    columns = act_low
    down_sums = lax.psum_scatter(
        dot_left_t(columns, out_grad).astype(jnp.bfloat16), "fsdp", scatter_dimension=0, tiled=True
    ).astype(jnp.float32)
    d_gate = (d_act * up_val * sig_gate * (1.0 + gate_val * (1.0 - sig_gate))).astype(jnp.bfloat16)
    d_up = (d_act * silu_gate).astype(jnp.bfloat16)
    pieces = (
        lax.all_gather(w_gate, "fsdp", axis=0, tiled=True),
        lax.all_gather(w_up, "fsdp", axis=0, tiled=True),
    )
    partial_value = dot_right_t(d_gate, pieces[0]) + dot_right_t(d_up, pieces[1])
    columns = normed_second
    mlp_sums = lax.psum_scatter(
        jnp.concatenate([dot_left_t(columns, d_gate), dot_left_t(columns, d_up)], axis=1).astype(
            jnp.bfloat16
        ),
        "fsdp",
        scatter_dimension=0,
        tiled=True,
    ).astype(jnp.float32)
    output = mid_state + mlp_out
    d_gain_second = jnp.sum(partial_value * unit_second, axis=0)
    scaled_second = partial_value * gain_second
    d_mid = cot_float + inv_second * (
        scaled_second - unit_second * jnp.mean(scaled_second * unit_second, axis=1, keepdims=True)
    )
    d_branch_low = d_mid.astype(jnp.bfloat16)
    d_attn_low = dot_right_t(d_branch_low, output_full).astype(jnp.bfloat16)
    d_attn_grouped = d_attn_low.reshape(tok_rows, KVH, group_size, HDIM)
    scores = masked_scores()
    soft_back = jnp.exp(scores - log_total)
    probs_low = soft_back.astype(jnp.bfloat16)
    prob_grad = jnp.einsum(
        "tgjd,rgd->gjtr", d_attn_grouped, values_grouped, preferred_element_type=jnp.float32
    )
    row_delta = jnp.sum(soft_back * prob_grad, axis=3, keepdims=True)
    score_grad = (soft_back * (prob_grad - row_delta)).astype(jnp.bfloat16)
    dquery_rot = (
        jnp.einsum("gjtr,rgd->tgjd", score_grad, keys_grouped, preferred_element_type=jnp.float32)
        * score_scale
    )
    dquery_low = (
        unrotate(dquery_rot.reshape(tok_rows, HEADS, HDIM), cosine, sine)
        .reshape(tok_rows, model_width)
        .astype(jnp.bfloat16)
    )
    key_grad = (
        jnp.einsum("gjtr,tgjd->rgd", score_grad, query_grouped, preferred_element_type=jnp.float32)
        * score_scale
    )
    value_grad = jnp.einsum(
        "gjtr,tgjd->rgd", probs_low, d_attn_grouped, preferred_element_type=jnp.float32
    )
    kv_sums = lax.psum_scatter(
        jnp.concatenate(
            [
                key_grad.reshape(lax.axis_size("fsdp") * tok_rows, kv_width),
                value_grad.reshape(lax.axis_size("fsdp") * tok_rows, kv_width),
            ],
            axis=1,
        ).astype(jnp.bfloat16),
        "fsdp",
        scatter_dimension=0,
        tiled=True,
    ).astype(jnp.float32)
    dkey_low = (
        unrotate(kv_sums[:, :kv_width].reshape(tok_rows, KVH, HDIM), cosine, sine)
        .reshape(tok_rows, kv_width)
        .astype(jnp.bfloat16)
    )
    dvalue_low = kv_sums[:, kv_width:].astype(jnp.bfloat16)
    d_norm_first = (
        dot_right_t(dquery_low, query_full)
        + dot_right_t(dkey_low, key_full)
        + dot_right_t(dvalue_low, value_full)
    )
    attn_sums = lax.psum_scatter(
        jnp.concatenate(
            [
                dot_left_t(normed_first, dquery_low),
                dot_left_t(normed_first, dkey_low),
                dot_left_t(normed_first, dvalue_low),
                dot_left_t(attn_low, d_branch_low),
            ],
            axis=1,
        ).astype(jnp.bfloat16),
        "fsdp",
        scatter_dimension=0,
        tiled=True,
    ).astype(jnp.float32)
    d_gain_first = jnp.sum(d_norm_first * unit_first, axis=0)
    scaled_first = d_norm_first * gain_first
    grad_input = d_mid + inv_first * (
        scaled_first - unit_first * jnp.mean(scaled_first * unit_first, axis=1, keepdims=True)
    )
    bias_query = jnp.sum(dquery_low.astype(jnp.float32), axis=0)
    bias_key = jnp.sum(dkey_low.astype(jnp.float32), axis=0)
    bias_value = jnp.sum(dvalue_low.astype(jnp.float32), axis=0)
    bias_query, bias_key, bias_value, gain_first_sum, gain_second_sum = (
        lax.psum_scatter(bias_query, "fsdp", scatter_dimension=0, tiled=True),
        lax.psum_scatter(bias_key, "fsdp", scatter_dimension=0, tiled=True),
        lax.psum_scatter(bias_value, "fsdp", scatter_dimension=0, tiled=True),
        lax.psum_scatter(d_gain_first, "fsdp", scatter_dimension=0, tiled=True),
        lax.psum_scatter(d_gain_second, "fsdp", scatter_dimension=0, tiled=True),
    )
    (
        attn_sums,
        mlp_sums,
        down_sums,
        bias_query,
        bias_key,
        bias_value,
        gain_first_sum,
        gain_second_sum,
    ) = (
        lax.psum(attn_sums.astype(jnp.bfloat16), "rep").astype(jnp.float32),
        lax.psum(mlp_sums.astype(jnp.bfloat16), "rep").astype(jnp.float32),
        lax.psum(down_sums.astype(jnp.bfloat16), "rep").astype(jnp.float32),
        lax.psum(bias_query.astype(jnp.bfloat16), "rep").astype(jnp.float32),
        lax.psum(bias_key.astype(jnp.bfloat16), "rep").astype(jnp.float32),
        lax.psum(bias_value.astype(jnp.bfloat16), "rep").astype(jnp.float32),
        lax.psum(gain_first_sum.astype(jnp.bfloat16), "rep").astype(jnp.float32),
        lax.psum(gain_second_sum.astype(jnp.bfloat16), "rep").astype(jnp.float32),
    )
    grad_query = attn_sums[:, :model_width]
    grad_key = attn_sums[:, model_width : model_width + kv_width]
    grad_value = attn_sums[:, model_width + kv_width : model_width + 2 * kv_width]
    grad_output = attn_sums[:, model_width + 2 * kv_width :]
    grad_gate = mlp_sums[:, :ff_width]
    grad_up = mlp_sums[:, ff_width:]
    return (
        output,
        grad_input,
        grad_query,
        bias_query,
        grad_key,
        bias_key,
        grad_value,
        bias_value,
        grad_output,
        gain_first_sum,
        grad_gate,
        grad_up,
        down_sums,
        gain_second_sum,
    )


def solution(mesh):
    placed = (
        P(("rep", "fsdp"), None),
        P(("rep", "fsdp"), None),
        P("rep", None),
        P("rep", None),
        P("fsdp", None),
        P("fsdp"),
        P("fsdp", None),
        P("fsdp"),
        P("fsdp", None),
        P("fsdp"),
        P("fsdp", None),
        P("fsdp"),
        P("fsdp", None),
        P("fsdp", None),
        P("fsdp", None),
        P("fsdp"),
    )
    return jax.shard_map(
        local,
        mesh=mesh,
        in_specs=placed,
        out_specs=(
            P(("rep", "fsdp"), None),
            P(("rep", "fsdp"), None),
            P("fsdp", None),
            P("fsdp"),
            P("fsdp", None),
            P("fsdp"),
            P("fsdp", None),
            P("fsdp"),
            P("fsdp", None),
            P("fsdp"),
            P("fsdp", None),
            P("fsdp", None),
            P("fsdp", None),
            P("fsdp"),
        ),
        check_vma=False,
    )
```

profile of v0, /device:TPU:0, one launch (start us, length us, event | category | flops | bytes accessed | tf_op | source)
XLA Modules:
  0.0 2377.8 jit_solution(16772693715200293686)
XLA Ops:
  12.5 11.3 all-reduce.10
  23.9 7.2 all-gather.2
  31.2 7.9 all-gather
  39.1 7.2 all-gather.1
  49.7 18.5 all_gather.49
  71.6 12.9 all_gather.51
  85.5 15.4 all_gather.46
  102.4 12.5 all_gather.48
  117.7 5.4 convolution_add_fusion.4
  123.0 2.1 copy.97
  127.3 3.8 fusion.69
  131.1 3.7 fusion.3
  134.8 3.0 copy-done
  137.7 5.9 fusion.36
  143.7 2.3 copy.104
  146.0 4.5 multiply_reduce_fusion.2
  150.8 242.3 %all-gather.15.cloned.1.call-done = bf16[1536,8960]{1,0:T(8,128)(2,1)} async-done(((bf16[384,8960]{1,0:T(8,128)(2,1)}), bf16[1536,8960]{1,0:T(8,128)(2,1)}) %all-gather.15.cloned.1.call-update) | async-done | bytes 27525136 | tf_op jit(solution)/shard_map/all_gather | solution.py:181
  393.2 17.3 fusion.71
  410.5 231.5 %all-gather.13.cloned.1.call-done = bf16[1536,8960]{1,0:T(8,128)(2,1)} async-done(((bf16[384,8960]{1,0:T(8,128)(2,1)}), bf16[1536,8960]{1,0:T(8,128)(2,1)}) %all-gather.13.cloned.1.call-update) | async-done | bytes 27525136 | tf_op jit(solution)/shard_map/all_gather | solution.py:180
  642.1 17.8 fusion.70
  659.9 231.1 %all-gather.17.cloned.1.call-done = bf16[8960,1536]{1,0:T(8,128)(2,1)} async-done(((bf16[2240,1536]{1,0:T(8,128)(2,1)}), bf16[8960,1536]{1,0:T(8,128)(2,1)}) %all-gather.17.cloned.1.call-update) | async-done | bytes 27525136 | tf_op jit(solution)/shard_map/all_gather | solution.py:190
  890.9 24.7 %multiply_convert_fusion = (bf16[320,8960]{1,0:T(8,128)(2,1)}, bf16[320,8960]{1,0:T(8,128)(2,1)}, bf16[320,8960]{1,0:T(8,128)(2,1)}) fusion(f32[320,8960]{1,0:T(8,128)} %fusion.70, f32[320,8960]{1,0:T(8,128)} %fusion.71, bf16[320,1536]{1,0:T(8,128)(2,1)S(1)} %copy-done.33, bf16[8960,1536]{1,0:T(8,128)(2,1)} %all-gather.17.cloned.1.call-done), kind=kOutput, calls=%fused_computation.15 | convolution fusion | flops 8851046400 | bytes 68648960 | tf_op jit(solution)/shard_map/dot_general | solution.py:62
  915.7 16.5 fusion.72
  932.1 17.3 multiply_reduce_fusion
  949.4 2.1 multiply_add_fusion
  955.3 9.0 fusion.19
  964.3 12.4 fusion
  977.0 13.4 fusion.2
  992.0 2.3 copy-done.1
  995.8 7.8 bitcast_multiply_fusion.3
  1003.6 2.1 copy.109
  1005.6 1.9 copy.112
  1007.6 1.9 broadcast_multiply_fusion
  1012.8 4.4 convolution_convert_fusion.3
  1017.2 4.3 convolution_convert_fusion.4
  1021.5 3.7 reduce-scatter.7.cloned.1.call-done
  1026.9 1.9 reshape.326
  1030.9 1.8 convert_reduce_fusion.2
  1033.4 2.0 convolution_convert_fusion.6
  1035.4 4.7 pad_maximum_fusion.1
  1040.0 14.6 copy.143
  1054.7 22.3 convolution_convert_fusion.2
  1077.1 21.4 convolution_convert_fusion
  1098.5 21.1 convolution_convert_fusion.1
  1119.7 37.7 %pad_maximum_fusion = bf16[1536,17920]{1,0:T(8,128)(2,1)} fusion(bf16[1536,8960]{1,0:T(8,128)(2,1)} %convolution_convert_fusion, bf16[1536,8960]{1,0:T(8,128)(2,1)} %convolution_convert_fusion.1), kind=kLoop, calls=%fused_computation | loop fusion | flops 110100480 | bytes 110100480 | tf_op jit(solution)/shard_map/concatenate | solution.py:205
  1157.5 5.2 reduce-scatter.13.cloned.1.call-done
  1162.7 4.8 copy.144
  1167.4 239.3 %reduce-scatter.11.cloned.1.call-done = bf16[2240,1536]{1,0:T(8,128)(2,1)} async-done(((bf16[8960,1536]{1,0:T(8,128)(2,1)}), bf16[2240,1536]{1,0:T(8,128)(2,1)}) %reduce-scatter.11.cloned.1.call-update) | async-done | bytes 6881296 | tf_op jit(solution)/shard_map/reduce_scatter | solution.py:193
  1406.8 465.6 %reduce-scatter.9.cloned.1.call-done = bf16[384,17920]{1,0:T(8,128)(2,1)} async-done(((bf16[1536,17920]{1,0:T(8,128)(2,1)}), bf16[384,17920]{1,0:T(8,128)(2,1)}) %reduce-scatter.9.cloned.1.call-update) | async-done | bytes 13762576 | tf_op jit(solution)/shard_map/reduce_scatter | solution.py:204
  1873.7 1.9 copy.117
  1875.6 1.9 copy.118
  1877.4 3.4 convert_reduce_fusion
  1880.9 5.1 fusion.73
  1886.0 16.9 convolution_add_fusion.3
  1904.2 2.0 fusion.30
  1906.2 15.9 all-reduce.7
  1922.5 14.6 all-reduce.8
  1939.9 3.4 fusion.29
  1943.3 392.3 %all-reduce.13.cloned.1.call-done = (bf16[384,3584]{0,1:T(8,128)(2,1)}, bf16[384,17920]{1,0:T(8,128)(2,1)}, bf16[2240,1536]{1,0:T(8,128)(2,1)}) async-done(((bf16[384,3584]{0,1:T(8,128)(2,1)}, bf16[384,17920]{1,0:T(8,128)(2,1)}, bf16[2240,1536]{1,0:T(8,128)(2,1)}), (bf16[384,3584]{0,1:T(8,128)(2,1)}, bf16[384,17920]{1,0:T(8,128)(2,1)}, bf16[2240,1536]{1,0:T(8,128)(2,1)})) %all-reduce.13.cloned.1.call-update) | async-done | bytes 23396368 | tf_op jit(solution)/shard_map/psum | solution.py:307
  2336.7 3.3 fusion.64
  2341.8 3.0 copy.122
  2344.9 1.9 copy.119
  2346.8 10.1 convert_element_type.209
  2356.9 13.6 fusion.63
  (214 shorter events, 41.0 us)
Async XLA Ops:
  7.2 110.5 %all-gather.9.cloned.1.call-start = ((), (), s32[]{:S(2)}) async-start(), calls=%async_computation.4 | async-start | bytes 5898240 | tf_op jit(solution)/shard_map/all_gather | solution.py:118
  7.9 138.1 %all-gather.11.cloned.1.call-start = ((), (), s32[]{:S(2)}) async-start(), calls=%async_computation.5 | async-start | bytes 5898240 | tf_op jit(solution)/shard_map/all_gather | solution.py:121
  8.7 384.5 %all-gather.15.cloned.1.call-start = ((), (), s32[]{:S(2)}) async-start(), calls=%async_computation.7 | async-start | bytes 34406400 | tf_op jit(solution)/shard_map/all_gather | solution.py:181
  9.4 632.7 %all-gather.13.cloned.1.call-start = ((), (), s32[]{:S(2)}) async-start(), calls=%async_computation.6 | async-start | bytes 34406400 | tf_op jit(solution)/shard_map/all_gather | solution.py:180
  10.0 2.0 copy-start.53
  10.0 2.2 copy-start.54
  10.0 13.8 copy-start.49
  10.0 13.8 copy-start.50
  10.0 13.8 copy-start.51
  10.0 37.0 %copy-start.52 = (s32[1,8]{1,0:T(1,128)S(1)}, s32[1,8]{1,0:T(1,128)}, u32[]{:S(2)}) copy-start(s32[1,8]{1,0:T(1,128)} %param.18) | copy-start | bytes 100
  10.1 39.6 %copy-start.37 = (bf16[384,256]{1,0:T(8,128)(2,1)S(1)}, bf16[384,256]{1,0:T(8,128)(2,1)}, u32[]{:S(2)}) copy-start(bf16[384,256]{1,0:T(8,128)(2,1)} %param.22) | copy-start | bytes 589828
  10.1 880.9 %all-gather.17.cloned.1.call-start = ((), (), s32[]{:S(2)}) async-start(), calls=%async_computation.8 | async-start | bytes 34406400 | tf_op jit(solution)/shard_map/all_gather | solution.py:190
  10.6 57.6 %copy-start.4 = (bf16[320,1536]{1,0:T(8,128)(2,1)S(1)}, bf16[320,1536]{1,0:T(8,128)(2,1)}, u32[]{:S(2)}) copy-start(bf16[320,1536]{1,0:T(8,128)(2,1)} %param.16) | copy-start | bytes 2949124
  10.7 1014.6 %reduce-scatter.7.cloned.1.call-start = ((), (), s32[]{:S(2)}) async-start(), calls=%async_computation.9 | async-start | bytes 1638400 | tf_op jit(solution)/shard_map/reduce_scatter | solution.py:245
  39.1 78.5 %copy-start.39 = (f32[1536]{0:T(1024)}, f32[1536]{0:T(1024)S(1)}, u32[]{:S(2)}) copy-start(f32[1536]{0:T(1024)S(1)} %reshape.339) | copy-start | bytes 18436
  48.7 21.5 copy-start.23
  48.9 76.5 %copy-start.26 = (f32[320,128]{0,1:T(8,128)}, f32[320,128]{0,1:T(8,128)S(1)}, u32[]{:S(2)}) copy-start(f32[320,128]{0,1:T(8,128)S(1)} %copy.98) | copy-start | bytes 491524
  68.2 0.9 copy-start.18
  69.2 48.5 %copy-start.41 = (f32[320]{0:T(512)}, f32[320]{0:T(512)S(1)}, u32[]{:S(2)}) copy-start(f32[320]{0:T(512)S(1)} %add_rsqrt_fusion.1) | copy-start | bytes 3844
  70.2 15.3 copy-start.38
  101.9 14.1 copy-start.48
  101.9 15.8 copy-start.43
  125.1 0.9 copy-start.28
  126.1 1.1 copy-start.11
  126.1 1.2 copy-start.17
  126.5 4.6 copy-start.13
  131.1 6.7 copy-start
  150.5 798.9 %copy-start.2 = (f32[320,1536]{1,0:T(8,128)}, f32[320,1536]{1,0:T(8,128)S(1)}, u32[]{:S(2)}) copy-start(f32[320,1536]{1,0:T(8,128)S(1)} %get-tuple-element.119) | copy-start | bytes 5898244
  150.8 242.4 %copy-start.34 = (bf16[320,1536]{1,0:T(8,128)(2,1)}, bf16[320,1536]{1,0:T(8,128)(2,1)S(1)}, u32[]{:S(2)}) copy-start(bf16[320,1536]{1,0:T(8,128)(2,1)S(1)} %multiply_convert_fusion.3) | copy-start | bytes 2949124
  410.5 480.4 %copy-start.33 = (bf16[320,1536]{1,0:T(8,128)(2,1)S(1)}, bf16[320,1536]{1,0:T(8,128)(2,1)}, u32[]{:S(2)}) copy-start(bf16[320,1536]{1,0:T(8,128)(2,1)} %param.17) | copy-start | bytes 2949124
  915.7 37.1 %slice-start = ((s8[4718592]{0:T(1024)(128)(4,1)}), s8[4194304]{0:T(1024)(128)(4,1)S(1)}, s32[]{:S(2)}) async-start(s8[4718592]{0:T(1024)(128)(4,1)} %bitcast.131), calls=%async_computation.14 | async-start | bytes 8388608
  932.1 20.7 slice-start.1
  951.5 1.3 copy-start.8
  955.3 9.0 copy-start.25
  976.9 13.5 copy-start.14
  990.4 3.9 copy-start.1
  994.3 1.5 copy-start.12
  995.7 166.9 %reduce-scatter.13.cloned.1.call-start = ((), (), s32[]{:S(2)}) async-start(), calls=%async_computation.12 | async-start | bytes 13762560
  1005.6 1.9 copy-start.29
  1009.7 1.7 copy-start.6
  1009.7 1.7 copy-start.27
  1011.4 1.4 copy-start.5
  1011.4 1.4 copy-start.40
  1011.4 1.4 copy-start.42
  1011.7 1.0 copy-start.31
  1012.7 4.5 copy-start.7
  1012.7 4.5 copy-start.9
  1017.2 11.6 copy-start.24
  1028.7 6.6 copy-start.16
  1032.7 2.7 copy-start.15
  1054.7 352.1 %reduce-scatter.11.cloned.1.call-start = ((), (), s32[]{:S(2)}) async-start(), calls=%async_computation.11 | async-start | bytes 34406400 | tf_op jit(solution)/shard_map/reduce_scatter | solution.py:193
  1077.0 795.3 %reduce-scatter.9.cloned.1.call-start = ((), (), s32[]{:S(2)}) async-start(), calls=%async_computation.10 | async-start | bytes 68812800 | tf_op jit(solution)/shard_map/reduce_scatter | solution.py:204
  1077.1 21.5 copy-start.35
  1157.4 1178.2 %all-reduce.13.cloned.1.call-start = ((), (), s32[]{:S(2)}) async-start(), calls=%async_computation.13 | async-start | bytes 46792704 | tf_op jit(solution)/shard_map/psum | solution.py:307
  1875.6 1.9 copy-start.36
  1877.4 3.4 copy-start.32
  1880.9 5.1 copy-start.3
  1886.0 17.0 copy-start.19
  1903.0 1.1 copy-start.21
  1903.0 1.2 copy-start.30
  1904.2 2.0 copy-start.44
  1904.2 2.0 copy-start.45
  1904.2 2.0 copy-start.46
  1904.2 35.7 %copy-start.10 = (f32[320,1536]{1,0:T(8,128)S(1)}, f32[320,1536]{1,0:T(8,128)}, u32[]{:S(2)}) copy-start(f32[320,1536]{1,0:T(8,128)} %copy-done.8) | copy-start | bytes 5898244
  (3 other events, 2.4 us)
Sparse Core Ops, SparseCore 0:
  9.9 69.6 all-gather.8
  81.4 62.6 all-gather.10
  146.0 247.1 all-gather.14
  394.9 247.1 all-gather.12
  643.8 247.1 all-gather.16
  995.8 29.3 reduce-scatter.6
  1054.8 107.8 reduce-scatter.12
  1165.8 240.9 reduce-scatter.10
  1410.2 462.1 reduce-scatter.8
  1875.7 459.8 all-reduce.12
where the time goes:
time: 2380 us
  waiting for transfers between devices  1810 us (76%)
  matrix products  247 us (10%)
  blocking collectives  124 us (5%)
  other arithmetic  96.1 us (4%)
  local copies, waits for them, and re-layouts  78.5 us (3%)
    reduce_scatter x1, waiting for transfers between devices, local(): lax.psum_scatter(jnp.concatenate([dot_left_t(columns, d_gate), dot_left_t...  466 us
    psum x1, waiting for transfers between devices, local(): lax.psum(attn_sums.astype(jnp.bfloat16), 'rep').astype(jnp.float32)  392 us
    all_gather x1, waiting for transfers between devices, local(): lax.all_gather(w_up, 'fsdp', axis=0, tiled=True)  242 us
    reduce_scatter x1, waiting for transfers between devices, local(): lax.psum_scatter(dot_left_t(columns, out_grad).astype(jnp.bfloat16), 'fsd...  239 us
    all_gather x1, waiting for transfers between devices, local(): lax.all_gather(w_gate, 'fsdp', axis=0, tiled=True)  232 us
    all_gather x1, waiting for transfers between devices, local(): lax.all_gather(w_down, 'fsdp', axis=0, tiled=True)  231 us
    dot_general x7, matrix products, dot_left_t(): lax.dot_general(left, right, (((0,), (0,)), ((), ())), preferred_element_...  76.2 us
    dot_general x7, matrix products, dot_right_t(): lax.dot_general(left, right, (((1,), (1,)), ((), ())), preferred_element_...  67.8 us
  transfers between devices with their start and end apart: 10, of which 8 were waited for; matrix products, arithmetic and copies ran while one was open for 10% of the time, Pallas kernels for 0%

commit v1 on v0

--- a/solution.py
+++ b/solution.py
@@ -68,6 +68,104 @@
     return lax.dot_general(
         left, right, (((0,), (0,)), ((), ())), preferred_element_type=jnp.float32
     )
+
+
+def xor_pairs(count, bit):
+    return [(i, i ^ bit) for i in range(count)]
+
+
+def bits_of(count):
+    return [1 << k for k in range(count.bit_length() - 1)]
+
+
+def gather_relative(block, axis):
+    count = lax.axis_size(axis)
+    bits = bits_of(count)
+    half = block.shape[0] // 2
+    halves = []
+    for part, order in ((block[:half], bits), (block[half:], bits[::-1])):
+        have = {0: part}
+        for bit in order:
+            fresh = {
+                d ^ bit: lax.ppermute(piece, axis, xor_pairs(count, bit))
+                for d, piece in have.items()
+            }
+            have.update(fresh)
+        halves.append(have)
+    return [(halves[0][d], halves[1][d]) for d in range(count)]
+
+
+def scatter_relative(pieces, axis):
+    count = lax.axis_size(axis)
+    bits = bits_of(count)
+    half = pieces[0].shape[0] // 2
+    sums = []
+    for lo, hi, order in ((0, half, bits[::-1]), (half, 2 * half, bits)):
+        have = {d: pieces[d][lo:hi] for d in range(count)}
+        for bit in order:
+            come = {
+                d ^ bit: lax.ppermute(have[d].astype(jnp.bfloat16), axis, xor_pairs(count, bit))
+                for d in have
+                if d & bit
+            }
+            have = {d: have[d].astype(jnp.float32) + come[d].astype(jnp.float32) for d in come}
+        sums.append(have[0])
+    return jnp.concatenate(sums, axis=0)
+
+
+def core_swap(block):
+    return lax.ppermute(block, "rep", xor_pairs(lax.axis_size("rep"), 1))
+
+
+def line_pairs(lows, way):
+    return [(2 * i + c, 2 * (i + way) + c) for i in lows for c in range(2)]
+
+
+def pick(array, index):
+    return lax.dynamic_index_in_dim(array, index, 0, keepdims=False)
+
+
+def line_scatter(parts):
+    count = lax.axis_size("rep") // 2
+    here = lax.axis_index("rep") // 2
+    arrived = [None, None]
+    for step in range(1, count):
+        sends = [
+            pick(parts, jnp.clip(count - step + here, 0, count - 1)),
+            pick(parts, jnp.clip(here - count + step, 0, count - 1)),
+        ]
+        for way in range(2):
+            if arrived[way] is not None:
+                sends[way] = (
+                    sends[way].astype(jnp.float32) + arrived[way].astype(jnp.float32)
+                ).astype(jnp.bfloat16)
+        arrived = [
+            lax.ppermute(sends[0], "rep", line_pairs(range(step), 1)),
+            lax.ppermute(sends[1], "rep", line_pairs(range(count - step, count), -1)),
+        ]
+    own = pick(parts, here).astype(jnp.float32)
+    return own + arrived[0].astype(jnp.float32) + arrived[1].astype(jnp.float32)
+
+
+def line_gather(block):
+    count = lax.axis_size("rep") // 2
+    here = lax.axis_index("rep") // 2
+    below, above = [block], [block]
+    for step in range(1, count):
+        below.append(lax.ppermute(below[-1], "rep", line_pairs(range(step - 1, count - 1), 1)))
+        above.append(lax.ppermute(above[-1], "rep", line_pairs(range(1, count - step + 1), -1)))
+    stacked = jnp.stack(below[:0:-1] + above)
+    return lax.dynamic_slice_in_dim(stacked, count - 1 - here, count, 0)
+
+
+def core_halves(mine, other, core):
+    return jnp.where(core == 0, jnp.stack([mine, other]), jnp.stack([other, mine]))
+
+
+def place(pieces, here):
+    count = len(pieces)
+    stacked = jnp.stack(pieces)
+    return jnp.stack([pick(stacked, here ^ j) for j in range(count)])
 
 
 def local(
@@ -104,27 +202,51 @@
     key_doc, unused_rel, key_piece = row_layout(row_pos, lengths, starts, PIECE)
     allowed = visible_pairs(query_doc, local_pos, query_piece, key_doc, row_pos, key_piece)
     cosine, sine = rope_tables(query_rel, HDIM)
-    (
-        query_full,
-        key_full,
-        value_full,
-        output_full,
-        query_bias,
-        key_bias,
-        value_bias,
-        attn_gain,
-        mlp_gain,
-    ) = (
-        lax.all_gather(w_query, "fsdp", axis=0, tiled=True),
-        lax.all_gather(w_key, "fsdp", axis=0, tiled=True),
-        lax.all_gather(w_value, "fsdp", axis=0, tiled=True),
-        lax.all_gather(w_output, "fsdp", axis=0, tiled=True),
-        lax.all_gather(b_query, "fsdp", axis=0, tiled=True),
-        lax.all_gather(b_key, "fsdp", axis=0, tiled=True),
-        lax.all_gather(b_value, "fsdp", axis=0, tiled=True),
-        lax.all_gather(gain_attn, "fsdp", axis=0, tiled=True),
-        lax.all_gather(gain_mlp, "fsdp", axis=0, tiled=True),
-    )
+    here = lax.axis_index("fsdp")
+    core = lax.axis_index("rep") % 2
+    line = lax.axis_size("rep") // 2
+    low = jnp.bfloat16
+
+    def gather_rows(weight):
+        half = weight.shape[0] // 2
+        mine = lax.dynamic_slice_in_dim(weight, core * half, half, 0)
+        mine = jnp.stack([jnp.concatenate(p, axis=0) for p in gather_relative(mine, "fsdp")])
+        both = core_halves(mine, core_swap(mine), core)
+        rows = place([both[:, d] for d in range(shard_count)], here)
+        return rows.reshape(2 * half * shard_count, weight.shape[1])
+
+    qkv_full = gather_rows(jnp.concatenate([w_query, w_key, w_value], axis=1))
+    query_full = qkv_full[:, :model_width]
+    key_full = qkv_full[:, model_width : model_width + kv_width]
+    value_full = qkv_full[:, model_width + kv_width :]
+    output_full = gather_rows(w_output)
+    vectors = lax.all_gather(
+        jnp.concatenate([b_query, b_key, b_value, gain_attn, gain_mlp]), "fsdp", axis=0
+    )
+    cuts = [0]
+    for vector in (b_query, b_key, b_value, gain_attn, gain_mlp):
+        cuts.append(cuts[-1] + vector.shape[0])
+    query_bias, key_bias, value_bias, attn_gain, mlp_gain = (
+        vectors[:, cuts[i] : cuts[i + 1]].reshape(-1) for i in range(5)
+    )
+
+    part = ff_width // shard_count
+
+    def exchange_columns(weight):
+        half = weight.shape[0] // 2
+        mine = lax.dynamic_slice_in_dim(weight, core * half, half, 0)
+        got = []
+        for d in range(shard_count):
+            piece = lax.dynamic_slice_in_dim(mine, (here ^ d) * part, part, 1)
+            got.append(piece if d == 0 else lax.ppermute(piece, "fsdp", xor_pairs(shard_count, d)))
+        got = jnp.stack(got)
+        both = core_halves(got, core_swap(got), core)
+        rows = place([both[:, d] for d in range(shard_count)], here)
+        return rows.reshape(2 * half * shard_count, part)
+
+    gate_part = exchange_columns(w_gate)
+    up_part = exchange_columns(w_up)
+    cot_all = jnp.concatenate([h for p in gather_relative(out_grad, "fsdp") for h in p], axis=0)
     x_float = hidden_in.astype(jnp.float32)
     inv_first = lax.rsqrt(jnp.mean(x_float * x_float, axis=1, keepdims=True) + epsilon)
     unit_first = x_float * inv_first
@@ -176,39 +298,58 @@
     gain_second = mlp_gain.astype(jnp.float32)
     normed_second = (unit_second * gain_second).astype(jnp.bfloat16)
     cot_float = out_grad.astype(jnp.float32)
-    pieces = (
-        lax.all_gather(w_gate, "fsdp", axis=0, tiled=True),
-        lax.all_gather(w_up, "fsdp", axis=0, tiled=True),
-    )
-    columns = normed_second
-    gate_val = mat_dot(columns, pieces[0])
-    up_val = mat_dot(columns, pieces[1])
+    normed_all = jnp.concatenate([h for p in gather_relative(normed_second, "fsdp") for h in p], axis=0)
+    gate_val = mat_dot(normed_all, gate_part)
+    up_val = mat_dot(normed_all, up_part)
     sig_gate = jax.nn.sigmoid(gate_val)
     silu_gate = gate_val * sig_gate
-    act_low = (silu_gate * up_val).astype(jnp.bfloat16)
-    columns = act_low
-    mlp_out = mat_dot(columns, lax.all_gather(w_down, "fsdp", axis=0, tiled=True))
-    d_act = dot_right_t(out_grad, lax.all_gather(w_down, "fsdp", axis=0, tiled=True))
-    columns = act_low
-    down_sums = lax.psum_scatter(
-        dot_left_t(columns, out_grad).astype(jnp.bfloat16), "fsdp", scatter_dimension=0, tiled=True
-    ).astype(jnp.float32)
-    d_gate = (d_act * up_val * sig_gate * (1.0 + gate_val * (1.0 - sig_gate))).astype(jnp.bfloat16)
-    d_up = (d_act * silu_gate).astype(jnp.bfloat16)
-    pieces = (
-        lax.all_gather(w_gate, "fsdp", axis=0, tiled=True),
-        lax.all_gather(w_up, "fsdp", axis=0, tiled=True),
-    )
-    partial_value = dot_right_t(d_gate, pieces[0]) + dot_right_t(d_up, pieces[1])
-    columns = normed_second
-    mlp_sums = lax.psum_scatter(
-        jnp.concatenate([dot_left_t(columns, d_gate), dot_left_t(columns, d_up)], axis=1).astype(
-            jnp.bfloat16
-        ),
-        "fsdp",
-        scatter_dimension=0,
-        tiled=True,
-    ).astype(jnp.float32)
+    act_low = (silu_gate * up_val).astype(low)
+    d_act = dot_right_t(cot_all, w_down)
+    d_gate = (d_act * up_val * sig_gate * (1.0 + gate_val * (1.0 - sig_gate))).astype(low)
+    d_up = (d_act * silu_gate).astype(low)
+    mlp_part = mat_dot(act_low, w_down).reshape(shard_count, tok_rows, model_width)
+    mlp_out = scatter_relative([mlp_part[d] for d in range(shard_count)], "fsdp")
+    norm_part = (dot_right_t(d_gate, gate_part) + dot_right_t(d_up, up_part)).reshape(
+        shard_count, tok_rows, model_width
+    )
+    partial_value = scatter_relative([norm_part[d] for d in range(shard_count)], "fsdp")
+
+    def keep_half(grad):
+        mine = lax.dynamic_index_in_dim(grad, core, 1, keepdims=False)
+        other = lax.dynamic_index_in_dim(grad, 1 - core, 1, keepdims=False)
+        return (mine.astype(jnp.float32) + core_swap(other).astype(jnp.float32)).astype(low)
+
+    def both_cores(half):
+        return core_halves(half, core_swap(half), core)
+
+    down_grad = dot_left_t(act_low, cot_all).astype(low)
+    half = part // 2
+    down_half = keep_half(down_grad.reshape(1, 2, half, model_width))[0]
+    wide = model_width // line
+    down_parts = jnp.stack([down_half[:, q * wide : (q + 1) * wide] for q in range(line)])
+    down_own = line_scatter(down_parts).astype(low)
+    down_rows = line_gather(down_own)
+    down_rows = jnp.concatenate([down_rows[q] for q in range(line)], axis=1)
+    down_sums = both_cores(down_rows).reshape(part, model_width).astype(jnp.float32)
+
+    rows = model_width // shard_count
+    thin = rows // 2 // line
+
+    def column_grad(d_value):
+        grad = dot_left_t(normed_all, d_value).astype(low)
+        kept = keep_half(grad.reshape(shard_count, 2, rows // 2, part))
+        kept = kept.reshape(shard_count, line, thin, part).transpose(1, 0, 2, 3)
+        own = line_scatter(kept).astype(low)
+        got = []
+        for d in range(shard_count):
+            piece = pick(own, here ^ d)
+            got.append(piece if d == 0 else lax.ppermute(piece, "fsdp", xor_pairs(shard_count, d)))
+        got = place(got, here).transpose(1, 0, 2).reshape(thin, ff_width)
+        full = line_gather(got).reshape(rows // 2, ff_width)
+        return both_cores(full).reshape(rows, ff_width).astype(jnp.float32)
+
+    grad_gate = column_grad(d_gate)
+    grad_up = column_grad(d_up)
     output = mid_state + mlp_out
     d_gain_second = jnp.sum(partial_value * unit_second, axis=0)
     scaled_second = partial_value * gain_second
@@ -265,20 +406,21 @@
         + dot_right_t(dkey_low, key_full)
         + dot_right_t(dvalue_low, value_full)
     )
-    attn_sums = lax.psum_scatter(
-        jnp.concatenate(
-            [
-                dot_left_t(normed_first, dquery_low),
-                dot_left_t(normed_first, dkey_low),
-                dot_left_t(normed_first, dvalue_low),
-                dot_left_t(attn_low, d_branch_low),
-            ],
-            axis=1,
-        ).astype(jnp.bfloat16),
-        "fsdp",
-        scatter_dimension=0,
-        tiled=True,
-    ).astype(jnp.float32)
+    attn_grads = jnp.concatenate(
+        [
+            dot_left_t(normed_first, dquery_low).astype(low),
+            dot_left_t(normed_first, dkey_low).astype(low),
+            dot_left_t(normed_first, dvalue_low).astype(low),
+            dot_left_t(attn_low, d_branch_low).astype(low),
+        ],
+        axis=1,
+    )
+    attn_wide = attn_grads.shape[1]
+    attn_kept = keep_half(attn_grads.reshape(shard_count, 2, rows // 2, attn_wide))
+    attn_own = scatter_relative([pick(attn_kept, here ^ d) for d in range(shard_count)], "fsdp").astype(low)
+    attn_own = line_scatter(attn_own.reshape(line, thin, attn_wide)).astype(low)
+    attn_rows = line_gather(attn_own).reshape(rows // 2, attn_wide)
+    attn_sums = both_cores(attn_rows).reshape(rows, attn_wide).astype(jnp.float32)
     d_gain_first = jnp.sum(d_norm_first * unit_first, axis=0)
     scaled_first = d_norm_first * gain_first
     grad_input = d_mid + inv_first * (
@@ -287,38 +429,19 @@
     bias_query = jnp.sum(dquery_low.astype(jnp.float32), axis=0)
     bias_key = jnp.sum(dkey_low.astype(jnp.float32), axis=0)
     bias_value = jnp.sum(dvalue_low.astype(jnp.float32), axis=0)
-    bias_query, bias_key, bias_value, gain_first_sum, gain_second_sum = (
-        lax.psum_scatter(bias_query, "fsdp", scatter_dimension=0, tiled=True),
-        lax.psum_scatter(bias_key, "fsdp", scatter_dimension=0, tiled=True),
-        lax.psum_scatter(bias_value, "fsdp", scatter_dimension=0, tiled=True),
-        lax.psum_scatter(d_gain_first, "fsdp", scatter_dimension=0, tiled=True),
-        lax.psum_scatter(d_gain_second, "fsdp", scatter_dimension=0, tiled=True),
-    )
-    (
-        attn_sums,
-        mlp_sums,
-        down_sums,
-        bias_query,
-        bias_key,
-        bias_value,
-        gain_first_sum,
-        gain_second_sum,
-    ) = (
-        lax.psum(attn_sums.astype(jnp.bfloat16), "rep").astype(jnp.float32),
-        lax.psum(mlp_sums.astype(jnp.bfloat16), "rep").astype(jnp.float32),
-        lax.psum(down_sums.astype(jnp.bfloat16), "rep").astype(jnp.float32),
-        lax.psum(bias_query.astype(jnp.bfloat16), "rep").astype(jnp.float32),
-        lax.psum(bias_key.astype(jnp.bfloat16), "rep").astype(jnp.float32),
-        lax.psum(bias_value.astype(jnp.bfloat16), "rep").astype(jnp.float32),
-        lax.psum(gain_first_sum.astype(jnp.bfloat16), "rep").astype(jnp.float32),
-        lax.psum(gain_second_sum.astype(jnp.bfloat16), "rep").astype(jnp.float32),
-    )
+    small = (bias_query, bias_key, bias_value, d_gain_first, d_gain_second)
+    summed = lax.psum(jnp.concatenate(small), ("rep", "fsdp"))
+    outs = []
+    at = 0
+    for vector in small:
+        size = vector.shape[0] // shard_count
+        outs.append(lax.dynamic_slice_in_dim(summed, at + here * size, size, 0))
+        at += vector.shape[0]
+    bias_query, bias_key, bias_value, gain_first_sum, gain_second_sum = outs
     grad_query = attn_sums[:, :model_width]
     grad_key = attn_sums[:, model_width : model_width + kv_width]
     grad_value = attn_sums[:, model_width + kv_width : model_width + 2 * kv_width]
     grad_output = attn_sums[:, model_width + 2 * kv_width :]
-    grad_gate = mlp_sums[:, :ff_width]
-    grad_up = mlp_sums[:, ff_width:]
     return (
         output,
         grad_input,

time: 2380 us -> 1300 us (0.55)
  waiting for transfers between devices: 1810 us -> 398 us
  starting transfers between devices: 0.39 us -> 223 us
  local copies, waits for them, and re-layouts: 78.5 us -> 197 us
  other arithmetic: 96.1 us -> 158 us
  blocking collectives: 124 us -> 80.6 us
  matrix products: 247 us -> 209 us
    all_gather x5 -> x0, waiting for transfers between devices: 705 us -> none  [the longest x1 242 us: local(): lax.all_gather(w_up, 'fsdp', axis=0, tiled=True)]
    reduce_scatter x2 -> x0, waiting for transfers between devices: 705 us -> none  [the longest x1 466 us: local(): lax.psum_scatter(jnp.concatenate([dot_left_t(columns, d_gate), dot_left_t...]
    ppermute x0 -> x114, waiting for transfers between devices: none -> 398 us  [the longest x12 118 us: line_gather(): lax.ppermute(above[-1], 'rep', line_pairs(range(1, count - step + 1), -1))]
    psum x1 -> x0, waiting for transfers between devices: 392 us -> none  [local(): lax.psum(attn_sums.astype(jnp.bfloat16), 'rep').astype(jnp.float32)]
    ppermute x0 -> x114, starting transfers between devices: none -> 223 us  [the longest x12 70.8 us: line_scatter(): lax.ppermute(sends[0], 'rep', line_pairs(range(step), 1))]
    all_gather x5 -> x1, blocking collectives: 56.3 us -> 19.1 us  [local(): lax.all_gather(jnp.concatenate([b_query, b_key, b_value, gain_attn, gain_...]
    concatenate x2 -> x3, other arithmetic: 42.4 us -> 5.96 us  [the longest x1 4.67 us: local(): jnp.concatenate([dot_left_t(normed_first, dquery_low).astype(low), dot_le...]
    convert_element_type x10 -> x26, other arithmetic: 13.1 us -> 48.2 us  [the longest x2 13 us: column_grad(): return both_cores(full).reshape(rows, ff_width).astype(jnp.float32)]
  transfers between devices with their start and end apart: 10 -> 115, of which waited for: 8 -> 37; matrix products, arithmetic and copies ran while one was open for 10% -> 31% of each run, Pallas kernels for 0% -> 0%
where the time goes in v1:
time: 1300 us; the launch traced here: 1280 us
  waiting for transfers between devices  398 us (31%)
  starting transfers between devices  223 us (17%)
  matrix products  209 us (16%)
  local copies, waits for them, and re-layouts  197 us (15%)
  other arithmetic  158 us (12%)
  blocking collectives  80.6 us (6%)
  between operations  17.2 us (1%)
    ppermute x12, waiting for transfers between devices, line_gather(): lax.ppermute(above[-1], 'rep', line_pairs(range(1, count - step + 1), -1))  118 us
    ppermute x18, waiting for transfers between devices, scatter_relative(): lax.ppermute(have[d].astype(jnp.bfloat16), axis, xor_pairs(count, bit))  86.4 us
    ppermute x12, starting transfers between devices, line_scatter(): lax.ppermute(sends[0], 'rep', line_pairs(range(step), 1))  70.8 us
    ppermute x24, waiting for transfers between devices, gather_relative(): lax.ppermute(piece, axis, xor_pairs(count, bit))  70 us
    dot_general x7, matrix products, dot_right_t(): lax.dot_general(left, right, (((1,), (1,)), ((), ())), preferred_element_...  64.7 us
    ppermute x12, waiting for transfers between devices, line_scatter(): lax.ppermute(sends[0], 'rep', line_pairs(range(step), 1))  62.6 us
    unnamed x263, local copies, waits for them, and re-layouts  57.8 us
    dot_general x7, matrix products, mat_dot(): return jnp.dot(left, right, preferred_element_type=jnp.float32)  51.8 us
  transfers between devices with their start and end apart: 115, of which 37 were waited for; matrix products, arithmetic and copies ran while one was open for 31% of the time, Pallas kernels for 0%

profile of v1, /device:TPU:0, one launch (start us, length us, event | category | flops | bytes accessed | tf_op | source)
XLA Modules:
  0.0 1283.9 jit_solution(9053746905817606389)
XLA Ops:
  18.6 19.1 %all-gather.1 = bf16[4,1,1280]{2,1,0:T(2,128)(2,1)S(1)} all-gather(bf16[1,1,1280]{2,1,0:T(2,128)(2,1)S(1)} %reshape.622), channel_id=2, replica_groups=mesh['rep'=8,'fsdp'=4] {'fsdp'}, dimensions={0}, use_global_device_ids=true | all-gather | bytes 12800 | tf_op jit(solution)/shard_map/all_gather | solution.py:223
  42.0 6.0 dynamic-slice_bitcast_fusion.9
  66.9 11.4 collective-permute-done.3
  90.5 6.6 collective-permute-done.35
  105.0 20.7 %collective-permute-done.11 = bf16[96,1536]{1,0:T(8,128)(2,1)S(1)} collective-permute-done((bf16[96,1536]{1,0:T(8,128)(2,1)}, bf16[96,1536]{1,0:T(8,128)(2,1)S(1)}, u32[]{:S(2)}, u32[]{:S(2)}) %collective-permute-start.11) | collective-permute-done | bytes 294944 | tf_op jit(solution)/shard_map/ppermute | solution.py:90
  131.3 6.4 collective-permute-done.5
  139.3 12.7 collective-permute-done.4
  164.6 15.4 %collective-permute-done.26 = bf16[192,2240]{1,0:T(8,128)(2,1)S(1)} collective-permute-done((bf16[192,2240]{1,0:T(8,128)(2,1)S(1)}, bf16[192,2240]{1,0:T(8,128)(2,1)S(1)}, u32[]{:S(2)}, u32[]{:S(2)}) %collective-permute-start.26) | collective-permute-done | bytes 860192 | tf_op jit(solution)/shard_map/ppermute | solution.py:241
  180.5 17.7 %collective-permute-done.25 = bf16[192,2240]{1,0:T(8,128)(2,1)S(1)} collective-permute-done((bf16[192,2240]{1,0:T(8,128)(2,1)S(1)}, bf16[192,2240]{1,0:T(8,128)(2,1)S(1)}, u32[]{:S(2)}, u32[]{:S(2)}) %collective-permute-start.25) | collective-permute-done | bytes 860192 | tf_op jit(solution)/shard_map/ppermute | solution.py:241
  202.0 6.1 collective-permute-done.38
  242.1 12.7 all_gather.15
  258.9 10.9 all_gather.14
  285.0 5.9 fusion.72
  305.5 8.5 maximum_select_fusion
  342.4 14.6 %fusion.138 = f32[1280,2240]{0,1:T(8,128)} fusion(bf16[1280,1536]{1,0:T(8,128)(2,1)} %constant_dynamic-update-slice_fusion, bf16[1536,2240]{1,0:T(8,128)(2,1)S(1)} %bitcast.541), kind=kOutput, calls=%fused_computation.417 | convolution fusion | flops 8808038400 | bytes 22282240 | tf_op jit(solution)/shard_map/dot_general | solution.py:58
  357.0 12.6 fusion.139
  369.5 24.3 %multiply_convert_fusion = (bf16[1280,2240]{0,1:T(8,128)(2,1)}, bf16[1280,2240]{0,1:T(8,128)(2,1)}, bf16[1280,2240]{0,1:T(8,128)(2,1)}) fusion(f32[1280,2240]{0,1:T(8,128)} %fusion.138, f32[1280,2240]{0,1:T(8,128)} %fusion.139, bf16[1280,1536]{1,0:T(8,128)(2,1)} %constant_dynamic-update-slice_fusion.7, bf16[2240,1536]{1,0:T(8,128)(2,1)} %param.30), kind=kOutput, calls=%fused_computation.11 | convolution fusion | flops 8851046400 | bytes 50954240 | tf_op jit(solution)/shard_map/dot_general | solution.py:62
  393.9 15.8 %fusion.140 = f32[1280,1536]{1,0:T(8,128)} fusion(bf16[1280,2240]{0,1:T(8,128)(2,1)} %get-tuple-element.25, bf16[1536,2240]{1,0:T(8,128)(2,1)} %bitcast.542), kind=kOutput, calls=%fused_computation.419 | convolution fusion | flops 8808038400 | bytes 20480000 | tf_op jit(solution)/shard_map/dot_general | solution.py:62
  409.7 11.2 convolution_convert_fusion.1
  421.0 13.0 %fusion.137 = (bf16[1280,1536]{1,0:T(8,128)(2,1)}, f32[1280,1536]{1,0:T(8,128)}) fusion(bf16[1280,2240]{0,1:T(8,128)(2,1)S(1)} %bitcast.591, bf16[2240,1536]{1,0:T(8,128)(2,1)S(1)} %bitcast.589), kind=kOutput, calls=%fused_computation.416 | convolution fusion | flops 8810004480 | bytes 24412160 | tf_op jit(solution)/shard_map/dot_general | solution.py:58
  433.9 11.2 convolution_convert_fusion.2
  445.1 13.7 %convolution_convert_fusion = bf16[1536,2240]{0,1:T(8,128)(2,1)} fusion(bf16[1280,2240]{0,1:T(8,128)(2,1)} %get-tuple-element.24, bf16[1280,1536]{1,0:T(8,128)(2,1)S(1)} %copy-done.67), kind=kOutput, calls=%fused_computation.16 | convolution fusion | flops 8811479040 | bytes 16547840 | tf_op jit(solution)/shard_map/dot_general | solution.py:68
  458.9 15.5 %fusion.136 = (bf16[1280,1536]{1,0:T(8,128)(2,1)}, f32[1280,1536]{1,0:T(8,128)}) fusion(f32[1280,1536]{1,0:T(8,128)} %fusion.140, bf16[1280,2240]{0,1:T(8,128)(2,1)} %get-tuple-element.24, bf16[1536,2240]{1,0:T(8,128)(2,1)S(1)} %bitcast.540), kind=kOutput, calls=%fused_computation.415 | convolution fusion | flops 8811970560 | bytes 32276480 | tf_op jit(solution)/shard_map/dot_general | solution.py:62
  482.9 10.2 copy.204
  501.2 9.6 copy.211
  521.9 9.8 collective-permute-done.42
  534.5 7.8 collective-permute-done.32
  542.3 13.2 %collective-permute-done.30 = bf16[160,1536]{1,0:T(8,128)(2,1)S(1)} collective-permute-done((bf16[160,1536]{1,0:T(8,128)(2,1)S(1)}, bf16[160,1536]{1,0:T(8,128)(2,1)S(1)}, u32[]{:S(2)}, u32[]{:S(2)}) %collective-permute-start.30) | collective-permute-done | bytes 491552 | tf_op jit(solution)/shard_map/ppermute | solution.py:107
  558.3 8.7 collective-permute-done.45
  569.9 6.0 collective-permute-done.33
  583.0 12.7 fusion
  595.6 9.6 fusion.31
  608.0 13.2 %fusion.2 = bf16[2,6,320,1280]{3,2,1,0:T(8,128)(2,1)} fusion(f32[2,1280,320,6]{1,2,3,0:T(8,128)S(1)} %copy-done.1, f32[2,6,320,1280]{3,2,1,0:T(8,128)} %copy-done, f32[2,6,320]{2,1,0:T(8,128)S(1)} %get-tuple-element.179, f32[2,6,320]{2,1,0:T(8,128)S(1)} %copy-done.64), kind=kLoop, calls=%fused_computation.4 | loop fusion | flops 19660800 | bytes 49182720 | tf_op jit(solution)/shard_map/convert_element_type | solution.py:369
  621.3 7.8 bitcast_multiply_fusion.3
  635.0 6.2 fusion.30
  721.6 14.6 %copy.201 = bf16[1536,3584]{1,0:T(8,128)(2,1)} copy(bf16[1536,3584]{0,1:T(8,128)(2,1)} %pad_maximum_fusion) | data formatting | bytes 22020096 | tf_op jit(solution)/shard_map/concatenate | solution.py:409
  736.2 37.8 %psum.7 = f32[5120]{0:T(1024)} all-reduce(f32[5120]{0:T(1024)} %constant_dynamic-update-slice_fusion.17), channel_id=1, replica_groups=mesh['rep'=8,'fsdp'=4] {'rep','fsdp'}, use_global_device_ids=true, to_apply=%region_19.20 | all-reduce | flops 5120 | bytes 40960 | tf_op jit(solution)/shard_map/psum | solution.py:433
  774.0 5.9 dynamic-slice_bitcast_fusion
  795.8 13.6 %collective-permute-done.68 = bf16[4,48,2240]{2,1,0:T(8,128)(2,1)S(1)} collective-permute-done((bf16[4,48,2240]{2,1,0:T(8,128)(2,1)S(1)}, bf16[4,48,2240]{2,1,0:T(8,128)(2,1)S(1)}, u32[]{:S(2)}, u32[]{:S(2)}) %collective-permute-start.68) | collective-permute-done | bytes 860192 | tf_op jit(solution)/shard_map/ppermute | solution.py:143
  816.2 11.6 collective-permute-done.102
  833.5 13.3 %collective-permute-done.85 = bf16[4,48,2240]{2,1,0:T(8,128)(2,1)S(1)} collective-permute-done((bf16[4,48,2240]{2,1,0:T(8,128)(2,1)S(1)}, bf16[4,48,2240]{2,1,0:T(8,128)(2,1)S(1)}, u32[]{:S(2)}, u32[]{:S(2)}) %collective-permute-start.85) | collective-permute-done | bytes 860192 | tf_op jit(solution)/shard_map/ppermute | solution.py:143
  856.0 24.3 %collective-permute-start.103 = (bf16[1120,384]{1,0:T(8,128)(2,1)S(1)}, bf16[1120,384]{1,0:T(8,128)(2,1)S(1)}, u32[]{:S(2)}, u32[]{:S(2)}) collective-permute-start(bf16[1120,384]{1,0:T(8,128)(2,1)S(1)} %get-tuple-element.107), channel_id=1, source_target_pairs={{0,8},{4,12},{8,16},{12,20},{16,24},{20,28},{1,9},{5,13},{9,17},{1... | collective-permute-start | bytes 2580488 | tf_op jit(solution)/shard_map/ppermute | solution.py:143
  883.8 17.7 %collective-permute-done.103 = bf16[1120,384]{1,0:T(8,128)(2,1)S(1)} collective-permute-done((bf16[1120,384]{1,0:T(8,128)(2,1)S(1)}, bf16[1120,384]{1,0:T(8,128)(2,1)S(1)}, u32[]{:S(2)}, u32[]{:S(2)}) %collective-permute-start.103) | collective-permute-done | bytes 860192 | tf_op jit(solution)/shard_map/ppermute | solution.py:143
  903.8 19.0 %collective-permute-done.106 = bf16[1120,384]{1,0:T(8,128)(2,1)S(1)} collective-permute-done((bf16[1120,384]{1,0:T(8,128)(2,1)S(1)}, bf16[1120,384]{1,0:T(8,128)(2,1)S(1)}, u32[]{:S(2)}, u32[]{:S(2)}) %collective-permute-start.106) | collective-permute-done | bytes 860192 | tf_op jit(solution)/shard_map/ppermute | solution.py:144
  926.4 9.7 collective-permute-start.107
  940.8 9.3 collective-permute-done.107
  956.3 7.6 collective-permute-start.76
  969.9 11.6 collective-permute-start.93
  986.7 7.6 collective-permute-done.79
  998.7 34.6 %collective-permute-done.96 = bf16[48,8960]{1,0:T(8,128)(2,1)S(1)} collective-permute-done((bf16[48,8960]{1,0:T(8,128)(2,1)}, bf16[48,8960]{1,0:T(8,128)(2,1)S(1)}, u32[]{:S(2)}, u32[]{:S(2)}) %collective-permute-start.96) | collective-permute-done | bytes 860192 | tf_op jit(solution)/shard_map/ppermute | solution.py:156
  1034.9 16.8 %collective-permute-done.111 = bf16[1120,384]{1,0:T(8,128)(2,1)S(1)} collective-permute-done((bf16[1120,384]{1,0:T(8,128)(2,1)}, bf16[1120,384]{1,0:T(8,128)(2,1)S(1)}, u32[]{:S(2)}, u32[]{:S(2)}) %collective-permute-start.111) | collective-permute-done | bytes 860192 | tf_op jit(solution)/shard_map/ppermute | solution.py:156
  1055.9 14.4 %collective-permute-done.80 = bf16[48,8960]{1,0:T(8,128)(2,1)} collective-permute-done((bf16[48,8960]{1,0:T(8,128)(2,1)}, bf16[48,8960]{1,0:T(8,128)(2,1)}, u32[]{:S(2)}, u32[]{:S(2)}) %collective-permute-start.80) | collective-permute-done | bytes 860192 | tf_op jit(solution)/shard_map/ppermute | solution.py:156
  1073.2 15.5 %collective-permute-done.97 = bf16[48,8960]{1,0:T(8,128)(2,1)} collective-permute-done((bf16[48,8960]{1,0:T(8,128)(2,1)S(1)}, bf16[48,8960]{1,0:T(8,128)(2,1)}, u32[]{:S(2)}, u32[]{:S(2)}) %collective-permute-start.97) | collective-permute-done | bytes 860192 | tf_op jit(solution)/shard_map/ppermute | solution.py:156
  1090.3 16.8 %collective-permute-done.112 = bf16[1120,384]{1,0:T(8,128)(2,1)S(1)} collective-permute-done((bf16[1120,384]{1,0:T(8,128)(2,1)S(1)}, bf16[1120,384]{1,0:T(8,128)(2,1)S(1)}, u32[]{:S(2)}, u32[]{:S(2)}) %collective-permute-start.112) | collective-permute-done | bytes 860192 | tf_op jit(solution)/shard_map/ppermute | solution.py:156
  1114.4 6.4 fusion.6
  1142.1 12.0 collective-permute-done.47
  1154.9 12.3 collective-permute-done.49
  1168.8 10.8 collective-permute-done.50
  1201.5 5.9 collective-permute-start.55
  1213.1 7.6 bitcast_convert_fusion
  1222.0 8.2 collective-permute-start.59
  1236.9 6.5 bitcast_convert_fusion.2
  1258.7 6.4 collective-permute-done.64
  1265.3 6.5 bitcast_convert_fusion.1
  (663 shorter events, 475.5 us)
Async XLA Ops:
  7.2 689.8 %reduce-scatter.2.cloned.1.call-start = ((), (), s32[]{:S(2)}) async-start(), calls=%async_computation.1 | async-start | bytes 1638400 | tf_op jit(solution)/shard_map/reduce_scatter | solution.py:386
  9.3 54.4 %collective-permute-start.7 = (bf16[96,1536]{1,0:T(8,128)(2,1)}, bf16[96,1536]{1,0:T(8,128)(2,1)}, u32[]{:S(2)}, u32[]{:S(2)}) collective-permute-start(bf16[96,1536]{1,0:T(8,128)(2,1)} %get-tuple-element.129), channel_id=1, source_target_pairs={{0,1},{1,0},{2,3},{3,2},{4,5},{5,4},{6,7},{7,6},{8,9},{9,8},{10,11... | collective-permute-start | bytes 884744 | tf_op jit(solution)/shard_map/ppermute | solution.py:90
  12.2 49.9 %collective-permute-start.9 = (bf16[96,1536]{1,0:T(8,128)(2,1)}, bf16[96,1536]{1,0:T(8,128)(2,1)}, u32[]{:S(2)}, u32[]{:S(2)}) collective-permute-start(bf16[96,1536]{1,0:T(8,128)(2,1)} %get-tuple-element.129), channel_id=1, source_target_pairs={{0,2},{1,3},{2,0},{3,1},{4,6},{5,7},{6,4},{7,5},{8,10},{9,11},{10,... | collective-permute-start | bytes 884744 | tf_op jit(solution)/shard_map/ppermute | solution.py:90
  13.8 46.7 %collective-permute-start.10 = (bf16[96,1536]{1,0:T(8,128)(2,1)}, bf16[96,1536]{1,0:T(8,128)(2,1)}, u32[]{:S(2)}, u32[]{:S(2)}) collective-permute-start(bf16[96,1536]{1,0:T(8,128)(2,1)} %get-tuple-element.130), channel_id=1, source_target_pairs={{0,2},{1,3},{2,0},{3,1},{4,6},{5,7},{6,4},{7,5},{8,10},{9,11},{10,... | collective-permute-start | bytes 884744 | tf_op jit(solution)/shard_map/ppermute | solution.py:90
  14.3 51.0 %collective-permute-start.8 = (bf16[96,1536]{1,0:T(8,128)(2,1)}, bf16[96,1536]{1,0:T(8,128)(2,1)}, u32[]{:S(2)}, u32[]{:S(2)}) collective-permute-start(bf16[96,1536]{1,0:T(8,128)(2,1)} %get-tuple-element.130), channel_id=1, source_target_pairs={{0,1},{1,0},{2,3},{3,2},{4,5},{5,4},{6,7},{7,6},{8,9},{9,8},{10,11... | collective-permute-start | bytes 884744 | tf_op jit(solution)/shard_map/ppermute | solution.py:90
  16.5 63.9 %collective-permute-start = (bf16[96,2048]{1,0:T(8,128)(2,1)}, bf16[96,2048]{1,0:T(8,128)(2,1)}, u32[]{:S(2)}, u32[]{:S(2)}) collective-permute-start(bf16[96,2048]{1,0:T(8,128)(2,1)} %get-tuple-element.151), channel_id=1, source_target_pairs={{0,1},{1,0},{2,3},{3,2},{4,5},{5,4},{6,7},{7,6},{8,9},{9,8},{10,11... | collective-permute-start | bytes 1179656 | tf_op jit(solution)/shard_map/ppermute | solution.py:90
  78.3 49.1 %collective-permute-start.36 = (bf16[160,1536]{1,0:T(8,128)(2,1)}, bf16[160,1536]{1,0:T(8,128)(2,1)S(1)}, u32[]{:S(2)}, u32[]{:S(2)}) collective-permute-start(bf16[160,1536]{1,0:T(8,128)(2,1)} %get-tuple-element.132), channel_id=1, source_target_pairs={{0,2},{1,3},{2,0},{3,1},{4,6},{5,7},{6,4},{7,5},{8,10},{9,11},{10,... | collective-permute-start | bytes 1474568 | tf_op jit(solution)/shard_map/ppermute | solution.py:90
  80.4 48.5 %collective-permute-start.37 = (bf16[160,1536]{1,0:T(8,128)(2,1)S(1)}, bf16[160,1536]{1,0:T(8,128)(2,1)S(1)}, u32[]{:S(2)}, u32[]{:S(2)}) collective-permute-start(bf16[160,1536]{1,0:T(8,128)(2,1)S(1)} %copy-done.63), channel_id=1, source_target_pairs={{0,2},{1,3},{2,0},{3,1},{4,6},{5,7},{6,4},{7,5},{8,10},{9,11},{10,... | collective-permute-start | bytes 1474568 | tf_op jit(solution)/shard_map/ppermute | solution.py:90
  88.1 37.5 %collective-permute-start.11 = (bf16[96,1536]{1,0:T(8,128)(2,1)}, bf16[96,1536]{1,0:T(8,128)(2,1)S(1)}, u32[]{:S(2)}, u32[]{:S(2)}) collective-permute-start(bf16[96,1536]{1,0:T(8,128)(2,1)} %collective-permute-done.7), channel_id=1, source_target_pairs={{0,2},{1,3},{2,0},{3,1},{4,6},{5,7},{6,4},{7,5},{8,10},{9,11},{10,... | collective-permute-start | bytes 884744 | tf_op jit(solution)/shard_map/ppermute | solution.py:90
  97.1 59.6 %collective-permute-start.22 = (bf16[192,2240]{1,0:T(8,128)(2,1)S(1)}, bf16[192,2240]{1,0:T(8,128)(2,1)S(1)}, u32[]{:S(2)}, u32[]{:S(2)}) collective-permute-start(bf16[192,2240]{1,0:T(8,128)(2,1)S(1)} %copy-done.56), channel_id=1, source_target_pairs={{0,3},{1,2},{2,1},{3,0},{4,7},{5,6},{6,5},{7,4},{8,11},{9,10},{10,... | collective-permute-start | bytes 2580488 | tf_op jit(solution)/shard_map/ppermute | solution.py:241
  103.4 55.2 %collective-permute-start.21 = (bf16[192,2240]{1,0:T(8,128)(2,1)S(1)}, bf16[192,2240]{1,0:T(8,128)(2,1)S(1)}, u32[]{:S(2)}, u32[]{:S(2)}) collective-permute-start(bf16[192,2240]{1,0:T(8,128)(2,1)S(1)} %copy-done.55), channel_id=1, source_target_pairs={{0,2},{1,3},{2,0},{3,1},{4,6},{5,7},{6,4},{7,5},{8,10},{9,11},{10,... | collective-permute-start | bytes 2580488 | tf_op jit(solution)/shard_map/ppermute | solution.py:241
  128.1 32.7 %collective-permute-start.20 = (bf16[192,2240]{1,0:T(8,128)(2,1)S(1)}, bf16[192,2240]{1,0:T(8,128)(2,1)S(1)}, u32[]{:S(2)}, u32[]{:S(2)}) collective-permute-start(bf16[192,2240]{1,0:T(8,128)(2,1)S(1)} %copy-done.54), channel_id=1, source_target_pairs={{0,1},{1,0},{2,3},{3,2},{4,5},{5,4},{6,7},{7,6},{8,9},{9,8},{10,11... | collective-permute-start | bytes 2580488 | tf_op jit(solution)/shard_map/ppermute | solution.py:241
  137.7 76.6 %collective-permute-start.13 = (bf16[4,192,1536]{2,1,0:T(8,128)(2,1)S(1)}, bf16[4,192,1536]{2,1,0:T(8,128)(2,1)S(1)}, u32[]{:S(2)}, u32[]{:S(2)}) collective-permute-start(bf16[4,192,1536]{2,1,0:T(8,128)(2,1)S(1)} %get-tuple-element.120), channel_id=1, source_target_pairs={{0,4},{4,0},{8,12},{12,8},{16,20},{20,16},{24,28},{28,24},{1,5},{5... | collective-permute-start | bytes 7077896 | tf_op jit(solution)/shard_map/ppermute | solution.py:117
  156.7 41.5 %collective-permute-start.25 = (bf16[192,2240]{1,0:T(8,128)(2,1)S(1)}, bf16[192,2240]{1,0:T(8,128)(2,1)S(1)}, u32[]{:S(2)}, u32[]{:S(2)}) collective-permute-start(bf16[192,2240]{1,0:T(8,128)(2,1)S(1)} %copy-done.52), channel_id=1, source_target_pairs={{0,2},{1,3},{2,0},{3,1},{4,6},{5,7},{6,4},{7,5},{8,10},{9,11},{10,... | collective-permute-start | bytes 2580488 | tf_op jit(solution)/shard_map/ppermute | solution.py:241
  158.6 39.6 %collective-permute-start.24 = (bf16[192,2240]{1,0:T(8,128)(2,1)S(1)}, bf16[192,2240]{1,0:T(8,128)(2,1)S(1)}, u32[]{:S(2)}, u32[]{:S(2)}) collective-permute-start(bf16[192,2240]{1,0:T(8,128)(2,1)S(1)} %copy-done.51), channel_id=1, source_target_pairs={{0,1},{1,0},{2,3},{3,2},{4,5},{5,4},{6,7},{7,6},{8,9},{9,8},{10,11... | collective-permute-start | bytes 2580488 | tf_op jit(solution)/shard_map/ppermute | solution.py:241
  160.7 47.4 %collective-permute-start.38 = (bf16[160,1536]{1,0:T(8,128)(2,1)S(1)}, bf16[160,1536]{1,0:T(8,128)(2,1)S(1)}, u32[]{:S(2)}, u32[]{:S(2)}) collective-permute-start(bf16[160,1536]{1,0:T(8,128)(2,1)S(1)} %collective-permute-done.34), channel_id=1, source_target_pairs={{0,2},{1,3},{2,0},{3,1},{4,6},{5,7},{6,4},{7,5},{8,10},{9,11},{10,... | collective-permute-start | bytes 1474568 | tf_op jit(solution)/shard_map/ppermute | solution.py:90
  180.0 33.5 %collective-permute-start.39 = (bf16[160,1536]{1,0:T(8,128)(2,1)S(1)}, bf16[160,1536]{1,0:T(8,128)(2,1)S(1)}, u32[]{:S(2)}, u32[]{:S(2)}) collective-permute-start(bf16[160,1536]{1,0:T(8,128)(2,1)S(1)} %collective-permute-done.37), channel_id=1, source_target_pairs={{0,1},{1,0},{2,3},{3,2},{4,5},{5,4},{6,7},{7,6},{8,9},{9,8},{10,11... | collective-permute-start | bytes 1474568 | tf_op jit(solution)/shard_map/ppermute | solution.py:90
  198.2 106.4 %collective-permute-start.23 = (bf16[4,192,2240]{2,1,0:T(8,128)(2,1)}, bf16[4,192,2240]{2,1,0:T(8,128)(2,1)}, u32[]{:S(2)}, u32[]{:S(2)}) collective-permute-start(bf16[4,192,2240]{2,1,0:T(8,128)(2,1)} %get-tuple-element.102), channel_id=1, source_target_pairs={{0,4},{4,0},{8,12},{12,8},{16,20},{20,16},{24,28},{28,24},{1,5},{5... | collective-permute-start | bytes 10321928 | tf_op jit(solution)/shard_map/ppermute | solution.py:117
  208.1 97.3 %collective-permute-start.27 = (bf16[4,192,2240]{2,1,0:T(8,128)(2,1)}, bf16[4,192,2240]{2,1,0:T(8,128)(2,1)}, u32[]{:S(2)}, u32[]{:S(2)}) collective-permute-start(bf16[4,192,2240]{2,1,0:T(8,128)(2,1)} %get-tuple-element.104), channel_id=1, source_target_pairs={{0,4},{4,0},{8,12},{12,8},{16,20},{20,16},{24,28},{28,24},{1,5},{5... | collective-permute-start | bytes 10321928 | tf_op jit(solution)/shard_map/ppermute | solution.py:117
  300.8 30.4 %collective-permute-start.14 = (bf16[160,1536]{1,0:T(8,128)(2,1)}, bf16[160,1536]{1,0:T(8,128)(2,1)S(1)}, u32[]{:S(2)}, u32[]{:S(2)}) collective-permute-start(bf16[160,1536]{1,0:T(8,128)(2,1)} %get-tuple-element.134), channel_id=1, source_target_pairs={{0,1},{1,0},{2,3},{3,2},{4,5},{5,4},{6,7},{7,6},{8,9},{9,8},{10,11... | collective-permute-start | bytes 1474568 | tf_op jit(solution)/shard_map/ppermute | solution.py:90
  302.0 34.0 %collective-permute-start.16 = (bf16[160,1536]{1,0:T(8,128)(2,1)}, bf16[160,1536]{1,0:T(8,128)(2,1)S(1)}, u32[]{:S(2)}, u32[]{:S(2)}) collective-permute-start(bf16[160,1536]{1,0:T(8,128)(2,1)} %get-tuple-element.134), channel_id=1, source_target_pairs={{0,2},{1,3},{2,0},{3,1},{4,6},{5,7},{6,4},{7,5},{8,10},{9,11},{10,... | collective-permute-start | bytes 1474568 | tf_op jit(solution)/shard_map/ppermute | solution.py:90
  302.8 31.4 %collective-permute-start.15 = (bf16[160,1536]{1,0:T(8,128)(2,1)}, bf16[160,1536]{1,0:T(8,128)(2,1)}, u32[]{:S(2)}, u32[]{:S(2)}) collective-permute-start(bf16[160,1536]{1,0:T(8,128)(2,1)} %get-tuple-element.133), channel_id=1, source_target_pairs={{0,1},{1,0},{2,3},{3,2},{4,5},{5,4},{6,7},{7,6},{8,9},{9,8},{10,11... | collective-permute-start | bytes 1474568 | tf_op jit(solution)/shard_map/ppermute | solution.py:90
  477.1 37.7 %collective-permute-start.41 = (bf16[160,1536]{1,0:T(8,128)(2,1)}, bf16[160,1536]{1,0:T(8,128)(2,1)}, u32[]{:S(2)}, u32[]{:S(2)}) collective-permute-start(bf16[160,1536]{1,0:T(8,128)(2,1)} %get-tuple-element.88), channel_id=1, source_target_pairs={{0,2},{1,3},{2,0},{3,1},{4,6},{5,7},{6,4},{7,5},{8,10},{9,11},{10,... | collective-permute-start | bytes 1474568 | tf_op jit(solution)/shard_map/ppermute | solution.py:107
  478.0 41.8 %collective-permute-start.40 = (bf16[160,1536]{1,0:T(8,128)(2,1)}, bf16[160,1536]{1,0:T(8,128)(2,1)S(1)}, u32[]{:S(2)}, u32[]{:S(2)}) collective-permute-start(bf16[160,1536]{1,0:T(8,128)(2,1)} %get-tuple-element.85), channel_id=1, source_target_pairs={{0,2},{1,3},{2,0},{3,1},{4,6},{5,7},{6,4},{7,5},{8,10},{9,11},{10,... | collective-permute-start | bytes 1474568 | tf_op jit(solution)/shard_map/ppermute | solution.py:107
  479.2 41.9 %collective-permute-start.44 = (bf16[160,1536]{1,0:T(8,128)(2,1)}, bf16[160,1536]{1,0:T(8,128)(2,1)S(1)}, u32[]{:S(2)}, u32[]{:S(2)}) collective-permute-start(bf16[160,1536]{1,0:T(8,128)(2,1)} %get-tuple-element.86), channel_id=1, source_target_pairs={{0,1},{1,0},{2,3},{3,2},{4,5},{5,4},{6,7},{7,6},{8,9},{9,8},{10,11... | collective-permute-start | bytes 1474568 | tf_op jit(solution)/shard_map/ppermute | solution.py:107
  480.0 78.2 %collective-permute-start.43 = (bf16[160,1536]{1,0:T(8,128)(2,1)S(1)}, bf16[160,1536]{1,0:T(8,128)(2,1)S(1)}, u32[]{:S(2)}, u32[]{:S(2)}) collective-permute-start(bf16[160,1536]{1,0:T(8,128)(2,1)S(1)} %get-tuple-element.87), channel_id=1, source_target_pairs={{0,1},{1,0},{2,3},{3,2},{4,5},{5,4},{6,7},{7,6},{8,9},{9,8},{10,11... | collective-permute-start | bytes 1474568 | tf_op jit(solution)/shard_map/ppermute | solution.py:107
  482.1 35.4 %collective-permute-start.29 = (bf16[160,1536]{1,0:T(8,128)(2,1)}, bf16[160,1536]{1,0:T(8,128)(2,1)}, u32[]{:S(2)}, u32[]{:S(2)}) collective-permute-start(bf16[160,1536]{1,0:T(8,128)(2,1)} %get-tuple-element.92), channel_id=1, source_target_pairs={{0,2},{1,3},{2,0},{3,1},{4,6},{5,7},{6,4},{7,5},{8,10},{9,11},{10,... | collective-permute-start | bytes 1474568 | tf_op jit(solution)/shard_map/ppermute | solution.py:107
  521.1 48.8 %collective-permute-start.31 = (bf16[160,1536]{1,0:T(8,128)(2,1)S(1)}, bf16[160,1536]{1,0:T(8,128)(2,1)S(1)}, u32[]{:S(2)}, u32[]{:S(2)}) collective-permute-start(bf16[160,1536]{1,0:T(8,128)(2,1)S(1)} %get-tuple-element.91), channel_id=1, source_target_pairs={{0,1},{1,0},{2,3},{3,2},{4,5},{5,4},{6,7},{7,6},{8,9},{9,8},{10,11... | collective-permute-start | bytes 1474568 | tf_op jit(solution)/shard_map/ppermute | solution.py:107
  534.4 134.5 %collective-permute-start.66 = (bf16[4,192,2240]{2,1,0:T(8,128)(2,1)}, bf16[4,192,2240]{2,1,0:T(8,128)(2,1)}, u32[]{:S(2)}, u32[]{:S(2)}) collective-permute-start(bf16[4,192,2240]{2,1,0:T(8,128)(2,1)} %dynamic-slice_bitcast_fusion.2), channel_id=1, source_target_pairs={{0,4},{4,0},{8,12},{12,8},{16,20},{20,16},{24,28},{28,24},{1,5},{5... | collective-permute-start | bytes 10321928 | tf_op jit(solution)/shard_map/ppermute | solution.py:117
  542.3 137.1 %collective-permute-start.83 = (bf16[4,192,2240]{2,1,0:T(8,128)(2,1)}, bf16[4,192,2240]{2,1,0:T(8,128)(2,1)}, u32[]{:S(2)}, u32[]{:S(2)}) collective-permute-start(bf16[4,192,2240]{2,1,0:T(8,128)(2,1)} %dynamic-slice_bitcast_fusion.1), channel_id=1, source_target_pairs={{0,4},{4,0},{8,12},{12,8},{16,20},{20,16},{24,28},{28,24},{1,5},{5... | collective-permute-start | bytes 10321928 | tf_op jit(solution)/shard_map/ppermute | solution.py:117
  558.2 129.3 %collective-permute-start.100 = (bf16[1,1120,1536]{2,1,0:T(8,128)(2,1)}, bf16[1,1120,1536]{2,1,0:T(8,128)(2,1)}, u32[]{:S(2)}, u32[]{:S(2)}) collective-permute-start(bf16[1,1120,1536]{2,1,0:T(8,128)(2,1)} %dynamic-slice_bitcast_fusion.3), channel_id=1, source_target_pairs={{0,4},{4,0},{8,12},{12,8},{16,20},{20,16},{24,28},{28,24},{1,5},{5... | collective-permute-start | bytes 10321928 | tf_op jit(solution)/shard_map/ppermute | solution.py:117
  673.4 109.3 %collective-permute-start.67 = (bf16[4,48,2240]{2,1,0:T(8,128)(2,1)}, bf16[4,48,2240]{2,1,0:T(8,128)(2,1)}, u32[]{:S(2)}, u32[]{:S(2)}) collective-permute-start(bf16[4,48,2240]{2,1,0:T(8,128)(2,1)} %get-tuple-element.99), channel_id=1, source_target_pairs={{0,8},{4,12},{1,9},{5,13},{2,10},{6,14},{3,11},{7,15}} | collective-permute-start | bytes 2580488 | tf_op jit(solution)/shard_map/ppermute | solution.py:143
  677.7 118.0 %collective-permute-start.70 = (bf16[4,48,2240]{2,1,0:T(8,128)(2,1)}, bf16[4,48,2240]{2,1,0:T(8,128)(2,1)}, u32[]{:S(2)}, u32[]{:S(2)}) collective-permute-start(bf16[4,48,2240]{2,1,0:T(8,128)(2,1)} %get-tuple-element.100), channel_id=1, source_target_pairs={{24,16},{28,20},{25,17},{29,21},{26,18},{30,22},{27,19},{31,23}} | collective-permute-start | bytes 2580488 | tf_op jit(solution)/shard_map/ppermute | solution.py:144
  683.7 107.1 %collective-permute-start.84 = (bf16[4,48,2240]{2,1,0:T(8,128)(2,1)}, bf16[4,48,2240]{2,1,0:T(8,128)(2,1)}, u32[]{:S(2)}, u32[]{:S(2)}) collective-permute-start(bf16[4,48,2240]{2,1,0:T(8,128)(2,1)} %get-tuple-element.95), channel_id=1, source_target_pairs={{0,8},{4,12},{1,9},{5,13},{2,10},{6,14},{3,11},{7,15}} | collective-permute-start | bytes 2580488 | tf_op jit(solution)/shard_map/ppermute | solution.py:143
  685.9 146.9 %collective-permute-start.87 = (bf16[4,48,2240]{2,1,0:T(8,128)(2,1)}, bf16[4,48,2240]{2,1,0:T(8,128)(2,1)}, u32[]{:S(2)}, u32[]{:S(2)}) collective-permute-start(bf16[4,48,2240]{2,1,0:T(8,128)(2,1)} %get-tuple-element.96), channel_id=1, source_target_pairs={{24,16},{28,20},{25,17},{29,21},{26,18},{30,22},{27,19},{31,23}} | collective-permute-start | bytes 2580488 | tf_op jit(solution)/shard_map/ppermute | solution.py:144
  694.7 90.1 %collective-permute-start.101 = (bf16[1120,384]{1,0:T(8,128)(2,1)}, bf16[1120,384]{1,0:T(8,128)(2,1)}, u32[]{:S(2)}, u32[]{:S(2)}) collective-permute-start(bf16[1120,384]{1,0:T(8,128)(2,1)} %get-tuple-element.109), channel_id=1, source_target_pairs={{0,8},{4,12},{1,9},{5,13},{2,10},{6,14},{3,11},{7,15}} | collective-permute-start | bytes 2580488 | tf_op jit(solution)/shard_map/ppermute | solution.py:143
  782.7 32.8 %collective-permute-start.104 = (bf16[1120,384]{1,0:T(8,128)(2,1)S(1)}, bf16[1120,384]{1,0:T(8,128)(2,1)S(1)}, u32[]{:S(2)}, u32[]{:S(2)}) collective-permute-start(bf16[1120,384]{1,0:T(8,128)(2,1)S(1)} %copy-done.61), channel_id=1, source_target_pairs={{24,16},{28,20},{25,17},{29,21},{26,18},{30,22},{27,19},{31,23}} | collective-permute-start | bytes 2580488 | tf_op jit(solution)/shard_map/ppermute | solution.py:144
  790.8 37.0 %collective-permute-start.102 = (bf16[1120,384]{1,0:T(8,128)(2,1)S(1)}, bf16[1120,384]{1,0:T(8,128)(2,1)S(1)}, u32[]{:S(2)}, u32[]{:S(2)}) collective-permute-start(bf16[1120,384]{1,0:T(8,128)(2,1)S(1)} %fusion.59), channel_id=1, source_target_pairs={{0,8},{4,12},{8,16},{12,20},{1,9},{5,13},{9,17},{13,21},{2,10},{6,... | collective-permute-start | bytes 2580488 | tf_op jit(solution)/shard_map/ppermute | solution.py:143
  795.7 317.4 %collective-permute-start.46 = (bf16[4,192,3584]{2,1,0:T(8,128)(2,1)}, bf16[4,192,3584]{2,1,0:T(8,128)(2,1)}, u32[]{:S(2)}, u32[]{:S(2)}) collective-permute-start(bf16[4,192,3584]{2,1,0:T(8,128)(2,1)} %dynamic-slice_bitcast_fusion), channel_id=1, source_target_pairs={{0,4},{4,0},{8,12},{12,8},{16,20},{20,16},{24,28},{28,24},{1,5},{5... | collective-permute-start | bytes 16515080 | tf_op jit(solution)/shard_map/ppermute | solution.py:117
  809.4 37.4 %collective-permute-start.85 = (bf16[4,48,2240]{2,1,0:T(8,128)(2,1)S(1)}, bf16[4,48,2240]{2,1,0:T(8,128)(2,1)S(1)}, u32[]{:S(2)}, u32[]{:S(2)}) collective-permute-start(bf16[4,48,2240]{2,1,0:T(8,128)(2,1)S(1)} %fusion.47), channel_id=1, source_target_pairs={{0,8},{4,12},{8,16},{12,20},{1,9},{5,13},{9,17},{13,21},{2,10},{6,... | collective-permute-start | bytes 2580488 | tf_op jit(solution)/shard_map/ppermute | solution.py:143
  815.5 33.6 %collective-permute-start.71 = (bf16[4,48,2240]{2,1,0:T(8,128)(2,1)S(1)}, bf16[4,48,2240]{2,1,0:T(8,128)(2,1)S(1)}, u32[]{:S(2)}, u32[]{:S(2)}) collective-permute-start(bf16[4,48,2240]{2,1,0:T(8,128)(2,1)S(1)} %get-tuple-element.98), channel_id=1, source_target_pairs={{16,8},{20,12},{24,16},{28,20},{17,9},{21,13},{25,17},{29,21},{18,... | collective-permute-start | bytes 2580488 | tf_op jit(solution)/shard_map/ppermute | solution.py:144
  827.8 52.7 %collective-permute-start.69 = (bf16[4,48,2240]{2,1,0:T(8,128)(2,1)S(1)}, bf16[4,48,2240]{2,1,0:T(8,128)(2,1)S(1)}, u32[]{:S(2)}, u32[]{:S(2)}) collective-permute-start(bf16[4,48,2240]{2,1,0:T(8,128)(2,1)S(1)} %get-tuple-element.97), channel_id=1, source_target_pairs={{0,8},{4,12},{8,16},{12,20},{16,24},{20,28},{1,9},{5,13},{9,17},{1... | collective-permute-start | bytes 2580488 | tf_op jit(solution)/shard_map/ppermute | solution.py:143
  849.2 75.7 %collective-permute-start.86 = (bf16[4,48,2240]{2,1,0:T(8,128)(2,1)S(1)}, bf16[4,48,2240]{2,1,0:T(8,128)(2,1)S(1)}, u32[]{:S(2)}, u32[]{:S(2)}) collective-permute-start(bf16[4,48,2240]{2,1,0:T(8,128)(2,1)S(1)} %get-tuple-element.93), channel_id=1, source_target_pairs={{0,8},{4,12},{8,16},{12,20},{16,24},{20,28},{1,9},{5,13},{9,17},{1... | collective-permute-start | bytes 2580488 | tf_op jit(solution)/shard_map/ppermute | solution.py:143
  856.0 45.5 %collective-permute-start.103 = (bf16[1120,384]{1,0:T(8,128)(2,1)S(1)}, bf16[1120,384]{1,0:T(8,128)(2,1)S(1)}, u32[]{:S(2)}, u32[]{:S(2)}) collective-permute-start(bf16[1120,384]{1,0:T(8,128)(2,1)S(1)} %get-tuple-element.107), channel_id=1, source_target_pairs={{0,8},{4,12},{8,16},{12,20},{16,24},{20,28},{1,9},{5,13},{9,17},{1... | collective-permute-start | bytes 2580488 | tf_op jit(solution)/shard_map/ppermute | solution.py:143
  880.5 45.8 %collective-permute-start.89 = (bf16[4,48,2240]{2,1,0:T(8,128)(2,1)S(1)}, bf16[4,48,2240]{2,1,0:T(8,128)(2,1)S(1)}, u32[]{:S(2)}, u32[]{:S(2)}) collective-permute-start(bf16[4,48,2240]{2,1,0:T(8,128)(2,1)S(1)} %fusion.46), channel_id=1, source_target_pairs={{8,0},{12,4},{16,8},{20,12},{24,16},{28,20},{9,1},{13,5},{17,9},{2... | collective-permute-start | bytes 2580488 | tf_op jit(solution)/shard_map/ppermute | solution.py:144
  881.8 40.9 %collective-permute-start.106 = (bf16[1120,384]{1,0:T(8,128)(2,1)S(1)}, bf16[1120,384]{1,0:T(8,128)(2,1)S(1)}, u32[]{:S(2)}, u32[]{:S(2)}) collective-permute-start(bf16[1120,384]{1,0:T(8,128)(2,1)S(1)} %fusion.58), channel_id=1, source_target_pairs={{8,0},{12,4},{16,8},{20,12},{24,16},{28,20},{9,1},{13,5},{17,9},{2... | collective-permute-start | bytes 2580488 | tf_op jit(solution)/shard_map/ppermute | solution.py:144
  901.5 35.8 %collective-permute-start.75 = (bf16[48,2240]{1,0:T(8,128)(2,1)S(1)}, bf16[48,2240]{1,0:T(8,128)(2,1)S(1)}, u32[]{:S(2)}, u32[]{:S(2)}) collective-permute-start(bf16[48,2240]{1,0:T(8,128)(2,1)S(1)} %get-tuple-element.148), channel_id=1, source_target_pairs={{0,3},{1,2},{2,1},{3,0},{4,7},{5,6},{6,5},{7,4},{8,11},{9,10},{10,... | collective-permute-start | bytes 645128 | tf_op jit(solution)/shard_map/ppermute | solution.py:346
  955.0 29.1 %collective-permute-start.110 = (bf16[1120,384]{1,0:T(8,128)(2,1)S(1)}, bf16[1120,384]{1,0:T(8,128)(2,1)}, u32[]{:S(2)}, u32[]{:S(2)}) collective-permute-start(bf16[1120,384]{1,0:T(8,128)(2,1)S(1)} %copy-done.41), channel_id=1, source_target_pairs={{8,0},{12,4},{16,8},{20,12},{24,16},{28,20},{9,1},{13,5},{17,9},{2... | collective-permute-start | bytes 2580488 | tf_op jit(solution)/shard_map/ppermute | solution.py:156
  956.3 29.1 %collective-permute-start.76 = (bf16[48,8960]{1,0:T(8,128)(2,1)}, bf16[48,8960]{1,0:T(8,128)(2,1)}, u32[]{:S(2)}, u32[]{:S(2)}) collective-permute-start(bf16[48,8960]{1,0:T(8,128)(2,1)} %reshape.577), channel_id=1, source_target_pairs={{0,8},{4,12},{8,16},{12,20},{16,24},{20,28},{1,9},{5,13},{9,17},{1... | collective-permute-start | bytes 2580488 | tf_op jit(solution)/shard_map/ppermute | solution.py:155
  963.9 30.5 %collective-permute-start.79 = (bf16[48,8960]{1,0:T(8,128)(2,1)}, bf16[48,8960]{1,0:T(8,128)(2,1)}, u32[]{:S(2)}, u32[]{:S(2)}) collective-permute-start(bf16[48,8960]{1,0:T(8,128)(2,1)} %reshape.577), channel_id=1, source_target_pairs={{8,0},{12,4},{16,8},{20,12},{24,16},{28,20},{9,1},{13,5},{17,9},{2... | collective-permute-start | bytes 2580488 | tf_op jit(solution)/shard_map/ppermute | solution.py:156
  984.1 49.3 %collective-permute-start.96 = (bf16[48,8960]{1,0:T(8,128)(2,1)}, bf16[48,8960]{1,0:T(8,128)(2,1)S(1)}, u32[]{:S(2)}, u32[]{:S(2)}) collective-permute-start(bf16[48,8960]{1,0:T(8,128)(2,1)} %reshape.581), channel_id=1, source_target_pairs={{8,0},{12,4},{16,8},{20,12},{24,16},{28,20},{9,1},{13,5},{17,9},{2... | collective-permute-start | bytes 2580488 | tf_op jit(solution)/shard_map/ppermute | solution.py:156
  985.4 66.4 %collective-permute-start.111 = (bf16[1120,384]{1,0:T(8,128)(2,1)}, bf16[1120,384]{1,0:T(8,128)(2,1)S(1)}, u32[]{:S(2)}, u32[]{:S(2)}) collective-permute-start(bf16[1120,384]{1,0:T(8,128)(2,1)} %collective-permute-done.110), channel_id=1, source_target_pairs={{8,0},{12,4},{16,8},{20,12},{9,1},{13,5},{17,9},{21,13},{10,2},{14... | collective-permute-start | bytes 2580488 | tf_op jit(solution)/shard_map/ppermute | solution.py:156
  994.3 58.8 %collective-permute-start.77 = (bf16[48,8960]{1,0:T(8,128)(2,1)}, bf16[48,8960]{1,0:T(8,128)(2,1)}, u32[]{:S(2)}, u32[]{:S(2)}) collective-permute-start(bf16[48,8960]{1,0:T(8,128)(2,1)} %collective-permute-done.76), channel_id=1, source_target_pairs={{8,16},{12,20},{16,24},{20,28},{9,17},{13,21},{17,25},{21,29},{10,... | collective-permute-start | bytes 2580488 | tf_op jit(solution)/shard_map/ppermute | solution.py:155
  997.4 72.9 %collective-permute-start.80 = (bf16[48,8960]{1,0:T(8,128)(2,1)}, bf16[48,8960]{1,0:T(8,128)(2,1)}, u32[]{:S(2)}, u32[]{:S(2)}) collective-permute-start(bf16[48,8960]{1,0:T(8,128)(2,1)} %collective-permute-done.79), channel_id=1, source_target_pairs={{8,0},{12,4},{16,8},{20,12},{9,1},{13,5},{17,9},{21,13},{10,2},{14... | collective-permute-start | bytes 2580488 | tf_op jit(solution)/shard_map/ppermute | solution.py:156
  1033.4 38.6 %collective-permute-start.94 = (bf16[48,8960]{1,0:T(8,128)(2,1)S(1)}, bf16[48,8960]{1,0:T(8,128)(2,1)}, u32[]{:S(2)}, u32[]{:S(2)}) collective-permute-start(bf16[48,8960]{1,0:T(8,128)(2,1)S(1)} %collective-permute-done.93), channel_id=1, source_target_pairs={{8,16},{12,20},{16,24},{20,28},{9,17},{13,21},{17,25},{21,29},{10,... | collective-permute-start | bytes 2580488 | tf_op jit(solution)/shard_map/ppermute | solution.py:155
  1051.8 37.0 %collective-permute-start.97 = (bf16[48,8960]{1,0:T(8,128)(2,1)S(1)}, bf16[48,8960]{1,0:T(8,128)(2,1)}, u32[]{:S(2)}, u32[]{:S(2)}) collective-permute-start(bf16[48,8960]{1,0:T(8,128)(2,1)S(1)} %collective-permute-done.96), channel_id=1, source_target_pairs={{8,0},{12,4},{16,8},{20,12},{9,1},{13,5},{17,9},{21,13},{10,2},{14... | collective-permute-start | bytes 2580488 | tf_op jit(solution)/shard_map/ppermute | solution.py:156
  1053.1 54.0 %collective-permute-start.112 = (bf16[1120,384]{1,0:T(8,128)(2,1)S(1)}, bf16[1120,384]{1,0:T(8,128)(2,1)S(1)}, u32[]{:S(2)}, u32[]{:S(2)}) collective-permute-start(bf16[1120,384]{1,0:T(8,128)(2,1)S(1)} %collective-permute-done.111), channel_id=1, source_target_pairs={{8,0},{12,4},{9,1},{13,5},{10,2},{14,6},{11,3},{15,7}} | collective-permute-start | bytes 2580488 | tf_op jit(solution)/shard_map/ppermute | solution.py:156
  1070.3 52.4 %collective-permute-start.78 = (bf16[48,8960]{1,0:T(8,128)(2,1)}, bf16[48,8960]{1,0:T(8,128)(2,1)}, u32[]{:S(2)}, u32[]{:S(2)}) collective-permute-start(bf16[48,8960]{1,0:T(8,128)(2,1)} %collective-permute-done.77), channel_id=1, source_target_pairs={{16,24},{20,28},{17,25},{21,29},{18,26},{22,30},{19,27},{23,31}} | collective-permute-start | bytes 2580488 | tf_op jit(solution)/shard_map/ppermute | solution.py:155
  1071.9 62.1 %collective-permute-start.81 = (bf16[48,8960]{1,0:T(8,128)(2,1)}, bf16[48,8960]{1,0:T(8,128)(2,1)}, u32[]{:S(2)}, u32[]{:S(2)}) collective-permute-start(bf16[48,8960]{1,0:T(8,128)(2,1)} %collective-permute-done.80), channel_id=1, source_target_pairs={{8,0},{12,4},{9,1},{13,5},{10,2},{14,6},{11,3},{15,7}} | collective-permute-start | bytes 2580488 | tf_op jit(solution)/shard_map/ppermute | solution.py:156
  1088.8 41.3 %collective-permute-start.95 = (bf16[48,8960]{1,0:T(8,128)(2,1)}, bf16[48,8960]{1,0:T(8,128)(2,1)}, u32[]{:S(2)}, u32[]{:S(2)}) collective-permute-start(bf16[48,8960]{1,0:T(8,128)(2,1)} %collective-permute-done.94), channel_id=1, source_target_pairs={{16,24},{20,28},{17,25},{21,29},{18,26},{22,30},{19,27},{23,31}} | collective-permute-start | bytes 2580488 | tf_op jit(solution)/shard_map/ppermute | solution.py:155
  1107.1 88.4 %collective-permute-start.98 = (bf16[48,8960]{1,0:T(8,128)(2,1)}, bf16[48,8960]{1,0:T(8,128)(2,1)}, u32[]{:S(2)}, u32[]{:S(2)}) collective-permute-start(bf16[48,8960]{1,0:T(8,128)(2,1)} %collective-permute-done.97), channel_id=1, source_target_pairs={{8,0},{12,4},{9,1},{13,5},{10,2},{14,6},{11,3},{15,7}} | collective-permute-start | bytes 2580488 | tf_op jit(solution)/shard_map/ppermute | solution.py:156
  1113.1 95.7 %collective-permute-start.113 = (bf16[1120,1536]{1,0:T(8,128)(2,1)}, bf16[1120,1536]{1,0:T(8,128)(2,1)}, u32[]{:S(2)}, u32[]{:S(2)}) collective-permute-start(bf16[1120,1536]{1,0:T(8,128)(2,1)} %get-tuple-element.106), channel_id=1, source_target_pairs={{0,4},{4,0},{8,12},{12,8},{16,20},{20,16},{24,28},{28,24},{1,5},{5... | collective-permute-start | bytes 10321928 | tf_op jit(solution)/shard_map/ppermute | solution.py:117
  1154.9 76.6 %collective-permute-start.82 = (bf16[192,8960]{1,0:T(8,128)(2,1)S(1)}, bf16[192,8960]{1,0:T(8,128)(2,1)}, u32[]{:S(2)}, u32[]{:S(2)}) collective-permute-start(bf16[192,8960]{1,0:T(8,128)(2,1)S(1)} %bitcast.513), channel_id=1, source_target_pairs={{0,4},{4,0},{8,12},{12,8},{16,20},{20,16},{24,28},{28,24},{1,5},{5... | collective-permute-start | bytes 10321928 | tf_op jit(solution)/shard_map/ppermute | solution.py:117
  1201.5 44.0 %collective-permute-start.99 = (bf16[192,8960]{1,0:T(8,128)(2,1)S(1)}, bf16[192,8960]{1,0:T(8,128)(2,1)}, u32[]{:S(2)}, u32[]{:S(2)}) collective-permute-start(bf16[192,8960]{1,0:T(8,128)(2,1)S(1)} %bitcast.515), channel_id=1, source_target_pairs={{0,4},{4,0},{8,12},{12,8},{16,20},{20,16},{24,28},{28,24},{1,5},{5... | collective-permute-start | bytes 10321928 | tf_op jit(solution)/shard_map/ppermute | solution.py:117
  (162 other events, 3025.6 us)
Sparse Core Ops, SparseCore 0:
  645.1 29.3 reduce-scatter.1

commit v2 on v1

--- a/solution.py
+++ b/solution.py
@@ -1,6 +1,8 @@
 import jax
 import jax.numpy as jnp
 from jax import lax
+from jax.experimental import pallas as pl
+from jax.experimental.pallas import tpu as pltpu
 from jax.sharding import PartitionSpec as P
 
 HEADS = 12
@@ -166,6 +168,487 @@
     count = len(pieces)
     stacked = jnp.stack(pieces)
     return jnp.stack([pick(stacked, here ^ j) for j in range(count)])
+
+
+MESH = pl.DeviceIdType.MESH
+MASKED = -1e30
+
+
+def dot_f32(left, right, dims=((1,), (0,))):
+    return lax.dot_general(left, right, (dims, ((), ())), preferred_element_type=jnp.float32)
+
+
+def layout_of(positions, lengths_ref, starts_ref):
+    end = jnp.int32(0)
+    doc = jnp.zeros_like(positions)
+    before = jnp.zeros_like(positions)
+    piece = jnp.zeros_like(positions)
+    for i in range(lengths_ref.shape[1]):
+        end = end + lengths_ref[0, i]
+        passed = positions >= end
+        doc = doc + jnp.where(passed, 1, 0)
+        before = before + jnp.where(passed, lengths_ref[0, i], 0)
+    for i in range(starts_ref.shape[1]):
+        first = starts_ref[0, i]
+        inside = (positions >= first) & (positions < first + PIECE)
+        piece = piece + jnp.where(inside, i + 1, 0)
+    return doc, positions - before, piece
+
+
+def mask_bias(here, rows, row_len, lengths_ref, starts_ref):
+    query_pos = here * rows + lax.broadcasted_iota(jnp.int32, (rows, 1), 0)
+    key_pos = lax.broadcasted_iota(jnp.int32, (1, row_len), 1)
+    query_doc, query_rel, query_piece = layout_of(query_pos, lengths_ref, starts_ref)
+    key_doc, unused, key_piece = layout_of(key_pos, lengths_ref, starts_ref)
+    allowed = (query_doc == key_doc) & (
+        (key_pos <= query_pos) | ((query_piece == key_piece) & (query_piece > 0))
+    )
+    return jnp.where(allowed, 0.0, MASKED), query_rel
+
+
+class Links:
+    def __init__(self):
+        self.here = lax.axis_index("fsdp")
+        self.rep = lax.axis_index("rep")
+        self.core = lax.rem(self.rep, 2)
+        self.line = self.rep // 2
+        reps = lax.axis_size("rep")
+        here = self.here
+        self.near = [here, here + 1 - 2 * lax.rem(here, 2), lax.rem(here + 2, 4), 3 - here]
+        self.plane = [{"fsdp": index} for index in self.near]
+        self.partner = {"rep": self.rep + 1 - 2 * self.core}
+        self.up = {"rep": lax.rem(self.rep + 2, reps)}
+        self.down = {"rep": lax.rem(self.rep + reps - 2, reps)}
+
+    def greet(self, line=True):
+        barrier = pltpu.get_barrier_semaphore()
+        others = self.plane[1:] + ([self.partner, self.up, self.down] if line else [])
+        for other in others:
+            pl.semaphore_signal(barrier, inc=1, device_id=other, device_id_type=MESH)
+        pl.semaphore_wait(barrier, len(others))
+
+
+def remote(src, dst, sems, index, device):
+    return pltpu.make_async_remote_copy(
+        src_ref=src,
+        dst_ref=dst,
+        send_sem=sems.at[0, index],
+        recv_sem=sems.at[1, index],
+        device_id=device,
+        device_id_type=MESH,
+    )
+
+
+class PlaneGather:
+    def __init__(self, links, own, slot, rows, sems):
+        x, y = links.plane[1], links.plane[2]
+        here, near_x, near_y, far = links.near
+        half = rows // 2
+
+        def part(index, lo):
+            return slot(index).at[pl.ds(lo, half)]
+
+        self.first = [
+            remote(own, slot(here), sems, 0, x),
+            remote(own, slot(here), sems, 1, y),
+        ]
+        self.second = [
+            remote(part(near_x, 0), part(near_x, 0), sems, 2, y),
+            remote(part(near_y, half), part(near_y, half), sems, 3, x),
+        ]
+        self.come = [
+            remote(slot(near_x), slot(near_x), sems, 0, x),
+            remote(slot(near_y), slot(near_y), sems, 1, y),
+            remote(part(far, 0), part(far, 0), sems, 2, y),
+            remote(part(far, half), part(far, half), sems, 3, x),
+        ]
+
+    def start(self):
+        for copy in self.first:
+            copy.start()
+
+    def hand_on(self):
+        for i in range(2):
+            self.come[i].wait_recv()
+            self.second[i].start()
+
+    def finish(self):
+        for i in (2, 3):
+            self.come[i].wait_recv()
+
+    def drain(self):
+        for copy in self.first + self.second:
+            copy.wait_send()
+
+
+def prologue_kernel(
+    lengths_ref,
+    starts_ref,
+    x_ref,
+    cot_ref,
+    vec_ref,
+    inverse_ref,
+    wqkv_ref,
+    wo_ref,
+    gu_ref,
+    normed_all,
+    cot_all,
+    wgu,
+    wqkv_full,
+    wo_full,
+    kv_full,
+    mid_ref,
+    normed_first_ref,
+    query_ref,
+    attn_ref,
+    lse_ref,
+    trig_ref,
+    gains_ref,
+    vec_all,
+    wqkv_buf,
+    wo_buf,
+    kv_buf,
+    normed_buf,
+    bias_ref,
+    local_sems,
+    vec_sems,
+    qkv_sems,
+    qkv_core,
+    wo_sems,
+    wo_core,
+    kv_sems,
+    cot_sems,
+    norm_sems,
+    gu_sems,
+    up_sems,
+    down_sems,
+    own_core,
+    up_core,
+    down_core,
+):
+    links = Links()
+    here, core, line = links.here, links.core, links.line
+    count = lax.axis_size("rep") // 2
+    rows, width = x_ref.shape
+    shard = wqkv_ref.shape[0]
+    half = shard // 2
+    links.greet()
+
+    def shard_rows(ref, index):
+        return ref.at[pl.ds(pl.multiple_of(index * shard, shard), shard)]
+
+    own_copies = [
+        pltpu.make_async_copy(wqkv_ref, shard_rows(wqkv_buf, here), local_sems.at[0]),
+        pltpu.make_async_copy(wo_ref, shard_rows(wo_buf, here), local_sems.at[1]),
+        pltpu.make_async_copy(cot_ref, cot_all.at[here], local_sems.at[2]),
+        pltpu.make_async_copy(vec_ref, vec_all.at[here], local_sems.at[3]),
+    ]
+
+    vec_sends = [remote(vec_ref, vec_all.at[here], vec_sems, d - 1, links.plane[d]) for d in (1, 2, 3)]
+    vec_comes = [
+        remote(vec_ref, vec_all.at[links.near[d]], vec_sems, d - 1, links.plane[d]) for d in (1, 2, 3)
+    ]
+
+    def half_rows(ref, index, which):
+        return ref.at[pl.ds(pl.multiple_of(index * shard + which * half, half), half)]
+
+    def weight_gather(src, buf, sems, core_sems):
+        gather = PlaneGather(
+            links,
+            src.at[pl.ds(pl.multiple_of(core * half, half), half)],
+            lambda index: half_rows(buf, index, core),
+            half,
+            sems,
+        )
+        swaps = [
+            remote(
+                half_rows(buf, links.near[d], core),
+                half_rows(buf, links.near[d], core),
+                core_sems,
+                d - 1,
+                links.partner,
+            )
+            for d in (1, 2, 3)
+        ]
+        comes = [
+            remote(
+                half_rows(buf, links.near[d], 1 - core),
+                half_rows(buf, links.near[d], 1 - core),
+                core_sems,
+                d - 1,
+                links.partner,
+            )
+            for d in (1, 2, 3)
+        ]
+        return gather, swaps, comes
+
+    qkv_gather, qkv_swaps, qkv_comes = weight_gather(wqkv_ref, wqkv_buf, qkv_sems, qkv_core)
+    wo_gather, wo_swaps, wo_comes = weight_gather(wo_ref, wo_buf, wo_sems, wo_core)
+    cot_gather = PlaneGather(links, cot_ref, lambda index: cot_all.at[index], rows, cot_sems)
+    norm_gather = PlaneGather(links, normed_buf, lambda index: normed_all.at[index], rows, norm_sems)
+
+    gu_sends = [
+        remote(gu_ref.at[links.near[d]], wgu.at[core, line, d - 1], gu_sems, d - 1, links.plane[d])
+        for d in (1, 2, 3)
+    ]
+    own_block = wgu.at[core, line]
+    own_swap = remote(own_block, own_block, own_core, 0, links.partner)
+    own_come = remote(wgu.at[1 - core, line], wgu.at[1 - core, line], own_core, 0, links.partner)
+
+    class Hop:
+        def __init__(self, k, way):
+            sems = up_sems if way > 0 else down_sems
+            core_sems = up_core if way > 0 else down_core
+            device = links.up if way > 0 else links.down
+            back = links.down if way > 0 else links.up
+            sent = jnp.clip(line - way * (k - 1), 0, count - 1)
+            come = jnp.clip(line - way * k, 0, count - 1)
+            if way > 0:
+                self.sends = (line <= count - 2) & (line >= k - 1)
+                self.comes = line >= k
+            else:
+                self.sends = (line >= 1) & (line + k - 1 <= count - 1)
+                self.comes = line + k <= count - 1
+            self.send = remote(wgu.at[core, sent], wgu.at[core, sent], sems, k - 1, device)
+            self.recv = remote(wgu.at[core, come], wgu.at[core, come], sems, k - 1, back)
+            self.swap = remote(wgu.at[core, come], wgu.at[core, come], core_sems, k - 1, links.partner)
+            self.swap_come = remote(
+                wgu.at[1 - core, come], wgu.at[1 - core, come], core_sems, k - 1, links.partner
+            )
+
+    hops = [(Hop(k, 1), Hop(k, -1)) for k in range(1, count)]
+
+    def start_hop(k):
+        for hop in hops[k - 1]:
+            pl.when(hop.sends)(hop.send.start)
+
+    def take_hop(k):
+        for hop in hops[k - 1]:
+
+            @pl.when(hop.comes)
+            def _():
+                hop.recv.wait_recv()
+                hop.swap.start()
+
+    for copy in vec_sends:
+        copy.start()
+    qkv_gather.start()
+    for copy in gu_sends:
+        copy.start()
+    for copy in own_copies:
+        copy.start()
+    wo_gather.start()
+
+    bias, query_rel = mask_bias(here, rows, kv_buf.shape[0] * rows, lengths_ref, starts_ref)
+    bias_ref[...] = bias
+    angles = query_rel.astype(jnp.float32) * inverse_ref[0:1, :]
+    lanes = lax.broadcasted_iota(jnp.int32, (1, HDIM), 1)
+    cosine = jnp.cos(angles)
+    sine = jnp.sin(angles) * jnp.where(lanes < HDIM // 2, -1.0, 1.0)
+    trig_ref[0] = cosine
+    trig_ref[1] = sine
+
+    x_float = x_ref[...].astype(jnp.float32)
+    unit = x_float * lax.rsqrt(jnp.mean(x_float * x_float, axis=1, keepdims=True) + epsilon)
+    own_copies[3].wait()
+    for copy in vec_comes:
+        copy.wait_recv()
+    gains_ref[...] = vec_all[0] + vec_all[1] + vec_all[2] + vec_all[3]
+    normed_first_ref[...] = (unit * gains_ref[1:2, :]).astype(jnp.bfloat16)
+
+    qkv_gather.hand_on()
+    for swap in qkv_swaps[:2]:
+        swap.start()
+    for copy in gu_sends:
+        copy.wait_recv()
+    start_hop(1)
+    own_swap.start()
+    qkv_gather.finish()
+    qkv_swaps[2].start()
+    cot_gather.start()
+    own_copies[0].wait()
+    for copy in qkv_comes:
+        copy.wait_recv()
+
+    full_copy = pltpu.make_async_copy(wqkv_buf, wqkv_full, local_sems.at[4])
+    full_copy.start()
+
+    def rope(value):
+        return value * trig_ref[0] + pltpu.roll(value, HDIM // 2, 1) * trig_ref[1]
+
+    def project(first, bias_row):
+        columns = pl.ds(pl.multiple_of(first, 2 * HDIM), 2 * HDIM)
+        return dot_f32(normed_first_ref[...], wqkv_buf[:, columns]) + bias_row
+
+    keys = project(width, gains_ref[3:4, 0 : 2 * HDIM])
+    own_kv = kv_buf.at[here]
+    for h in range(2):
+        kv_buf[here, :, h * HDIM : (h + 1) * HDIM] = rope(keys[:, h * HDIM : (h + 1) * HDIM]).astype(
+            jnp.bfloat16
+        )
+    values = project(width + 2 * HDIM, gains_ref[3:4, 2 * HDIM : 4 * HDIM])
+    kv_buf[here, :, 2 * HDIM : 4 * HDIM] = values.astype(jnp.bfloat16)
+    kv_sends = [remote(own_kv, own_kv, kv_sems, d - 1, links.plane[d]) for d in (1, 2, 3)]
+    kv_comes = [
+        remote(kv_buf.at[links.near[d]], kv_buf.at[links.near[d]], kv_sems, d - 1, links.plane[d])
+        for d in (1, 2, 3)
+    ]
+    for copy in kv_sends:
+        copy.start()
+
+    def query_pair(pair, carry):
+        columns = pl.ds(pl.multiple_of(pair * 2 * HDIM, 2 * HDIM), 2 * HDIM)
+        got = project(pair * 2 * HDIM, gains_ref[0:1, columns])
+        for h in range(2):
+            where = pl.ds(pl.multiple_of(pair * 2 * HDIM + h * HDIM, HDIM), HDIM)
+            query_ref[:, where] = rope(got[:, h * HDIM : (h + 1) * HDIM]).astype(jnp.bfloat16)
+        return carry
+
+    lax.fori_loop(0, HEADS // 2, query_pair, 0)
+    wo_gather.hand_on()
+    for swap in wo_swaps[:2]:
+        swap.start()
+    for copy in kv_comes:
+        copy.wait_recv()
+    kv_copy = pltpu.make_async_copy(kv_buf, kv_full, local_sems.at[5])
+    kv_copy.start()
+
+    group = HEADS // KVH
+    row_len = kv_buf.shape[0] * rows
+    head_lane = lax.broadcasted_iota(jnp.int32, (1, HDIM), 1)
+
+    def head_step(h, lse):
+        columns = pl.ds(pl.multiple_of(h * HDIM, HDIM), HDIM)
+        shared = h // group
+        key = kv_buf[:, :, pl.ds(pl.multiple_of(shared * HDIM, HDIM), HDIM)].reshape(row_len, HDIM)
+        value = kv_buf[:, :, pl.ds(pl.multiple_of((KVH + shared) * HDIM, HDIM), HDIM)].reshape(
+            row_len, HDIM
+        )
+        scores = dot_f32(query_ref[:, columns], key, ((1,), (1,))) * (1.0 / HDIM**0.5) + bias_ref[...]
+        peak = jnp.max(scores, axis=1, keepdims=True)
+        expo = jnp.exp(scores - peak)
+        total = jnp.sum(expo, axis=1, keepdims=True)
+        mixed = dot_f32(expo.astype(jnp.bfloat16), value) / total
+        attn_ref[:, columns] = mixed.astype(jnp.bfloat16)
+        return jnp.where(head_lane == h, peak + jnp.log(total), lse)
+
+    lse = lax.fori_loop(0, HEADS // 2, head_step, jnp.zeros((rows, HDIM), jnp.float32))
+    wo_gather.finish()
+    wo_swaps[2].start()
+    take_hop(1)
+    start_hop(2)
+    lse_ref[...] = lax.fori_loop(HEADS // 2, HEADS, head_step, lse)
+    cot_gather.hand_on()
+    take_hop(2)
+    start_hop(3)
+    own_copies[1].wait()
+    for copy in wo_comes:
+        copy.wait_recv()
+    wo_copy = pltpu.make_async_copy(wo_buf, wo_full, local_sems.at[6])
+    wo_copy.start()
+
+    def out_columns(i, carry):
+        columns = pl.ds(pl.multiple_of(i * 256, 256), 256)
+        mid_ref[:, columns] = x_ref[:, columns].astype(jnp.float32) + dot_f32(
+            attn_ref[...], wo_buf[:, columns]
+        )
+        return carry
+
+    lax.fori_loop(0, width // 256, out_columns, 0)
+    mid = mid_ref[...]
+    unit = mid * lax.rsqrt(jnp.mean(mid * mid, axis=1, keepdims=True) + epsilon)
+    normed_buf[...] = (unit * gains_ref[2:3, :]).astype(jnp.bfloat16)
+    norm_gather.start()
+    norm_copy = pltpu.make_async_copy(normed_buf, normed_all.at[here], local_sems.at[7])
+    norm_copy.start()
+    norm_gather.hand_on()
+    cot_gather.finish()
+    take_hop(3)
+    norm_gather.finish()
+
+    own_copies[2].wait()
+    full_copy.wait()
+    kv_copy.wait()
+    wo_copy.wait()
+    norm_copy.wait()
+    for copy in vec_sends + gu_sends + qkv_swaps + wo_swaps + kv_sends + [own_swap]:
+        copy.wait_send()
+    own_come.wait_recv()
+    for copy in wo_comes[:0]:
+        copy.wait_recv()
+    for gather in (qkv_gather, wo_gather, cot_gather, norm_gather):
+        gather.drain()
+    for pair in hops:
+        for hop in pair:
+            pl.when(hop.sends)(hop.send.wait_send)
+
+            @pl.when(hop.comes)
+            def _():
+                hop.swap.wait_send()
+                hop.swap_come.wait_recv()
+
+
+def prologue(lengths, starts, x, cot, vec, inverse, wqkv, wo, pieces):
+    rows, width = x.shape
+    shards = lax.axis_size("fsdp")
+    count = lax.axis_size("rep") // 2
+    thin, part = pieces.shape[2:]
+    bf16, f32 = jnp.bfloat16, jnp.float32
+    any_space = pl.BlockSpec(memory_space=pl.ANY)
+    vmem = pl.BlockSpec(memory_space=pltpu.VMEM)
+    smem = pl.BlockSpec(memory_space=pltpu.SMEM)
+    shape = jax.ShapeDtypeStruct
+
+    def sems(n):
+        return pltpu.SemaphoreType.DMA((2, n))
+
+    return pl.pallas_call(
+        prologue_kernel,
+        name="prologue",
+        out_shape=(
+            shape((shards, rows, width), bf16),
+            shape((shards, rows, width), bf16),
+            shape((2, count, shards - 1, 2, thin, part), bf16),
+            shape((width, wqkv.shape[1]), bf16),
+            shape((width, width), bf16),
+            shape((shards, rows, 4 * HDIM), bf16),
+            shape((rows, width), f32),
+            shape((rows, width), bf16),
+            shape((rows, width), bf16),
+            shape((rows, width), bf16),
+            shape((rows, HDIM), f32),
+            shape((2, rows, HDIM), f32),
+            shape((8, width), f32),
+        ),
+        in_specs=[smem, smem, vmem, vmem, vmem, vmem, any_space, any_space, any_space],
+        out_specs=[any_space] * 6 + [vmem] * 7,
+        scratch_shapes=[
+            pltpu.VMEM((shards, 8, width), f32),
+            pltpu.VMEM((width, wqkv.shape[1]), bf16),
+            pltpu.VMEM((width, width), bf16),
+            pltpu.VMEM((shards, rows, 4 * HDIM), bf16),
+            pltpu.VMEM((rows, width), bf16),
+            pltpu.VMEM((rows, shards * rows), f32),
+            pltpu.SemaphoreType.DMA((8,)),
+            sems(3),
+            sems(4),
+            sems(3),
+            sems(4),
+            sems(3),
+            sems(3),
+            sems(4),
+            sems(4),
+            sems(3),
+            sems(count - 1),
+            sems(count - 1),
+            sems(1),
+            sems(count - 1),
+            sems(count - 1),
+        ],
+        compiler_params=pltpu.CompilerParams(
+            collective_id=0, has_side_effects=True, vmem_limit_bytes=60 * 2**20
+        ),
+    )(lengths, starts, x, cot, vec, inverse, wqkv, wo, pieces)
 
 
 def local(
@@ -460,7 +943,302 @@
     )
 
 
+def local_fast(
+    hidden_in,
+    out_grad,
+    doc_lengths,
+    piece_starts,
+    w_query,
+    b_query,
+    w_key,
+    b_key,
+    w_value,
+    b_value,
+    w_output,
+    gain_attn,
+    w_gate,
+    w_up,
+    w_down,
+    gain_mlp,
+):
+    tok_rows = hidden_in.shape[0]
+    model_width = hidden_in.shape[1]
+    shard_count = lax.axis_size("fsdp")
+    row_len = tok_rows * shard_count
+    group_size = HEADS // KVH
+    kv_width = KVH * HDIM
+    ff_width = w_gate.shape[1]
+    score_scale = 1.0 / HDIM**0.5
+    row_pos = jnp.arange(row_len, dtype=jnp.int32)
+    lengths = doc_lengths[0]
+    starts = piece_starts[0]
+    here = lax.axis_index("fsdp")
+    core = lax.axis_index("rep") % 2
+    line = lax.axis_size("rep") // 2
+    line_pos = lax.axis_index("rep") // 2
+    low = jnp.bfloat16
+    part = ff_width // shard_count
+    shard_rows = model_width // shard_count
+    thin = shard_rows // 2 // line
+    halves = jnp.arange(0, HDIM, 2).astype(jnp.float32) / HDIM
+    inverse = rope_base ** (-halves)
+    inverse = jnp.broadcast_to(jnp.concatenate([inverse, inverse])[None], (8, HDIM))
+
+    def spread(vector, first, size):
+        zeros = jnp.zeros((1, size), jnp.float32)
+        return lax.dynamic_update_slice(
+            zeros, vector.astype(jnp.float32)[None], (0, first + here * vector.shape[0])
+        )
+
+    kv_bias = spread(b_key, 0, model_width) + spread(b_value, kv_width, model_width)
+    vec = jnp.concatenate(
+        [
+            spread(b_query, 0, model_width),
+            spread(gain_attn, 0, model_width),
+            spread(gain_mlp, 0, model_width),
+            kv_bias,
+            jnp.zeros((4, model_width), jnp.float32),
+        ]
+    )
+    first_row = core * (shard_rows // 2) + line_pos * thin
+
+    def cut(weight):
+        piece = lax.dynamic_slice_in_dim(weight, first_row, thin, 0)
+        return jnp.stack([piece[:, t * part : (t + 1) * part] for t in range(shard_count)])
+
+    pieces = jnp.stack([cut(w_gate), cut(w_up)], axis=1)
+    (
+        normed_all,
+        cot_all,
+        wgu,
+        wqkv_full,
+        output_full,
+        kv_full,
+        mid_state,
+        normed_first,
+        query_rot,
+        attn_low,
+        lse,
+        trig,
+        gains,
+    ) = prologue(
+        doc_lengths,
+        piece_starts,
+        hidden_in,
+        out_grad,
+        vec,
+        inverse,
+        jnp.concatenate([w_query, w_key, w_value], axis=1),
+        w_output,
+        pieces,
+    )
+    query_full = wqkv_full[:, :model_width]
+    key_full = wqkv_full[:, model_width : model_width + kv_width]
+    value_full = wqkv_full[:, model_width + kv_width :]
+    cosine = trig[0]
+    sine = trig[1] * jnp.where(jnp.arange(HDIM) < HDIM // 2, -1.0, 1.0)
+    local_pos = here * tok_rows + jnp.arange(tok_rows, dtype=jnp.int32)
+    query_doc, query_rel, query_piece = row_layout(local_pos, lengths, starts, PIECE)
+    key_doc, unused_rel, key_piece = row_layout(row_pos, lengths, starts, PIECE)
+    allowed = visible_pairs(query_doc, local_pos, query_piece, key_doc, row_pos, key_piece)
+    x_float = hidden_in.astype(jnp.float32)
+    inv_first = lax.rsqrt(jnp.mean(x_float * x_float, axis=1, keepdims=True) + epsilon)
+    unit_first = x_float * inv_first
+    gain_first = gains[1]
+    gain_second = gains[2]
+    inv_second = lax.rsqrt(jnp.mean(mid_state * mid_state, axis=1, keepdims=True) + epsilon)
+    unit_second = mid_state * inv_second
+    kv_rows = kv_full.reshape(row_len, 2 * kv_width)
+    query_grouped = query_rot.reshape(tok_rows, KVH, group_size, HDIM)
+    keys_grouped = kv_rows[:, :kv_width].reshape(row_len, KVH, HDIM)
+    values_grouped = kv_rows[:, kv_width:].reshape(row_len, KVH, HDIM)
+    log_total = lse[:, :HEADS].T.reshape(KVH, group_size, tok_rows, 1)
+
+    def masked_scores():
+        raw_scores = (
+            jnp.einsum(
+                "tgjd,rgd->gjtr", query_grouped, keys_grouped, preferred_element_type=jnp.float32
+            )
+            * score_scale
+        )
+        return jnp.where(allowed[None, None], raw_scores, -1e30)
+
+    def whole(which, weight):
+        mine = lax.dynamic_slice_in_dim(weight, here * part, part, 1)
+        other = wgu[:, :, :, which].transpose(2, 0, 1, 3, 4).reshape(
+            shard_count - 1, shard_rows, part
+        )
+        rows = place([mine] + [other[d] for d in range(shard_count - 1)], here)
+        return rows.reshape(model_width, part)
+
+    gate_part = whole(0, w_gate)
+    up_part = whole(1, w_up)
+    cot_float = out_grad.astype(jnp.float32)
+    cot_all = cot_all.reshape(row_len, model_width)
+    normed_all = normed_all.reshape(row_len, model_width)
+    gate_val = mat_dot(normed_all, gate_part)
+    up_val = mat_dot(normed_all, up_part)
+    sig_gate = jax.nn.sigmoid(gate_val)
+    silu_gate = gate_val * sig_gate
+    act_low = (silu_gate * up_val).astype(low)
+    d_act = dot_right_t(cot_all, w_down)
+    d_gate = (d_act * up_val * sig_gate * (1.0 + gate_val * (1.0 - sig_gate))).astype(low)
+    d_up = (d_act * silu_gate).astype(low)
+    mlp_part = mat_dot(act_low, w_down).reshape(shard_count, tok_rows, model_width)
+    mlp_out = scatter_relative([pick(mlp_part, here ^ d) for d in range(shard_count)], "fsdp")
+    norm_part = (dot_right_t(d_gate, gate_part) + dot_right_t(d_up, up_part)).reshape(
+        shard_count, tok_rows, model_width
+    )
+    partial_value = scatter_relative([pick(norm_part, here ^ d) for d in range(shard_count)], "fsdp")
+
+    def keep_half(grad):
+        mine = lax.dynamic_index_in_dim(grad, core, 1, keepdims=False)
+        other = lax.dynamic_index_in_dim(grad, 1 - core, 1, keepdims=False)
+        return (mine.astype(jnp.float32) + core_swap(other).astype(jnp.float32)).astype(low)
+
+    def both_cores(half):
+        return core_halves(half, core_swap(half), core)
+
+    down_grad = dot_left_t(act_low, cot_all).astype(low)
+    half = part // 2
+    down_half = keep_half(down_grad.reshape(1, 2, half, model_width))[0]
+    wide = model_width // line
+    down_parts = jnp.stack([down_half[:, q * wide : (q + 1) * wide] for q in range(line)])
+    down_own = line_scatter(down_parts).astype(low)
+    down_rows = line_gather(down_own)
+    down_rows = jnp.concatenate([down_rows[q] for q in range(line)], axis=1)
+    down_sums = both_cores(down_rows).reshape(part, model_width).astype(jnp.float32)
+
+    rows = model_width // shard_count
+    thin = rows // 2 // line
+
+    def column_grad(d_value):
+        grad = dot_left_t(normed_all, d_value).astype(low)
+        kept = keep_half(grad.reshape(shard_count, 2, rows // 2, part))
+        kept = kept.reshape(shard_count, line, thin, part).transpose(1, 0, 2, 3)
+        own = line_scatter(kept).astype(low)
+        got = []
+        for d in range(shard_count):
+            piece = pick(own, here ^ d)
+            got.append(piece if d == 0 else lax.ppermute(piece, "fsdp", xor_pairs(shard_count, d)))
+        got = place(got, here).transpose(1, 0, 2).reshape(thin, ff_width)
+        full = line_gather(got).reshape(rows // 2, ff_width)
+        return both_cores(full).reshape(rows, ff_width).astype(jnp.float32)
+
+    grad_gate = column_grad(d_gate)
+    grad_up = column_grad(d_up)
+    output = mid_state + mlp_out
+    d_gain_second = jnp.sum(partial_value * unit_second, axis=0)
+    scaled_second = partial_value * gain_second
+    d_mid = cot_float + inv_second * (
+        scaled_second - unit_second * jnp.mean(scaled_second * unit_second, axis=1, keepdims=True)
+    )
+    d_branch_low = d_mid.astype(jnp.bfloat16)
+    d_attn_low = dot_right_t(d_branch_low, output_full).astype(jnp.bfloat16)
+    d_attn_grouped = d_attn_low.reshape(tok_rows, KVH, group_size, HDIM)
+    scores = masked_scores()
+    soft_back = jnp.exp(scores - log_total)
+    probs_low = soft_back.astype(jnp.bfloat16)
+    prob_grad = jnp.einsum(
+        "tgjd,rgd->gjtr", d_attn_grouped, values_grouped, preferred_element_type=jnp.float32
+    )
+    row_delta = jnp.sum(soft_back * prob_grad, axis=3, keepdims=True)
+    score_grad = (soft_back * (prob_grad - row_delta)).astype(jnp.bfloat16)
+    dquery_rot = (
+        jnp.einsum("gjtr,rgd->tgjd", score_grad, keys_grouped, preferred_element_type=jnp.float32)
+        * score_scale
+    )
+    dquery_low = (
+        unrotate(dquery_rot.reshape(tok_rows, HEADS, HDIM), cosine, sine)
+        .reshape(tok_rows, model_width)
+        .astype(jnp.bfloat16)
+    )
+    key_grad = (
+        jnp.einsum("gjtr,tgjd->rgd", score_grad, query_grouped, preferred_element_type=jnp.float32)
+        * score_scale
+    )
+    value_grad = jnp.einsum(
+        "gjtr,tgjd->rgd", probs_low, d_attn_grouped, preferred_element_type=jnp.float32
+    )
+    kv_sums = lax.psum_scatter(
+        jnp.concatenate(
+            [
+                key_grad.reshape(lax.axis_size("fsdp") * tok_rows, kv_width),
+                value_grad.reshape(lax.axis_size("fsdp") * tok_rows, kv_width),
+            ],
+            axis=1,
+        ).astype(jnp.bfloat16),
+        "fsdp",
+        scatter_dimension=0,
+        tiled=True,
+    ).astype(jnp.float32)
+    dkey_low = (
+        unrotate(kv_sums[:, :kv_width].reshape(tok_rows, KVH, HDIM), cosine, sine)
+        .reshape(tok_rows, kv_width)
+        .astype(jnp.bfloat16)
+    )
+    dvalue_low = kv_sums[:, kv_width:].astype(jnp.bfloat16)
+    d_norm_first = (
+        dot_right_t(dquery_low, query_full)
+        + dot_right_t(dkey_low, key_full)
+        + dot_right_t(dvalue_low, value_full)
+    )
+    attn_grads = jnp.concatenate(
+        [
+            dot_left_t(normed_first, dquery_low).astype(low),
+            dot_left_t(normed_first, dkey_low).astype(low),
+            dot_left_t(normed_first, dvalue_low).astype(low),
+            dot_left_t(attn_low, d_branch_low).astype(low),
+        ],
+        axis=1,
+    )
+    attn_wide = attn_grads.shape[1]
+    attn_kept = keep_half(attn_grads.reshape(shard_count, 2, rows // 2, attn_wide))
+    attn_own = scatter_relative([pick(attn_kept, here ^ d) for d in range(shard_count)], "fsdp").astype(low)
+    attn_own = line_scatter(attn_own.reshape(line, thin, attn_wide)).astype(low)
+    attn_rows = line_gather(attn_own).reshape(rows // 2, attn_wide)
+    attn_sums = both_cores(attn_rows).reshape(rows, attn_wide).astype(jnp.float32)
+    d_gain_first = jnp.sum(d_norm_first * unit_first, axis=0)
+    scaled_first = d_norm_first * gain_first
+    grad_input = d_mid + inv_first * (
+        scaled_first - unit_first * jnp.mean(scaled_first * unit_first, axis=1, keepdims=True)
+    )
+    bias_query = jnp.sum(dquery_low.astype(jnp.float32), axis=0)
+    bias_key = jnp.sum(dkey_low.astype(jnp.float32), axis=0)
+    bias_value = jnp.sum(dvalue_low.astype(jnp.float32), axis=0)
+    small = (bias_query, bias_key, bias_value, d_gain_first, d_gain_second)
+    summed = lax.psum(jnp.concatenate(small), ("rep", "fsdp"))
+    outs = []
+    at = 0
+    for vector in small:
+        size = vector.shape[0] // shard_count
+        outs.append(lax.dynamic_slice_in_dim(summed, at + here * size, size, 0))
+        at += vector.shape[0]
+    bias_query, bias_key, bias_value, gain_first_sum, gain_second_sum = outs
+    grad_query = attn_sums[:, :model_width]
+    grad_key = attn_sums[:, model_width : model_width + kv_width]
+    grad_value = attn_sums[:, model_width + kv_width : model_width + 2 * kv_width]
+    grad_output = attn_sums[:, model_width + 2 * kv_width :]
+    return (
+        output,
+        grad_input,
+        grad_query,
+        bias_query,
+        grad_key,
+        bias_key,
+        grad_value,
+        bias_value,
+        grad_output,
+        gain_first_sum,
+        grad_gate,
+        grad_up,
+        down_sums,
+        gain_second_sum,
+    )
+
+
 def solution(mesh):
+    body = local_fast if mesh.shape["fsdp"] == 4 and mesh.shape["rep"] == 8 else local
     placed = (
         P(("rep", "fsdp"), None),
         P(("rep", "fsdp"), None),
@@ -480,7 +1258,7 @@
         P("fsdp"),
     )
     return jax.shard_map(
-        local,
+        body,
         mesh=mesh,
         in_specs=placed,
         out_specs=(

time: 1300 us -> 1240 us (0.954)
  Pallas kernels: 0 us -> 185 us
  waiting for transfers between devices: 398 us -> 281 us
  blocking collectives: 80.6 us -> 37.4 us
  starting transfers between devices: 223 us -> 185 us
  local copies, waits for them, and re-layouts: 197 us -> 172 us
  other arithmetic: 158 us -> 135 us
    pallas_call x0 -> x1, Pallas kernels: none -> 185 us  [prologue(): pl.pallas_call(prologue_kernel, name='prologue', out_shape=(shape((shards...]
    ppermute x30 -> x0, waiting for transfers between devices: 103 us -> none  [the longest x24 70 us: gather_relative(): lax.ppermute(piece, axis, xor_pairs(count, bit))]
    ppermute x30 -> x0, starting transfers between devices: 44.1 us -> none  [the longest x24 32.2 us: gather_relative(): lax.ppermute(piece, axis, xor_pairs(count, bit))]
    all_gather x3 -> x0, blocking collectives: 42.7 us -> none  [the longest x1 19.1 us: local(): lax.all_gather(jnp.concatenate([b_query, b_key, b_value, gain_attn, gain_...]
    dot_general x1, matrix products: 3.8 us -> 17.9 us  [masked_scores(): jnp.einsum('tgjd,rgd->gjtr', query_grouped, keys_grouped, preferred_eleme...]
    unnamed x263 -> x200, local copies, waits for them, and re-layouts: 57.8 us -> 45.7 us
    dot_general x5 -> x4, matrix products: 42.2 us -> 31.8 us  [the longest x1 9.32 us: local_fast(): jnp.einsum('tgjd,rgd->gjtr', d_attn_grouped, values_grouped, preferred_el...]
    dot_general x7 -> x3, matrix products: 51.8 us -> 47.6 us  [mat_dot(): return jnp.dot(left, right, preferred_element_type=jnp.float32)]
  transfers between devices with their start and end apart: 115 -> 81, of which waited for: 37 -> 26; matrix products, arithmetic and copies ran while one was open for 31% -> 30% of each run, Pallas kernels for 0% -> 0%
where the time goes in v2:
time: 1240 us; the launch traced here: 1220 us
  waiting for transfers between devices  281 us (23%)
  matrix products  210 us (17%)
  starting transfers between devices  185 us (15%)
  Pallas kernels  185 us (15%)
  local copies, waits for them, and re-layouts  172 us (14%)
  other arithmetic  135 us (11%)
  blocking collectives  37.4 us (3%)
  between operations  16.7 us (1%)
    pallas_call x1, Pallas kernels, prologue(): pl.pallas_call(prologue_kernel, name='prologue', out_shape=(shape((shards...  185 us
    ppermute x12, waiting for transfers between devices, line_gather(): lax.ppermute(above[-1], 'rep', line_pairs(range(1, count - step + 1), -1))  118 us
    ppermute x18, waiting for transfers between devices, scatter_relative(): lax.ppermute(have[d].astype(jnp.bfloat16), axis, xor_pairs(count, bit))  77.5 us
    ppermute x12, starting transfers between devices, line_scatter(): lax.ppermute(sends[0], 'rep', line_pairs(range(step), 1))  70.5 us
    ppermute x12, waiting for transfers between devices, line_scatter(): lax.ppermute(sends[0], 'rep', line_pairs(range(step), 1))  64.6 us
    dot_general x7, matrix products, dot_right_t(): lax.dot_general(left, right, (((1,), (1,)), ((), ())), preferred_element_...  64.4 us
    ppermute x12, starting transfers between devices, line_gather(): lax.ppermute(below[-1], 'rep', line_pairs(range(step - 1, count - 1), 1))  56.2 us
    dot_general x7, matrix products, dot_left_t(): lax.dot_general(left, right, (((0,), (0,)), ((), ())), preferred_element_...  48.2 us
  transfers between devices with their start and end apart: 81, of which 26 were waited for; matrix products, arithmetic and copies ran while one was open for 30% of the time, Pallas kernels for 0%

profile of v2, /device:TPU:0, one launch (start us, length us, event | category | flops | bytes accessed | tf_op | source)
XLA Modules:
  0.0 1221.7 jit_solution(4448975555786047494)
XLA Ops:
  17.4 184.8 %prologue.1 = (bf16[4,320,1536]{2,1,0:T(8,128)(2,1)}, bf16[4,320,1536]{2,1,0:T(8,128)(2,1)}, bf16[2,4,3,2,48,2240]{5,4,3,2,1,0:T(8,128)(2,1)}, bf16[1536,2048]{1...) custom-call(s32[1,8]{1,0:T(1,128)} %lengths_ref.1, ...), custom_call_target="tpu_custom_call" | custom-call | tf_op jit(solution)/shard_map/prologue/pallas_call | solution.py:605
  202.2 9.1 slice_bitcast_fusion.1
  211.3 5.0 fusion.100
  235.2 17.0 %fusion.108 = f32[1280,2240]{0,1:T(8,128)} fusion(bf16[1280,1536]{1,0:T(8,128)(2,1)} %bitcast.599, bf16[1536,2240]{1,0:T(8,128)(2,1)S(1)} %bitcast.544), kind=kOutput, calls=%fused_computation.345 | convolution fusion | flops 8808038400 | bytes 22282240 | tf_op jit(solution)/shard_map/dot_general | solution.py:60
  253.1 17.0 %fusion.109 = f32[1280,2240]{0,1:T(8,128)} fusion(bf16[1280,1536]{1,0:T(8,128)(2,1)} %bitcast.600, bf16[1536,2240]{1,0:T(8,128)(2,1)S(1)} %bitcast.546), kind=kOutput, calls=%fused_computation.346 | convolution fusion | flops 8808038400 | bytes 22282240 | tf_op jit(solution)/shard_map/dot_general | solution.py:60
  270.2 24.6 %multiply_convert_fusion = (bf16[1280,2240]{0,1:T(8,128)(2,1)}, bf16[1280,2240]{0,1:T(8,128)(2,1)}, bf16[1280,2240]{0,1:T(8,128)(2,1)}) fusion(f32[1280,2240]{0,1:T(8,128)} %fusion.108, f32[1280,2240]{0,1:T(8,128)} %fusion.109, bf16[1280,1536]{1,0:T(8,128)(2,1)} %bitcast.597, bf16[2240,1536]{1,0:T(8,128)(2,1)} %param.30), kind=kOutput, calls=%fused_computation.8 | convolution fusion | flops 8851046400 | bytes 50954240 | tf_op jit(solution)/shard_map/dot_general | solution.py:64
  294.7 15.5 %fusion.111 = f32[1280,1536]{1,0:T(8,128)} fusion(bf16[1280,2240]{0,1:T(8,128)(2,1)} %get-tuple-element.49, bf16[1536,2240]{1,0:T(8,128)(2,1)} %bitcast.545), kind=kOutput, calls=%fused_computation.348 | convolution fusion | flops 8808038400 | bytes 20480000 | tf_op jit(solution)/shard_map/dot_general | solution.py:64
  310.2 13.4 %convolution_add_fusion = f32[1280,1536]{1,0:T(8,128)} fusion(f32[1280,1536]{1,0:T(8,128)} %fusion.111, bf16[1280,2240]{0,1:T(8,128)(2,1)S(1)} %copy-done.61, bf16[1536,2240]{1,0:T(8,128)(2,1)S(1)} %bitcast.547), kind=kOutput, calls=%fused_computation.21 | convolution fusion | flops 8810004480 | bytes 28344320 | tf_op jit(solution)/shard_map/dot_general | solution.py:64
  332.9 13.6 %fusion.110 = f32[1280,1536]{1,0:T(8,128)S(1)} fusion(bf16[1280,2240]{0,1:T(8,128)(2,1)} %get-tuple-element.50, bf16[2240,1536]{1,0:T(8,128)(2,1)} %param.30), kind=kOutput, calls=%fused_computation.347 | convolution fusion | flops 8808038400 | bytes 20480000 | tf_op jit(solution)/shard_map/dot_general | solution.py:60
  350.9 14.8 %convolution_convert_fusion.1 = bf16[1536,2240]{0,1:T(8,128)(2,1)} fusion(bf16[1280,2240]{0,1:T(8,128)(2,1)} %get-tuple-element.49, bf16[1280,1536]{1,0:T(8,128)(2,1)} %bitcast.601), kind=kOutput, calls=%fused_computation.14 | convolution fusion | flops 8811479040 | bytes 16547840 | tf_op jit(solution)/shard_map/dot_general | solution.py:70
  365.8 11.3 convolution_convert_fusion
  377.2 11.5 convolution_convert_fusion.2
  393.1 10.2 copy.146
  403.3 9.6 copy.153
  447.4 7.2 collective-permute-done.4
  454.6 15.4 %collective-permute-done.2 = bf16[160,1536]{1,0:T(8,128)(2,1)S(1)} collective-permute-done((bf16[160,1536]{1,0:T(8,128)(2,1)S(1)}, bf16[160,1536]{1,0:T(8,128)(2,1)S(1)}, u32[]{:S(2)}, u32[]{:S(2)}) %collective-permute-start.2) | collective-permute-done | bytes 491552 | tf_op jit(solution)/shard_map/ppermute | solution.py:109
  473.4 7.8 collective-permute-done.11
  499.2 9.3 fusion.112
  508.5 17.9 %fusion = (f32[2,6,320]{2,1,0:T(8,128)S(1)}, f32[2,6,320,1280]{3,2,1,0:T(8,128)}) fusion(f32[2,1280,320,6]{1,2,3,0:T(8,128)} %fusion.112, f32[2,6,320]{2,1,0:T(8,128)S(1)} %sub.66, bf16[1280,2,128,1]{0,2,3,1:T(8,128)(2,1)S(1)} %bitcast.558, bf16[320,2,6,128]{0,3,2,1:T(8,128)(2,1)S(1)} %bitcast.562, pred[320,1280]{1,0:T(8,128)(4,1)S(1)} %fusion.53), kind=kOutput, calls=%fused_computation.2 | convolution fusion | flops 1282863360 | bytes 41400320 | tf_op jit(solution)/shard_map/tgjd,rgd->gjtr/dot_general | solution.py:1059
  526.4 9.3 fusion.20
  538.8 12.9 %fusion.2 = bf16[2,6,320,1280]{3,2,1,0:T(8,128)(2,1)} fusion(f32[2,6,320,1280]{3,2,1,0:T(8,128)} %get-tuple-element.157, f32[2,1280,320,6]{1,2,3,0:T(8,128)S(1)} %copy-done, f32[2,6,320]{2,1,0:T(8,128)S(1)} %get-tuple-element.156), kind=kLoop, calls=%fused_computation.4 | loop fusion | flops 14745600 | bytes 49167360 | tf_op jit(solution)/shard_map/convert_element_type | solution.py:1146
  551.7 7.8 bitcast_multiply_fusion.3
  563.3 5.4 fusion.19
  600.0 5.6 collective-permute-start.33
  650.3 7.3 pad_maximum_fusion
  658.9 14.6 %copy.143 = bf16[1536,3584]{1,0:T(8,128)(2,1)} copy(bf16[1536,3584]{0,1:T(8,128)(2,1)} %pad_maximum_fusion) | data formatting | bytes 22020096 | tf_op jit(solution)/shard_map/concatenate | solution.py:1186
  673.5 37.4 %psum.7 = f32[5120]{0:T(1024)} all-reduce(f32[5120]{0:T(1024)} %constant_dynamic-update-slice_fusion.6), channel_id=1, replica_groups=mesh['rep'=8,'fsdp'=4] {'rep','fsdp'}, use_global_device_ids=true, to_apply=%region_16.17 | all-reduce | flops 5120 | bytes 40960 | tf_op jit(solution)/shard_map/psum | solution.py:1210
  710.9 5.9 dynamic-slice_bitcast_fusion
  721.7 4.8 collective-permute-start.34
  732.6 14.0 %collective-permute-done.34 = bf16[4,48,2240]{2,1,0:T(8,128)(2,1)S(1)} collective-permute-done((bf16[4,48,2240]{2,1,0:T(8,128)(2,1)S(1)}, bf16[4,48,2240]{2,1,0:T(8,128)(2,1)S(1)}, u32[]{:S(2)}, u32[]{:S(2)}) %collective-permute-start.34) | collective-permute-done | bytes 860192 | tf_op jit(solution)/shard_map/ppermute | solution.py:145
  746.6 4.4 collective-permute-start.51
  753.4 11.6 collective-permute-done.68
  765.0 4.4 collective-permute-start.35
  770.7 13.3 %collective-permute-done.51 = bf16[4,48,2240]{2,1,0:T(8,128)(2,1)S(1)} collective-permute-done((bf16[4,48,2240]{2,1,0:T(8,128)(2,1)S(1)}, bf16[4,48,2240]{2,1,0:T(8,128)(2,1)S(1)}, u32[]{:S(2)}, u32[]{:S(2)}) %collective-permute-start.51) | collective-permute-done | bytes 860192 | tf_op jit(solution)/shard_map/ppermute | solution.py:145
  786.3 5.2 collective-permute-start.52
  793.3 22.7 %collective-permute-start.69 = (bf16[1120,384]{1,0:T(8,128)(2,1)S(1)}, bf16[1120,384]{1,0:T(8,128)(2,1)S(1)}, u32[]{:S(2)}, u32[]{:S(2)}) collective-permute-start(bf16[1120,384]{1,0:T(8,128)(2,1)S(1)} %get-tuple-element.107), channel_id=1, source_target_pairs={{0,8},{4,12},{8,16},{12,20},{16,24},{20,28},{1,9},{5,13},{9,17},{1... | collective-permute-start | bytes 2580488 | tf_op jit(solution)/shard_map/ppermute | solution.py:145
  819.3 19.4 %collective-permute-done.69 = bf16[1120,384]{1,0:T(8,128)(2,1)S(1)} collective-permute-done((bf16[1120,384]{1,0:T(8,128)(2,1)S(1)}, bf16[1120,384]{1,0:T(8,128)(2,1)S(1)}, u32[]{:S(2)}, u32[]{:S(2)}) %collective-permute-start.69) | collective-permute-done | bytes 860192 | tf_op jit(solution)/shard_map/ppermute | solution.py:145
  840.9 11.3 collective-permute-done.72
  855.6 18.0 %collective-permute-start.73 = (bf16[1120,384]{1,0:T(8,128)(2,1)S(1)}, bf16[1120,384]{1,0:T(8,128)(2,1)}, u32[]{:S(2)}, u32[]{:S(2)}) collective-permute-start(bf16[1120,384]{1,0:T(8,128)(2,1)S(1)} %fusion.51), channel_id=1, source_target_pairs={{0,8},{4,12},{8,16},{12,20},{16,24},{20,28},{1,9},{5,13},{9,17},{1... | collective-permute-start | bytes 2580488 | tf_op jit(solution)/shard_map/ppermute | solution.py:157
  878.4 9.7 collective-permute-done.73
  894.1 7.6 collective-permute-start.42
  907.8 11.6 collective-permute-start.59
  924.7 7.9 collective-permute-done.45
  936.9 34.7 %collective-permute-done.62 = bf16[48,8960]{1,0:T(8,128)(2,1)S(1)} collective-permute-done((bf16[48,8960]{1,0:T(8,128)(2,1)}, bf16[48,8960]{1,0:T(8,128)(2,1)S(1)}, u32[]{:S(2)}, u32[]{:S(2)}) %collective-permute-start.62) | collective-permute-done | bytes 860192 | tf_op jit(solution)/shard_map/ppermute | solution.py:158
  973.2 16.9 %collective-permute-done.77 = bf16[1120,384]{1,0:T(8,128)(2,1)S(1)} collective-permute-done((bf16[1120,384]{1,0:T(8,128)(2,1)}, bf16[1120,384]{1,0:T(8,128)(2,1)S(1)}, u32[]{:S(2)}, u32[]{:S(2)}) %collective-permute-start.77) | collective-permute-done | bytes 860192 | tf_op jit(solution)/shard_map/ppermute | solution.py:158
  994.1 14.4 %collective-permute-done.46 = bf16[48,8960]{1,0:T(8,128)(2,1)} collective-permute-done((bf16[48,8960]{1,0:T(8,128)(2,1)}, bf16[48,8960]{1,0:T(8,128)(2,1)}, u32[]{:S(2)}, u32[]{:S(2)}) %collective-permute-start.46) | collective-permute-done | bytes 860192 | tf_op jit(solution)/shard_map/ppermute | solution.py:158
  1011.4 15.6 %collective-permute-done.63 = bf16[48,8960]{1,0:T(8,128)(2,1)} collective-permute-done((bf16[48,8960]{1,0:T(8,128)(2,1)S(1)}, bf16[48,8960]{1,0:T(8,128)(2,1)}, u32[]{:S(2)}, u32[]{:S(2)}) %collective-permute-start.63) | collective-permute-done | bytes 860192 | tf_op jit(solution)/shard_map/ppermute | solution.py:158
  1028.6 16.7 %collective-permute-done.78 = bf16[1120,384]{1,0:T(8,128)(2,1)S(1)} collective-permute-done((bf16[1120,384]{1,0:T(8,128)(2,1)S(1)}, bf16[1120,384]{1,0:T(8,128)(2,1)S(1)}, u32[]{:S(2)}, u32[]{:S(2)}) %collective-permute-start.78) | collective-permute-done | bytes 860192 | tf_op jit(solution)/shard_map/ppermute | solution.py:158
  1052.6 6.4 fusion.6
  1074.3 5.1 collective-permute-done.14
  1080.3 12.0 collective-permute-done.13
  1092.9 12.5 %collective-permute-done.15 = bf16[96,3584]{1,0:T(8,128)(2,1)S(1)} collective-permute-done((bf16[96,3584]{1,0:T(8,128)(2,1)S(1)}, bf16[96,3584]{1,0:T(8,128)(2,1)S(1)}, u32[]{:S(2)}, u32[]{:S(2)}) %collective-permute-start.15) | collective-permute-done | bytes 688160 | tf_op jit(solution)/shard_map/ppermute | solution.py:109
  1106.5 11.2 collective-permute-done.16
  1119.0 5.4 collective-permute-start.19
  1129.2 4.4 collective-permute-start.20
  1139.7 5.9 collective-permute-start.21
  1151.2 7.6 bitcast_convert_fusion
  1160.1 8.2 collective-permute-start.25
  1169.5 4.6 maximum_select_fusion
  1174.8 6.5 bitcast_convert_fusion.2
  1183.3 4.7 maximum_select_fusion.1
  1188.0 5.7 collective-permute-done.29
  1196.5 6.4 collective-permute-done.30
  1203.1 6.5 bitcast_convert_fusion.1
  (503 shorter events, 306.5 us)
Async XLA Ops:
  7.2 617.8 %reduce-scatter.4.cloned.1.call-start = ((), (), s32[]{:S(2)}) async-start(), calls=%async_computation.1 | async-start | bytes 1638400
  326.3 98.8 %collective-permute-start.7 = (bf16[160,1536]{1,0:T(8,128)(2,1)}, bf16[160,1536]{1,0:T(8,128)(2,1)}, u32[]{:S(2)}, u32[]{:S(2)}) collective-permute-start(bf16[160,1536]{1,0:T(8,128)(2,1)} %get-tuple-element.125), channel_id=1, source_target_pairs={{0,2},{1,3},{2,0},{3,1},{4,6},{5,7},{6,4},{7,5},{8,10},{9,11},{10,... | collective-permute-start | bytes 1474568 | tf_op jit(solution)/shard_map/ppermute | solution.py:109
  330.7 109.5 %collective-permute-start.6 = (bf16[160,1536]{1,0:T(8,128)(2,1)}, bf16[160,1536]{1,0:T(8,128)(2,1)}, u32[]{:S(2)}, u32[]{:S(2)}) collective-permute-start(bf16[160,1536]{1,0:T(8,128)(2,1)} %get-tuple-element.55), channel_id=1, source_target_pairs={{0,2},{1,3},{2,0},{3,1},{4,6},{5,7},{6,4},{7,5},{8,10},{9,11},{10,... | collective-permute-start | bytes 1474568 | tf_op jit(solution)/shard_map/ppermute | solution.py:109
  330.9 111.0 %collective-permute-start.10 = (bf16[160,1536]{1,0:T(8,128)(2,1)}, bf16[160,1536]{1,0:T(8,128)(2,1)}, u32[]{:S(2)}, u32[]{:S(2)}) collective-permute-start(bf16[160,1536]{1,0:T(8,128)(2,1)} %get-tuple-element.126), channel_id=1, source_target_pairs={{0,1},{1,0},{2,3},{3,2},{4,5},{5,4},{6,7},{7,6},{8,9},{9,8},{10,11... | collective-permute-start | bytes 1474568 | tf_op jit(solution)/shard_map/ppermute | solution.py:109
  332.7 140.5 %collective-permute-start.9 = (bf16[160,1536]{1,0:T(8,128)(2,1)}, bf16[160,1536]{1,0:T(8,128)(2,1)}, u32[]{:S(2)}, u32[]{:S(2)}) collective-permute-start(bf16[160,1536]{1,0:T(8,128)(2,1)} %get-tuple-element.56), channel_id=1, source_target_pairs={{0,1},{1,0},{2,3},{3,2},{4,5},{5,4},{6,7},{7,6},{8,9},{9,8},{10,11... | collective-permute-start | bytes 1474568 | tf_op jit(solution)/shard_map/ppermute | solution.py:109
  347.7 90.6 %collective-permute-start.1 = (bf16[160,1536]{1,0:T(8,128)(2,1)}, bf16[160,1536]{1,0:T(8,128)(2,1)}, u32[]{:S(2)}, u32[]{:S(2)}) collective-permute-start(bf16[160,1536]{1,0:T(8,128)(2,1)} %get-tuple-element.127), channel_id=1, source_target_pairs={{0,2},{1,3},{2,0},{3,1},{4,6},{5,7},{6,4},{7,5},{8,10},{9,11},{10,... | collective-permute-start | bytes 1474568 | tf_op jit(solution)/shard_map/ppermute | solution.py:109
  427.3 15.0 %collective-permute-start.8 = (bf16[160,1536]{1,0:T(8,128)(2,1)}, bf16[160,1536]{1,0:T(8,128)(2,1)}, u32[]{:S(2)}, u32[]{:S(2)}) collective-permute-start(bf16[160,1536]{1,0:T(8,128)(2,1)} %fusion.65), channel_id=1, source_target_pairs={{0,1},{1,0},{2,3},{3,2},{4,5},{5,4},{6,7},{7,6},{8,9},{9,8},{10,11... | collective-permute-start | bytes 1474568 | tf_op jit(solution)/shard_map/ppermute | solution.py:109
  440.2 14.4 %collective-permute-start.4 = (bf16[160,1536]{1,0:T(8,128)(2,1)}, bf16[160,1536]{1,0:T(8,128)(2,1)S(1)}, u32[]{:S(2)}, u32[]{:S(2)}) collective-permute-start(bf16[160,1536]{1,0:T(8,128)(2,1)} %get-tuple-element.128), channel_id=1, source_target_pairs={{0,1},{1,0},{2,3},{3,2},{4,5},{5,4},{6,7},{7,6},{8,9},{9,8},{10,11... | collective-permute-start | bytes 1474568 | tf_op jit(solution)/shard_map/ppermute | solution.py:109
  441.8 44.2 %collective-permute-start.3 = (bf16[160,1536]{1,0:T(8,128)(2,1)}, bf16[160,1536]{1,0:T(8,128)(2,1)S(1)}, u32[]{:S(2)}, u32[]{:S(2)}) collective-permute-start(bf16[160,1536]{1,0:T(8,128)(2,1)} %get-tuple-element.60), channel_id=1, source_target_pairs={{0,1},{1,0},{2,3},{3,2},{4,5},{5,4},{6,7},{7,6},{8,9},{9,8},{10,11... | collective-permute-start | bytes 1474568 | tf_op jit(solution)/shard_map/ppermute | solution.py:109
  442.3 27.8 %collective-permute-start.2 = (bf16[160,1536]{1,0:T(8,128)(2,1)S(1)}, bf16[160,1536]{1,0:T(8,128)(2,1)S(1)}, u32[]{:S(2)}, u32[]{:S(2)}) collective-permute-start(bf16[160,1536]{1,0:T(8,128)(2,1)S(1)} %fusion.73), channel_id=1, source_target_pairs={{0,1},{1,0},{2,3},{3,2},{4,5},{5,4},{6,7},{7,6},{8,9},{9,8},{10,11... | collective-permute-start | bytes 1474568 | tf_op jit(solution)/shard_map/ppermute | solution.py:109
  447.4 148.0 %collective-permute-start.32 = (bf16[4,192,2240]{2,1,0:T(8,128)(2,1)}, bf16[4,192,2240]{2,1,0:T(8,128)(2,1)}, u32[]{:S(2)}, u32[]{:S(2)}) collective-permute-start(bf16[4,192,2240]{2,1,0:T(8,128)(2,1)} %dynamic-slice_bitcast_fusion.2), channel_id=1, source_target_pairs={{0,4},{4,0},{8,12},{12,8},{16,20},{20,16},{24,28},{28,24},{1,5},{5... | collective-permute-start | bytes 10321928 | tf_op jit(solution)/shard_map/ppermute | solution.py:119
  454.6 152.8 %collective-permute-start.49 = (bf16[4,192,2240]{2,1,0:T(8,128)(2,1)}, bf16[4,192,2240]{2,1,0:T(8,128)(2,1)}, u32[]{:S(2)}, u32[]{:S(2)}) collective-permute-start(bf16[4,192,2240]{2,1,0:T(8,128)(2,1)} %dynamic-slice_bitcast_fusion.1), channel_id=1, source_target_pairs={{0,4},{4,0},{8,12},{12,8},{16,20},{20,16},{24,28},{28,24},{1,5},{5... | collective-permute-start | bytes 10321928 | tf_op jit(solution)/shard_map/ppermute | solution.py:119
  473.3 142.3 %collective-permute-start.66 = (bf16[1,1120,1536]{2,1,0:T(8,128)(2,1)}, bf16[1,1120,1536]{2,1,0:T(8,128)(2,1)}, u32[]{:S(2)}, u32[]{:S(2)}) collective-permute-start(bf16[1,1120,1536]{2,1,0:T(8,128)(2,1)} %dynamic-slice_bitcast_fusion.3), channel_id=1, source_target_pairs={{0,4},{4,0},{8,12},{12,8},{16,20},{20,16},{24,28},{28,24},{1,5},{5... | collective-permute-start | bytes 10321928 | tf_op jit(solution)/shard_map/ppermute | solution.py:119
  600.0 119.6 %collective-permute-start.33 = (bf16[4,48,2240]{2,1,0:T(8,128)(2,1)}, bf16[4,48,2240]{2,1,0:T(8,128)(2,1)}, u32[]{:S(2)}, u32[]{:S(2)}) collective-permute-start(bf16[4,48,2240]{2,1,0:T(8,128)(2,1)} %get-tuple-element.103), channel_id=1, source_target_pairs={{0,8},{4,12},{1,9},{5,13},{2,10},{6,14},{3,11},{7,15}} | collective-permute-start | bytes 2580488 | tf_op jit(solution)/shard_map/ppermute | solution.py:145
  605.6 126.9 %collective-permute-start.36 = (bf16[4,48,2240]{2,1,0:T(8,128)(2,1)}, bf16[4,48,2240]{2,1,0:T(8,128)(2,1)}, u32[]{:S(2)}, u32[]{:S(2)}) collective-permute-start(bf16[4,48,2240]{2,1,0:T(8,128)(2,1)} %get-tuple-element.104), channel_id=1, source_target_pairs={{24,16},{28,20},{25,17},{29,21},{26,18},{30,22},{27,19},{31,23}} | collective-permute-start | bytes 2580488 | tf_op jit(solution)/shard_map/ppermute | solution.py:146
  611.7 116.3 %collective-permute-start.50 = (bf16[4,48,2240]{2,1,0:T(8,128)(2,1)}, bf16[4,48,2240]{2,1,0:T(8,128)(2,1)}, u32[]{:S(2)}, u32[]{:S(2)}) collective-permute-start(bf16[4,48,2240]{2,1,0:T(8,128)(2,1)} %get-tuple-element.99), channel_id=1, source_target_pairs={{0,8},{4,12},{1,9},{5,13},{2,10},{6,14},{3,11},{7,15}} | collective-permute-start | bytes 2580488 | tf_op jit(solution)/shard_map/ppermute | solution.py:145
  614.0 156.0 %collective-permute-start.53 = (bf16[4,48,2240]{2,1,0:T(8,128)(2,1)}, bf16[4,48,2240]{2,1,0:T(8,128)(2,1)}, u32[]{:S(2)}, u32[]{:S(2)}) collective-permute-start(bf16[4,48,2240]{2,1,0:T(8,128)(2,1)} %get-tuple-element.100), channel_id=1, source_target_pairs={{24,16},{28,20},{25,17},{29,21},{26,18},{30,22},{27,19},{31,23}} | collective-permute-start | bytes 2580488 | tf_op jit(solution)/shard_map/ppermute | solution.py:146
  622.7 99.0 %collective-permute-start.67 = (bf16[1120,384]{1,0:T(8,128)(2,1)}, bf16[1120,384]{1,0:T(8,128)(2,1)}, u32[]{:S(2)}, u32[]{:S(2)}) collective-permute-start(bf16[1120,384]{1,0:T(8,128)(2,1)} %get-tuple-element.109), channel_id=1, source_target_pairs={{0,8},{4,12},{1,9},{5,13},{2,10},{6,14},{3,11},{7,15}} | collective-permute-start | bytes 2580488 | tf_op jit(solution)/shard_map/ppermute | solution.py:145
  719.6 33.1 %collective-permute-start.70 = (bf16[1120,384]{1,0:T(8,128)(2,1)S(1)}, bf16[1120,384]{1,0:T(8,128)(2,1)S(1)}, u32[]{:S(2)}, u32[]{:S(2)}) collective-permute-start(bf16[1120,384]{1,0:T(8,128)(2,1)S(1)} %copy-done.46), channel_id=1, source_target_pairs={{24,16},{28,20},{25,17},{29,21},{26,18},{30,22},{27,19},{31,23}} | collective-permute-start | bytes 2580488 | tf_op jit(solution)/shard_map/ppermute | solution.py:146
  721.7 24.9 %collective-permute-start.34 = (bf16[4,48,2240]{2,1,0:T(8,128)(2,1)S(1)}, bf16[4,48,2240]{2,1,0:T(8,128)(2,1)S(1)}, u32[]{:S(2)}, u32[]{:S(2)}) collective-permute-start(bf16[4,48,2240]{2,1,0:T(8,128)(2,1)S(1)} %fusion.42), channel_id=1, source_target_pairs={{0,8},{4,12},{8,16},{12,20},{1,9},{5,13},{9,17},{13,21},{2,10},{6,... | collective-permute-start | bytes 2580488 | tf_op jit(solution)/shard_map/ppermute | solution.py:145
  728.0 37.0 %collective-permute-start.68 = (bf16[1120,384]{1,0:T(8,128)(2,1)S(1)}, bf16[1120,384]{1,0:T(8,128)(2,1)S(1)}, u32[]{:S(2)}, u32[]{:S(2)}) collective-permute-start(bf16[1120,384]{1,0:T(8,128)(2,1)S(1)} %fusion.48), channel_id=1, source_target_pairs={{0,8},{4,12},{8,16},{12,20},{1,9},{5,13},{9,17},{13,21},{2,10},{6,... | collective-permute-start | bytes 2580488 | tf_op jit(solution)/shard_map/ppermute | solution.py:145
  732.5 318.8 %collective-permute-start.12 = (bf16[4,192,3584]{2,1,0:T(8,128)(2,1)}, bf16[4,192,3584]{2,1,0:T(8,128)(2,1)}, u32[]{:S(2)}, u32[]{:S(2)}) collective-permute-start(bf16[4,192,3584]{2,1,0:T(8,128)(2,1)} %dynamic-slice_bitcast_fusion), channel_id=1, source_target_pairs={{0,4},{4,0},{8,12},{12,8},{16,20},{20,16},{24,28},{28,24},{1,5},{5... | collective-permute-start | bytes 16515080 | tf_op jit(solution)/shard_map/ppermute | solution.py:119
  746.6 37.4 %collective-permute-start.51 = (bf16[4,48,2240]{2,1,0:T(8,128)(2,1)S(1)}, bf16[4,48,2240]{2,1,0:T(8,128)(2,1)S(1)}, u32[]{:S(2)}, u32[]{:S(2)}) collective-permute-start(bf16[4,48,2240]{2,1,0:T(8,128)(2,1)S(1)} %fusion.36), channel_id=1, source_target_pairs={{0,8},{4,12},{8,16},{12,20},{1,9},{5,13},{9,17},{13,21},{2,10},{6,... | collective-permute-start | bytes 2580488 | tf_op jit(solution)/shard_map/ppermute | solution.py:145
  752.7 33.6 %collective-permute-start.37 = (bf16[4,48,2240]{2,1,0:T(8,128)(2,1)S(1)}, bf16[4,48,2240]{2,1,0:T(8,128)(2,1)S(1)}, u32[]{:S(2)}, u32[]{:S(2)}) collective-permute-start(bf16[4,48,2240]{2,1,0:T(8,128)(2,1)S(1)} %get-tuple-element.102), channel_id=1, source_target_pairs={{16,8},{20,12},{24,16},{28,20},{17,9},{21,13},{25,17},{29,21},{18,... | collective-permute-start | bytes 2580488 | tf_op jit(solution)/shard_map/ppermute | solution.py:146
  765.0 51.2 %collective-permute-start.35 = (bf16[4,48,2240]{2,1,0:T(8,128)(2,1)S(1)}, bf16[4,48,2240]{2,1,0:T(8,128)(2,1)S(1)}, u32[]{:S(2)}, u32[]{:S(2)}) collective-permute-start(bf16[4,48,2240]{2,1,0:T(8,128)(2,1)S(1)} %get-tuple-element.101), channel_id=1, source_target_pairs={{0,8},{4,12},{8,16},{12,20},{16,24},{20,28},{1,9},{5,13},{9,17},{1... | collective-permute-start | bytes 2580488 | tf_op jit(solution)/shard_map/ppermute | solution.py:145
  770.0 21.8 %collective-permute-start.71 = (bf16[1120,384]{1,0:T(8,128)(2,1)S(1)}, bf16[1120,384]{1,0:T(8,128)(2,1)S(1)}, u32[]{:S(2)}, u32[]{:S(2)}) collective-permute-start(bf16[1120,384]{1,0:T(8,128)(2,1)S(1)} %get-tuple-element.108), channel_id=1, source_target_pairs={{16,8},{20,12},{24,16},{28,20},{17,9},{21,13},{25,17},{29,21},{18,... | collective-permute-start | bytes 2580488 | tf_op jit(solution)/shard_map/ppermute | solution.py:146
  786.3 66.3 %collective-permute-start.52 = (bf16[4,48,2240]{2,1,0:T(8,128)(2,1)S(1)}, bf16[4,48,2240]{2,1,0:T(8,128)(2,1)S(1)}, u32[]{:S(2)}, u32[]{:S(2)}) collective-permute-start(bf16[4,48,2240]{2,1,0:T(8,128)(2,1)S(1)} %get-tuple-element.97), channel_id=1, source_target_pairs={{0,8},{4,12},{8,16},{12,20},{16,24},{20,28},{1,9},{5,13},{9,17},{1... | collective-permute-start | bytes 2580488 | tf_op jit(solution)/shard_map/ppermute | solution.py:145
  791.8 25.8 %collective-permute-start.38 = (bf16[4,48,2240]{2,1,0:T(8,128)(2,1)S(1)}, bf16[4,48,2240]{2,1,0:T(8,128)(2,1)S(1)}, u32[]{:S(2)}, u32[]{:S(2)}) collective-permute-start(bf16[4,48,2240]{2,1,0:T(8,128)(2,1)S(1)} %fusion.41), channel_id=1, source_target_pairs={{8,0},{12,4},{16,8},{20,12},{24,16},{28,20},{9,1},{13,5},{17,9},{2... | collective-permute-start | bytes 2580488 | tf_op jit(solution)/shard_map/ppermute | solution.py:146
  793.3 45.4 %collective-permute-start.69 = (bf16[1120,384]{1,0:T(8,128)(2,1)S(1)}, bf16[1120,384]{1,0:T(8,128)(2,1)S(1)}, u32[]{:S(2)}, u32[]{:S(2)}) collective-permute-start(bf16[1120,384]{1,0:T(8,128)(2,1)S(1)} %get-tuple-element.107), channel_id=1, source_target_pairs={{0,8},{4,12},{8,16},{12,20},{16,24},{20,28},{1,9},{5,13},{9,17},{1... | collective-permute-start | bytes 2580488 | tf_op jit(solution)/shard_map/ppermute | solution.py:145
  816.2 39.4 %collective-permute-start.55 = (bf16[4,48,2240]{2,1,0:T(8,128)(2,1)S(1)}, bf16[4,48,2240]{2,1,0:T(8,128)(2,1)S(1)}, u32[]{:S(2)}, u32[]{:S(2)}) collective-permute-start(bf16[4,48,2240]{2,1,0:T(8,128)(2,1)S(1)} %fusion.35), channel_id=1, source_target_pairs={{8,0},{12,4},{16,8},{20,12},{24,16},{28,20},{9,1},{13,5},{17,9},{2... | collective-permute-start | bytes 2580488 | tf_op jit(solution)/shard_map/ppermute | solution.py:146
  817.6 34.7 %collective-permute-start.72 = (bf16[1120,384]{1,0:T(8,128)(2,1)S(1)}, bf16[1120,384]{1,0:T(8,128)(2,1)S(1)}, u32[]{:S(2)}, u32[]{:S(2)}) collective-permute-start(bf16[1120,384]{1,0:T(8,128)(2,1)S(1)} %fusion.47), channel_id=1, source_target_pairs={{8,0},{12,4},{16,8},{20,12},{24,16},{28,20},{9,1},{13,5},{17,9},{2... | collective-permute-start | bytes 2580488 | tf_op jit(solution)/shard_map/ppermute | solution.py:146
  838.7 36.2 %collective-permute-start.41 = (bf16[48,2240]{1,0:T(8,128)(2,1)S(1)}, bf16[48,2240]{1,0:T(8,128)(2,1)S(1)}, u32[]{:S(2)}, u32[]{:S(2)}) collective-permute-start(bf16[48,2240]{1,0:T(8,128)(2,1)S(1)} %get-tuple-element.142), channel_id=1, source_target_pairs={{0,3},{1,2},{2,1},{3,0},{4,7},{5,6},{6,5},{7,4},{8,11},{9,10},{10,... | collective-permute-start | bytes 645128 | tf_op jit(solution)/shard_map/ppermute | solution.py:1123
  852.3 23.3 %collective-permute-start.40 = (bf16[48,2240]{1,0:T(8,128)(2,1)S(1)}, bf16[48,2240]{1,0:T(8,128)(2,1)S(1)}, u32[]{:S(2)}, u32[]{:S(2)}) collective-permute-start(bf16[48,2240]{1,0:T(8,128)(2,1)S(1)} %get-tuple-element.143), channel_id=1, source_target_pairs={{0,2},{1,3},{2,0},{3,1},{4,6},{5,7},{6,4},{7,5},{8,10},{9,11},{10,... | collective-permute-start | bytes 645128 | tf_op jit(solution)/shard_map/ppermute | solution.py:1123
  852.6 23.8 %collective-permute-start.39 = (bf16[48,2240]{1,0:T(8,128)(2,1)S(1)}, bf16[48,2240]{1,0:T(8,128)(2,1)S(1)}, u32[]{:S(2)}, u32[]{:S(2)}) collective-permute-start(bf16[48,2240]{1,0:T(8,128)(2,1)S(1)} %get-tuple-element.144), channel_id=1, source_target_pairs={{0,1},{1,0},{2,3},{3,2},{4,5},{5,4},{6,7},{7,6},{8,9},{9,8},{10,11... | collective-permute-start | bytes 645128 | tf_op jit(solution)/shard_map/ppermute | solution.py:1123
  855.6 32.4 %collective-permute-start.73 = (bf16[1120,384]{1,0:T(8,128)(2,1)S(1)}, bf16[1120,384]{1,0:T(8,128)(2,1)}, u32[]{:S(2)}, u32[]{:S(2)}) collective-permute-start(bf16[1120,384]{1,0:T(8,128)(2,1)S(1)} %fusion.51), channel_id=1, source_target_pairs={{0,8},{4,12},{8,16},{12,20},{16,24},{20,28},{1,9},{5,13},{9,17},{1... | collective-permute-start | bytes 2580488 | tf_op jit(solution)/shard_map/ppermute | solution.py:157
  874.9 17.9 %collective-permute-start.58 = (bf16[48,2240]{1,0:T(8,128)(2,1)}, bf16[48,2240]{1,0:T(8,128)(2,1)S(1)}, u32[]{:S(2)}, u32[]{:S(2)}) collective-permute-start(bf16[48,2240]{1,0:T(8,128)(2,1)} %get-tuple-element.134), channel_id=1, source_target_pairs={{0,3},{1,2},{2,1},{3,0},{4,7},{5,6},{6,5},{7,4},{8,11},{9,10},{10,... | collective-permute-start | bytes 645128 | tf_op jit(solution)/shard_map/ppermute | solution.py:1123
  875.5 18.6 %collective-permute-start.57 = (bf16[48,2240]{1,0:T(8,128)(2,1)}, bf16[48,2240]{1,0:T(8,128)(2,1)S(1)}, u32[]{:S(2)}, u32[]{:S(2)}) collective-permute-start(bf16[48,2240]{1,0:T(8,128)(2,1)} %get-tuple-element.135), channel_id=1, source_target_pairs={{0,2},{1,3},{2,0},{3,1},{4,6},{5,7},{6,4},{7,5},{8,10},{9,11},{10,... | collective-permute-start | bytes 645128 | tf_op jit(solution)/shard_map/ppermute | solution.py:1123
  876.4 25.4 %collective-permute-start.56 = (bf16[48,2240]{1,0:T(8,128)(2,1)}, bf16[48,2240]{1,0:T(8,128)(2,1)S(1)}, u32[]{:S(2)}, u32[]{:S(2)}) collective-permute-start(bf16[48,2240]{1,0:T(8,128)(2,1)} %get-tuple-element.136), channel_id=1, source_target_pairs={{0,1},{1,0},{2,3},{3,2},{4,5},{5,4},{6,7},{7,6},{8,9},{9,8},{10,11... | collective-permute-start | bytes 645128 | tf_op jit(solution)/shard_map/ppermute | solution.py:1123
  888.0 15.0 %collective-permute-start.74 = (bf16[1120,384]{1,0:T(8,128)(2,1)}, bf16[1120,384]{1,0:T(8,128)(2,1)}, u32[]{:S(2)}, u32[]{:S(2)}) collective-permute-start(bf16[1120,384]{1,0:T(8,128)(2,1)} %collective-permute-done.73), channel_id=1, source_target_pairs={{8,16},{12,20},{16,24},{20,28},{9,17},{13,21},{17,25},{21,29},{10,... | collective-permute-start | bytes 2580488 | tf_op jit(solution)/shard_map/ppermute | solution.py:157
  892.8 29.2 %collective-permute-start.76 = (bf16[1120,384]{1,0:T(8,128)(2,1)S(1)}, bf16[1120,384]{1,0:T(8,128)(2,1)}, u32[]{:S(2)}, u32[]{:S(2)}) collective-permute-start(bf16[1120,384]{1,0:T(8,128)(2,1)S(1)} %copy-done.32), channel_id=1, source_target_pairs={{8,0},{12,4},{16,8},{20,12},{24,16},{28,20},{9,1},{13,5},{17,9},{2... | collective-permute-start | bytes 2580488 | tf_op jit(solution)/shard_map/ppermute | solution.py:158
  894.1 29.2 %collective-permute-start.42 = (bf16[48,8960]{1,0:T(8,128)(2,1)}, bf16[48,8960]{1,0:T(8,128)(2,1)}, u32[]{:S(2)}, u32[]{:S(2)}) collective-permute-start(bf16[48,8960]{1,0:T(8,128)(2,1)} %reshape.487), channel_id=1, source_target_pairs={{0,8},{4,12},{8,16},{12,20},{16,24},{20,28},{1,9},{5,13},{9,17},{1... | collective-permute-start | bytes 2580488 | tf_op jit(solution)/shard_map/ppermute | solution.py:157
  901.7 30.8 %collective-permute-start.45 = (bf16[48,8960]{1,0:T(8,128)(2,1)}, bf16[48,8960]{1,0:T(8,128)(2,1)}, u32[]{:S(2)}, u32[]{:S(2)}) collective-permute-start(bf16[48,8960]{1,0:T(8,128)(2,1)} %reshape.487), channel_id=1, source_target_pairs={{8,0},{12,4},{16,8},{20,12},{24,16},{28,20},{9,1},{13,5},{17,9},{2... | collective-permute-start | bytes 2580488 | tf_op jit(solution)/shard_map/ppermute | solution.py:158
  907.8 27.7 %collective-permute-start.59 = (bf16[48,8960]{1,0:T(8,128)(2,1)}, bf16[48,8960]{1,0:T(8,128)(2,1)S(1)}, u32[]{:S(2)}, u32[]{:S(2)}) collective-permute-start(bf16[48,8960]{1,0:T(8,128)(2,1)} %reshape.491), channel_id=1, source_target_pairs={{0,8},{4,12},{8,16},{12,20},{16,24},{20,28},{1,9},{5,13},{9,17},{1... | collective-permute-start | bytes 2580488 | tf_op jit(solution)/shard_map/ppermute | solution.py:157
  922.0 49.5 %collective-permute-start.62 = (bf16[48,8960]{1,0:T(8,128)(2,1)}, bf16[48,8960]{1,0:T(8,128)(2,1)S(1)}, u32[]{:S(2)}, u32[]{:S(2)}) collective-permute-start(bf16[48,8960]{1,0:T(8,128)(2,1)} %reshape.491), channel_id=1, source_target_pairs={{8,0},{12,4},{16,8},{20,12},{24,16},{28,20},{9,1},{13,5},{17,9},{2... | collective-permute-start | bytes 2580488 | tf_op jit(solution)/shard_map/ppermute | solution.py:158
  923.4 66.7 %collective-permute-start.77 = (bf16[1120,384]{1,0:T(8,128)(2,1)}, bf16[1120,384]{1,0:T(8,128)(2,1)S(1)}, u32[]{:S(2)}, u32[]{:S(2)}) collective-permute-start(bf16[1120,384]{1,0:T(8,128)(2,1)} %collective-permute-done.76), channel_id=1, source_target_pairs={{8,0},{12,4},{16,8},{20,12},{9,1},{13,5},{17,9},{21,13},{10,2},{14... | collective-permute-start | bytes 2580488 | tf_op jit(solution)/shard_map/ppermute | solution.py:158
  932.5 58.8 %collective-permute-start.43 = (bf16[48,8960]{1,0:T(8,128)(2,1)}, bf16[48,8960]{1,0:T(8,128)(2,1)}, u32[]{:S(2)}, u32[]{:S(2)}) collective-permute-start(bf16[48,8960]{1,0:T(8,128)(2,1)} %collective-permute-done.42), channel_id=1, source_target_pairs={{8,16},{12,20},{16,24},{20,28},{9,17},{13,21},{17,25},{21,29},{10,... | collective-permute-start | bytes 2580488 | tf_op jit(solution)/shard_map/ppermute | solution.py:157
  935.6 72.9 %collective-permute-start.46 = (bf16[48,8960]{1,0:T(8,128)(2,1)}, bf16[48,8960]{1,0:T(8,128)(2,1)}, u32[]{:S(2)}, u32[]{:S(2)}) collective-permute-start(bf16[48,8960]{1,0:T(8,128)(2,1)} %collective-permute-done.45), channel_id=1, source_target_pairs={{8,0},{12,4},{16,8},{20,12},{9,1},{13,5},{17,9},{21,13},{10,2},{14... | collective-permute-start | bytes 2580488 | tf_op jit(solution)/shard_map/ppermute | solution.py:158
  971.6 38.5 %collective-permute-start.60 = (bf16[48,8960]{1,0:T(8,128)(2,1)S(1)}, bf16[48,8960]{1,0:T(8,128)(2,1)}, u32[]{:S(2)}, u32[]{:S(2)}) collective-permute-start(bf16[48,8960]{1,0:T(8,128)(2,1)S(1)} %collective-permute-done.59), channel_id=1, source_target_pairs={{8,16},{12,20},{16,24},{20,28},{9,17},{13,21},{17,25},{21,29},{10,... | collective-permute-start | bytes 2580488 | tf_op jit(solution)/shard_map/ppermute | solution.py:157
  990.0 37.0 %collective-permute-start.63 = (bf16[48,8960]{1,0:T(8,128)(2,1)S(1)}, bf16[48,8960]{1,0:T(8,128)(2,1)}, u32[]{:S(2)}, u32[]{:S(2)}) collective-permute-start(bf16[48,8960]{1,0:T(8,128)(2,1)S(1)} %collective-permute-done.62), channel_id=1, source_target_pairs={{8,0},{12,4},{16,8},{20,12},{9,1},{13,5},{17,9},{21,13},{10,2},{14... | collective-permute-start | bytes 2580488 | tf_op jit(solution)/shard_map/ppermute | solution.py:158
  991.3 54.0 %collective-permute-start.78 = (bf16[1120,384]{1,0:T(8,128)(2,1)S(1)}, bf16[1120,384]{1,0:T(8,128)(2,1)S(1)}, u32[]{:S(2)}, u32[]{:S(2)}) collective-permute-start(bf16[1120,384]{1,0:T(8,128)(2,1)S(1)} %collective-permute-done.77), channel_id=1, source_target_pairs={{8,0},{12,4},{9,1},{13,5},{10,2},{14,6},{11,3},{15,7}} | collective-permute-start | bytes 2580488 | tf_op jit(solution)/shard_map/ppermute | solution.py:158
  1008.6 52.4 %collective-permute-start.44 = (bf16[48,8960]{1,0:T(8,128)(2,1)}, bf16[48,8960]{1,0:T(8,128)(2,1)}, u32[]{:S(2)}, u32[]{:S(2)}) collective-permute-start(bf16[48,8960]{1,0:T(8,128)(2,1)} %collective-permute-done.43), channel_id=1, source_target_pairs={{16,24},{20,28},{17,25},{21,29},{18,26},{22,30},{19,27},{23,31}} | collective-permute-start | bytes 2580488 | tf_op jit(solution)/shard_map/ppermute | solution.py:157
  1010.1 62.0 %collective-permute-start.47 = (bf16[48,8960]{1,0:T(8,128)(2,1)}, bf16[48,8960]{1,0:T(8,128)(2,1)}, u32[]{:S(2)}, u32[]{:S(2)}) collective-permute-start(bf16[48,8960]{1,0:T(8,128)(2,1)} %collective-permute-done.46), channel_id=1, source_target_pairs={{8,0},{12,4},{9,1},{13,5},{10,2},{14,6},{11,3},{15,7}} | collective-permute-start | bytes 2580488 | tf_op jit(solution)/shard_map/ppermute | solution.py:158
  1027.0 40.8 %collective-permute-start.61 = (bf16[48,8960]{1,0:T(8,128)(2,1)}, bf16[48,8960]{1,0:T(8,128)(2,1)}, u32[]{:S(2)}, u32[]{:S(2)}) collective-permute-start(bf16[48,8960]{1,0:T(8,128)(2,1)} %collective-permute-done.60), channel_id=1, source_target_pairs={{16,24},{20,28},{17,25},{21,29},{18,26},{22,30},{19,27},{23,31}} | collective-permute-start | bytes 2580488 | tf_op jit(solution)/shard_map/ppermute | solution.py:157
  1045.3 88.3 %collective-permute-start.64 = (bf16[48,8960]{1,0:T(8,128)(2,1)}, bf16[48,8960]{1,0:T(8,128)(2,1)}, u32[]{:S(2)}, u32[]{:S(2)}) collective-permute-start(bf16[48,8960]{1,0:T(8,128)(2,1)} %collective-permute-done.63), channel_id=1, source_target_pairs={{8,0},{12,4},{9,1},{13,5},{10,2},{14,6},{11,3},{15,7}} | collective-permute-start | bytes 2580488 | tf_op jit(solution)/shard_map/ppermute | solution.py:158
  1051.3 95.7 %collective-permute-start.79 = (bf16[1120,1536]{1,0:T(8,128)(2,1)}, bf16[1120,1536]{1,0:T(8,128)(2,1)}, u32[]{:S(2)}, u32[]{:S(2)}) collective-permute-start(bf16[1120,1536]{1,0:T(8,128)(2,1)} %get-tuple-element.106), channel_id=1, source_target_pairs={{0,4},{4,0},{8,12},{12,8},{16,20},{20,16},{24,28},{28,24},{1,5},{5... | collective-permute-start | bytes 10321928 | tf_op jit(solution)/shard_map/ppermute | solution.py:119
  1060.9 18.4 %collective-permute-start.14 = (bf16[96,3584]{1,0:T(8,128)(2,1)S(1)}, bf16[96,3584]{1,0:T(8,128)(2,1)S(1)}, u32[]{:S(2)}, u32[]{:S(2)}) collective-permute-start(bf16[96,3584]{1,0:T(8,128)(2,1)S(1)} %get-tuple-element.88), channel_id=1, source_target_pairs={{0,2},{1,3},{2,0},{3,1},{4,6},{5,7},{6,4},{7,5},{8,10},{9,11},{10,... | collective-permute-start | bytes 2064392 | tf_op jit(solution)/shard_map/ppermute | solution.py:109
  1067.8 24.5 %collective-permute-start.13 = (bf16[96,3584]{1,0:T(8,128)(2,1)S(1)}, bf16[96,3584]{1,0:T(8,128)(2,1)S(1)}, u32[]{:S(2)}, u32[]{:S(2)}) collective-permute-start(bf16[96,3584]{1,0:T(8,128)(2,1)S(1)} %get-tuple-element.87), channel_id=1, source_target_pairs={{0,2},{1,3},{2,0},{3,1},{4,6},{5,7},{6,4},{7,5},{8,10},{9,11},{10,... | collective-permute-start | bytes 2064392 | tf_op jit(solution)/shard_map/ppermute | solution.py:109
  1072.2 20.7 %collective-permute-start.17 = (bf16[96,3584]{1,0:T(8,128)(2,1)S(1)}, bf16[96,3584]{1,0:T(8,128)(2,1)S(1)}, u32[]{:S(2)}, u32[]{:S(2)}) collective-permute-start(bf16[96,3584]{1,0:T(8,128)(2,1)S(1)} %get-tuple-element.89), channel_id=1, source_target_pairs={{0,1},{1,0},{2,3},{3,2},{4,5},{5,4},{6,7},{7,6},{8,9},{9,8},{10,11... | collective-permute-start | bytes 2064392 | tf_op jit(solution)/shard_map/ppermute | solution.py:109
  1079.6 25.8 %collective-permute-start.15 = (bf16[96,3584]{1,0:T(8,128)(2,1)S(1)}, bf16[96,3584]{1,0:T(8,128)(2,1)S(1)}, u32[]{:S(2)}, u32[]{:S(2)}) collective-permute-start(bf16[96,3584]{1,0:T(8,128)(2,1)S(1)} %fusion.57), channel_id=1, source_target_pairs={{0,1},{1,0},{2,3},{3,2},{4,5},{5,4},{6,7},{7,6},{8,9},{9,8},{10,11... | collective-permute-start | bytes 2064392 | tf_op jit(solution)/shard_map/ppermute | solution.py:109
  1092.3 25.4 %collective-permute-start.16 = (bf16[96,3584]{1,0:T(8,128)(2,1)S(1)}, bf16[96,3584]{1,0:T(8,128)(2,1)S(1)}, u32[]{:S(2)}, u32[]{:S(2)}) collective-permute-start(bf16[96,3584]{1,0:T(8,128)(2,1)S(1)} %get-tuple-element.90), channel_id=1, source_target_pairs={{0,1},{1,0},{2,3},{3,2},{4,5},{5,4},{6,7},{7,6},{8,9},{9,8},{10,11... | collective-permute-start | bytes 2064392 | tf_op jit(solution)/shard_map/ppermute | solution.py:109
  1092.9 76.6 %collective-permute-start.48 = (bf16[192,8960]{1,0:T(8,128)(2,1)S(1)}, bf16[192,8960]{1,0:T(8,128)(2,1)}, u32[]{:S(2)}, u32[]{:S(2)}) collective-permute-start(bf16[192,8960]{1,0:T(8,128)(2,1)S(1)} %bitcast.533), channel_id=1, source_target_pairs={{0,4},{4,0},{8,12},{12,8},{16,20},{20,16},{24,28},{28,24},{1,5},{5... | collective-permute-start | bytes 10321928 | tf_op jit(solution)/shard_map/ppermute | solution.py:119
  1139.6 43.7 %collective-permute-start.65 = (bf16[192,8960]{1,0:T(8,128)(2,1)S(1)}, bf16[192,8960]{1,0:T(8,128)(2,1)}, u32[]{:S(2)}, u32[]{:S(2)}) collective-permute-start(bf16[192,8960]{1,0:T(8,128)(2,1)S(1)} %bitcast.535), channel_id=1, source_target_pairs={{0,4},{4,0},{8,12},{12,8},{16,20},{20,16},{24,28},{28,24},{1,5},{5... | collective-permute-start | bytes 10321928 | tf_op jit(solution)/shard_map/ppermute | solution.py:119
  1139.7 19.0 %collective-permute-start.21 = (bf16[48,3584]{1,0:T(8,128)(2,1)S(1)}, bf16[48,3584]{1,0:T(8,128)(2,1)}, u32[]{:S(2)}, u32[]{:S(2)}) collective-permute-start(bf16[48,3584]{1,0:T(8,128)(2,1)S(1)} %get-tuple-element.119), channel_id=1, source_target_pairs={{0,8},{4,12},{8,16},{12,20},{16,24},{20,28},{1,9},{5,13},{9,17},{1... | collective-permute-start | bytes 1032200 | tf_op jit(solution)/shard_map/ppermute | solution.py:145
  1160.1 14.0 %collective-permute-start.25 = (bf16[48,3584]{1,0:T(8,128)(2,1)S(1)}, bf16[48,3584]{1,0:T(8,128)(2,1)}, u32[]{:S(2)}, u32[]{:S(2)}) collective-permute-start(bf16[48,3584]{1,0:T(8,128)(2,1)S(1)} %fusion.83), channel_id=1, source_target_pairs={{0,8},{4,12},{8,16},{12,20},{16,24},{20,28},{1,9},{5,13},{9,17},{1... | collective-permute-start | bytes 1032200 | tf_op jit(solution)/shard_map/ppermute | solution.py:157
  (100 other events, 1362.7 us)
Sparse Core Ops, SparseCore 0:
  572.5 29.5 reduce-scatter.3

commit v3 on v2

--- a/solution.py
+++ b/solution.py
@@ -651,6 +651,765 @@
     )(lengths, starts, x, cot, vec, inverse, wqkv, wo, pieces)
 
 
+class Stream:
+    def __init__(self, links, pairs, size, own, land_end, land_mid, final, loads, stage, sems, local_sems, targets):
+        self.links, self.pairs, self.size = links, pairs, size
+        self.own, self.land_end, self.land_mid, self.final = own, land_end, land_mid, final
+        self.loads, self.stage, self.sems, self.local_sems = loads, stage, sems, local_sems
+        self.targets = targets
+        self.near = links.line // 2
+        self.far = 1 - self.near
+        self.busy = {}
+
+    def rows(self, kind, p):
+        return pl.ds(pl.multiple_of((kind * self.pairs + p) * self.size, self.size), self.size)
+
+    def copy(self, src, dst, p, index, device):
+        return pltpu.make_async_remote_copy(
+            src_ref=src,
+            dst_ref=dst,
+            send_sem=self.sems.at[0, p, index],
+            recv_sem=self.sems.at[1, p, index],
+            device_id=device,
+            device_id_type=MESH,
+        )
+
+    def total(self, refs):
+        copies = [
+            pltpu.make_async_copy(ref, self.loads.at[i], self.local_sems.at[i]) for i, ref in enumerate(refs)
+        ]
+        for copy in copies:
+            copy.start()
+        for copy in copies:
+            copy.wait()
+        out = self.loads[0].astype(jnp.float32)
+        for i in range(1, len(refs)):
+            out = out + self.loads[i].astype(jnp.float32)
+        return out.astype(jnp.bfloat16)
+
+    def free(self, role, which, p):
+        for copy in self.busy.pop((role, which, p % 2), list)():
+            copy.wait_send()
+
+    def hold(self, role, which, p, make):
+        copies = make()
+        for copy in copies:
+            copy.start()
+        self.busy[(role, which, p % 2)] = make
+
+    def finals(self, p, which):
+        links = self.links
+        near, far = self.rows(self.near, p), self.rows(self.far, p)
+        ref_near, ref_far = self.final(links.core, near), self.final(links.core, far)
+        plans = (
+            (ref_near, 3, links.away),
+            (ref_near, 4, links.toward),
+            (ref_far, 5, links.away),
+            (ref_near, 6, links.partner),
+            (ref_far, 7, links.partner),
+        )
+        return [
+            self.copy(ref, ref, p, index, device)
+            for i, (ref, index, device) in enumerate(plans)
+            if i in which
+        ]
+
+    def end_send(self, p):
+        for which, kind in ((0, self.far), (1, self.near)):
+            self.free("end", which, p)
+            self.stage[which, p % 2] = self.total(self.own(self.rows(kind, p)))
+            self.hold(
+                "end",
+                which,
+                p,
+                lambda which=which: [
+                    self.copy(
+                        self.stage.at[which, p % 2], self.land_end.at[p, which], p, which, self.links.toward
+                    )
+                ],
+            )
+
+    def mid_pass(self, p):
+        self.free("mid", 0, p)
+        self.copy(self.land_end.at[p, 0], self.land_end.at[p, 0], p, 0, self.links.away).wait_recv()
+        self.stage[0, p % 2] = self.total(self.own(self.rows(self.far, p)) + [self.land_end.at[p, 0]])
+        self.hold(
+            "mid",
+            0,
+            p,
+            lambda: [self.copy(self.stage.at[0, p % 2], self.land_mid.at[p], p, 2, self.links.toward)],
+        )
+
+    def mid_sum(self, p):
+        links = self.links
+        self.free("mid", 1, p)
+        self.copy(self.land_end.at[p, 1], self.land_end.at[p, 1], p, 1, links.away).wait_recv()
+        self.copy(self.land_mid.at[p], self.land_mid.at[p], p, 2, links.toward).wait_recv()
+        near = self.rows(self.near, p)
+        self.stage[1, p % 2] = self.total(self.own(near) + [self.land_end.at[p, 1], self.land_mid.at[p]])
+        self.own_copy(p).start()
+
+        def sends():
+            buf = self.stage.at[1, p % 2]
+            near = self.rows(self.near, p)
+            final = self.final(links.core, near)
+            if self.targets:
+                ref = self.target(links.core, near, links.here)
+                return [
+                    self.copy(buf.at[links.near[d]], ref, p, 7 + d, links.plane[d]) for d in (1, 2, 3)
+                ]
+            return [
+                self.copy(buf, final, p, 3, links.away),
+                self.copy(buf, final, p, 4, links.toward),
+                self.copy(buf, final, p, 6, links.partner),
+            ]
+
+        self.hold("mid", 1, p, sends)
+
+    def own_copy(self, p):
+        links = self.links
+        buf, near = self.stage.at[1, p % 2], self.rows(self.near, p)
+        final = self.final(links.core, near)
+        if self.targets:
+            buf, final = buf.at[links.here], self.target(links.core, near, links.here)
+        return pltpu.make_async_copy(buf, final, self.local_sems.at[6 + p % 2])
+
+    def target(self, core, rows, source):
+        return self.final(core, rows).at[source]
+
+    def mid_out(self, p):
+        links = self.links
+        self.own_copy(p).wait()
+        if not self.targets:
+            return
+        near = self.rows(self.near, p)
+        for d in (1, 2, 3):
+            ref = self.target(links.core, near, links.near[d])
+            self.copy(ref, ref, p, 7 + d, links.plane[d]).wait_recv()
+        for copy in self.finals(p, (0, 1, 3)):
+            copy.start()
+
+    def mid_far(self, p):
+        far = self.final(self.links.core, self.rows(self.far, p))
+        self.copy(far, far, p, 4, self.links.toward).wait_recv()
+        for copy in self.finals(p, (2, 4)):
+            copy.start()
+
+    def end_take(self, p):
+        for kind, index, out in ((self.near, 3, 3), (self.far, 5, 4)):
+            ref = self.final(self.links.core, self.rows(kind, p))
+            self.copy(ref, ref, p, index, self.links.toward).wait_recv()
+            self.finals(p, (out,))[0].start()
+
+    def close_mid(self):
+        for key in [k for k in self.busy if k[0] == "mid"]:
+            for copy in self.busy.pop(key)():
+                copy.wait_send()
+        for p in range(self.pairs):
+            for copy in self.finals(p, (0, 1, 2, 3, 4) if self.targets else (2, 4)):
+                copy.wait_send()
+
+    def close_end(self):
+        for key in [k for k in self.busy if k[0] == "end"]:
+            for copy in self.busy.pop(key)():
+                copy.wait_send()
+        for p in range(self.pairs):
+            for copy in self.finals(p, (3, 4)):
+                copy.wait_send()
+
+    def close_core(self):
+        for p in range(self.pairs):
+            for kind, index in ((self.near, 6), (self.far, 7)):
+                ref = self.final(1 - self.links.core, self.rows(kind, p))
+                self.copy(ref, ref, p, index, self.links.partner).wait_recv()
+
+
+def epilogue_kernel(
+    lengths_ref,
+    starts_ref,
+    query_ref,
+    lse_ref,
+    trig_ref,
+    gains_ref,
+    x_hbm,
+    cot_hbm,
+    mid_hbm,
+    part_hbm,
+    normed_hbm,
+    attn_hbm,
+    mlp_hbm,
+    kv_hbm,
+    wqkv_hbm,
+    wo_hbm,
+    down_part,
+    gate_part,
+    up_part,
+    grad_input_ref,
+    sums_ref,
+    down_final,
+    gate_final,
+    up_final,
+    attn_final,
+    down_core,
+    gate_core,
+    up_core,
+    attn_core,
+    attn_own,
+    mlp_land,
+    down_end,
+    down_mid,
+    gate_end,
+    gate_mid,
+    up_end,
+    up_mid,
+    attn_end,
+    attn_mid,
+    kv_buf,
+    key_turned,
+    bias_ref,
+    lse_turned,
+    dmid_ref,
+    branch_ref,
+    dattn_ref,
+    dqkv_ref,
+    dkey_ref,
+    dvalue_ref,
+    kv_out,
+    kv_land,
+    normed_turned,
+    attn_turned,
+    half_buf,
+    half_load,
+    plane_first,
+    plane_second,
+    plane_send,
+    vec_plane,
+    vec_core,
+    vec_line,
+    vec_send,
+    down_loads,
+    down_stage,
+    gu_loads,
+    gate_stage,
+    up_stage,
+    attn_loads,
+    attn_stage,
+    local_sems,
+    scope_sems,
+    mlp_sems,
+    load_sems,
+    core_sems,
+    kv_sems,
+    half_sems,
+    plane_sems,
+    vec_sems,
+    down_sems,
+    gate_sems,
+    up_sems,
+    attn_sems,
+):
+    links = Links()
+    here, core, line = links.here, links.core, links.line
+    rows, width = x_hbm.shape
+    scale = 1.0 / HDIM**0.5
+    group = HEADS // KVH
+    bf16, f32 = jnp.bfloat16, jnp.float32
+    step = 2 - 4 * (line // 2)
+    links.toward = {"rep": links.rep + step}
+    links.away = {"rep": links.rep - step}
+    is_end = (line == 0) | (line == 3)
+    is_mid = (line == 1) | (line == 2)
+
+    barrier = pltpu.get_barrier_semaphore()
+    line_others = [{"rep": 2 * lax.rem(line + j, 4) + core} for j in (1, 2, 3)]
+    others = links.plane[1:] + [links.partner] + line_others
+    for other in others:
+        pl.semaphore_signal(barrier, inc=1, device_id=other, device_id_type=MESH)
+    pl.semaphore_wait(barrier, len(others))
+
+    swaps = [
+        remote(down_part.at[1 - core], down_core, core_sems, 0, links.partner),
+        remote(gate_part.at[:, 1 - core], gate_core, core_sems, 1, links.partner),
+        remote(up_part.at[:, 1 - core], up_core, core_sems, 2, links.partner),
+    ]
+    for swap in swaps:
+        swap.start()
+    fetches = [pltpu.make_async_copy(kv_hbm, kv_buf, local_sems.at[1])]
+    mlp_sends = [
+        remote(mlp_hbm.at[links.near[d]], mlp_land.at[d - 1], mlp_sems, d - 1, links.plane[d]) for d in (1, 2, 3)
+    ]
+    for copy in mlp_sends:
+        copy.start()
+    for fetch in fetches:
+        fetch.start()
+
+    def stream(size, total, own, end, mid, final, loads, stage, sems, targets=False):
+        return Stream(
+            links, total // (2 * size), size, own, end, mid, final, loads, stage, sems, load_sems, targets
+        )
+
+    down = stream(
+        down_stage.shape[2],
+        down_core.shape[0],
+        lambda r: [down_part.at[core, r], down_core.at[r]],
+        down_end,
+        down_mid,
+        lambda c, r: down_final.at[c, r],
+        down_loads,
+        down_stage,
+        down_sems,
+    )
+    gate = stream(
+        gate_stage.shape[3],
+        gate_core.shape[1],
+        lambda r: [gate_part.at[:, core, r], gate_core.at[:, r]],
+        gate_end,
+        gate_mid,
+        lambda c, r: gate_final.at[c, :, r],
+        gu_loads,
+        gate_stage,
+        gate_sems,
+        True,
+    )
+    up = stream(
+        up_stage.shape[3],
+        up_core.shape[1],
+        lambda r: [up_part.at[:, core, r], up_core.at[:, r]],
+        up_end,
+        up_mid,
+        lambda c, r: up_final.at[c, :, r],
+        gu_loads,
+        up_stage,
+        up_sems,
+        True,
+    )
+    attn = stream(
+        attn_stage.shape[2],
+        attn_own.shape[0],
+        lambda r: [attn_own.at[r]],
+        attn_end,
+        attn_mid,
+        lambda c, r: attn_final.at[c, r],
+        attn_loads,
+        attn_stage,
+        attn_sems,
+    )
+    pairs = [(s, p) for s in (down, gate, up, attn) for p in range(s.pairs)]
+
+    def service(n):
+        def at(back):
+            return pairs[n - back] if 0 <= n - back < len(pairs) else None
+
+        first = {0: down, down.pairs: gate, down.pairs + gate.pairs: up}
+        if n in first:
+            swaps[list(first).index(n)].wait_recv()
+
+        @pl.when(is_end)
+        def _():
+            for back, action in ((7, "end_take"), (0, "end_send")):
+                if at(back):
+                    getattr(at(back)[0], action)(at(back)[1])
+
+        @pl.when(is_mid)
+        def _():
+            for back, action in ((4, "mid_far"), (3, "mid_out"), (2, "mid_sum"), (1, "mid_pass")):
+                if at(back):
+                    getattr(at(back)[0], action)(at(back)[1])
+
+    def scoped(refs, body):
+        def inner(*bufs):
+            copies = [pltpu.make_async_copy(r, b, scope_sems.at[i]) for i, (r, b) in enumerate(zip(refs, bufs))]
+            for copy in copies:
+                copy.start()
+            for copy in copies:
+                copy.wait()
+            body(*bufs)
+
+        pl.run_scoped(inner, *[pltpu.VMEM(r.shape, r.dtype) for r in refs])
+
+    def norm_back():
+        scoped((mid_hbm, part_hbm, cot_hbm), norm_body)
+
+    def norm_body(mid_ref, part_ref, cot_ref):
+        mid = mid_ref[...]
+        inv = lax.rsqrt(jnp.mean(mid * mid, axis=1, keepdims=True) + epsilon)
+        unit = mid * inv
+        part = part_ref[...]
+        vec_send[2:3, :] = jnp.sum(part * unit, axis=0, keepdims=True)
+        scaled = part * gains_ref[2:3, :]
+        d_mid = cot_ref[...].astype(f32) + inv * (
+            scaled - unit * jnp.mean(scaled * unit, axis=1, keepdims=True)
+        )
+        dmid_ref[...] = d_mid
+        branch_ref[...] = d_mid.astype(bf16)
+        query_pos = here * rows + lax.broadcasted_iota(jnp.int32, (1, rows), 1)
+        key_pos = lax.broadcasted_iota(jnp.int32, (4 * rows, 1), 0)
+        query_doc, unused, query_piece = layout_of(query_pos, lengths_ref, starts_ref)
+        key_doc, unused, key_piece = layout_of(key_pos, lengths_ref, starts_ref)
+        allowed = (query_doc == key_doc) & (
+            (key_pos <= query_pos) | ((query_piece == key_piece) & (query_piece > 0))
+        )
+        bias_ref[...] = jnp.where(allowed, 0.0, MASKED)
+        lse_turned[...] = lse_ref[...].T
+
+    def attn_back():
+        scoped((wo_hbm,), attn_body)
+
+    def attn_body(wo_buf):
+        def tile(i, carry):
+            columns = pl.ds(pl.multiple_of(i * 256, 256), 256)
+            dattn_ref[:, columns] = dot_f32(branch_ref[...], wo_buf[columns, :], ((1,), (1,))).astype(bf16)
+            return carry
+
+        lax.fori_loop(0, width // 256, tile, 0)
+        fetches[0].wait()
+        for g in range(KVH):
+            key_turned[g] = kv_buf[:, :, g * HDIM : (g + 1) * HDIM].reshape(4 * rows, HDIM).T
+        dkey_ref[...] = jnp.zeros_like(dkey_ref)
+        dvalue_ref[...] = jnp.zeros_like(dvalue_ref)
+
+    def head_back(h, carry):
+        columns = pl.ds(pl.multiple_of(h * HDIM, HDIM), HDIM)
+        shared = h // group
+        key = kv_buf[:, :, pl.ds(pl.multiple_of(shared * HDIM, HDIM), HDIM)].reshape(4 * rows, HDIM)
+        value = kv_buf[:, :, pl.ds(pl.multiple_of((KVH + shared) * HDIM, HDIM), HDIM)].reshape(
+            4 * rows, HDIM
+        )
+        query, d_out = query_ref[:, columns], dattn_ref[:, columns]
+        scores = dot_f32(key, query, ((1,), (1,))) * scale + bias_ref[...]
+        probs = jnp.exp(scores - lse_turned[pl.ds(h, 1), :])
+        d_probs = dot_f32(value, d_out, ((1,), (1,)))
+        delta = jnp.sum(probs * d_probs, axis=0, keepdims=True)
+        d_scores = (probs * (d_probs - delta)).astype(bf16)
+        dkey_ref[shared] += dot_f32(d_scores, query)
+        dvalue_ref[shared] += dot_f32(probs.astype(bf16), d_out)
+        d_query = dot_f32(key_turned[shared], d_scores).T * scale
+        d_query = d_query * trig_ref[0] - pltpu.roll(d_query, HDIM // 2, 1) * trig_ref[1]
+        dqkv_ref[:, columns] = d_query.astype(bf16)
+        return carry
+
+    kv_sends = [
+        remote(kv_out.at[links.near[d]], kv_land.at[d - 1], kv_sems, d - 1, links.plane[d]) for d in (1, 2, 3)
+    ]
+
+    def kv_send():
+        for g in range(KVH):
+            kv_out[:, :, g * HDIM : (g + 1) * HDIM] = (
+                (dkey_ref[g] * scale).astype(bf16).reshape(4, rows, HDIM)
+            )
+            kv_out[:, :, (KVH + g) * HDIM : (KVH + g + 1) * HDIM] = (
+                dvalue_ref[g].astype(bf16).reshape(4, rows, HDIM)
+            )
+        for copy in kv_sends:
+            copy.start()
+
+    vec_copies = {
+        "plane": [remote(vec_send, vec_plane.at[here], vec_sems, d - 1, links.plane[d]) for d in (1, 2, 3)],
+        "core": [remote(vec_core.at[core], vec_core.at[core], vec_sems, 3, links.partner)],
+        "line": [
+            remote(vec_line.at[line], vec_line.at[line], vec_sems, 4 + j, line_others[j]) for j in range(3)
+        ],
+    }
+    vec_comes = {
+        "plane": [
+            remote(vec_send, vec_plane.at[links.near[d]], vec_sems, d - 1, links.plane[d]) for d in (1, 2, 3)
+        ],
+        "core": [remote(vec_core.at[core], vec_core.at[1 - core], vec_sems, 3, links.partner)],
+        "line": [
+            remote(
+                vec_line.at[line],
+                vec_line.at[lax.rem(line + 3 - j, 4)],
+                vec_sems,
+                4 + j,
+                line_others[2 - j],
+            )
+            for j in range(3)
+        ],
+    }
+
+    def input_back():
+        for d in (1, 2, 3):
+            remote(kv_land.at[d - 1], kv_land.at[d - 1], kv_sems, d - 1, links.plane[d]).wait_recv()
+        kv = kv_out[here].astype(f32)
+        for d in range(3):
+            kv = kv + kv_land[d].astype(f32)
+        for g in range(KVH):
+            d_key = kv[:, g * HDIM : (g + 1) * HDIM]
+            d_key = d_key * trig_ref[0] - pltpu.roll(d_key, HDIM // 2, 1) * trig_ref[1]
+            dqkv_ref[:, width + g * HDIM : width + (g + 1) * HDIM] = d_key.astype(bf16)
+        dqkv_ref[:, width + KVH * HDIM :] = kv[:, KVH * HDIM :].astype(bf16)
+        scoped((wqkv_hbm, x_hbm), input_body)
+        scoped((normed_hbm, attn_hbm), turn_body)
+
+    def turn_body(normed_ref, attn_ref):
+        normed_turned[...] = normed_ref[...].T
+        attn_turned[...] = attn_ref[...].T
+
+    def input_body(wqkv_buf, x_ref):
+        def tile(i, carry):
+            columns = pl.ds(pl.multiple_of(i * 256, 256), 256)
+            grad_input_ref[:, columns] = dot_f32(dqkv_ref[...], wqkv_buf[columns, :], ((1,), (1,)))
+            return carry
+
+        lax.fori_loop(0, width // 256, tile, 0)
+        x = x_ref[...].astype(f32)
+        inv = lax.rsqrt(jnp.mean(x * x, axis=1, keepdims=True) + epsilon)
+        unit = x * inv
+        part = grad_input_ref[...]
+        vec_send[1:2, :] = jnp.sum(part * unit, axis=0, keepdims=True)
+        scaled = part * gains_ref[1:2, :]
+        grad_input_ref[...] = dmid_ref[...] + inv * (
+            scaled - unit * jnp.mean(scaled * unit, axis=1, keepdims=True)
+        )
+        sums = jnp.sum(dqkv_ref[...].astype(f32), axis=0, keepdims=True)
+        vec_send[0:1, :] = sums[:, :width]
+        vec_send[3:4, 0 : 2 * KVH * HDIM] = sums[:, width:]
+        vec_send[3:4, 2 * KVH * HDIM :] = jnp.zeros((1, width - 2 * KVH * HDIM), f32)
+        vec_send[4:8, :] = jnp.zeros((4, width), f32)
+        vec_plane[here] = vec_send[...]
+        for copy in vec_copies["plane"]:
+            copy.start()
+
+    shard = width // 4
+    half = shard // 2
+    qkv_width = wqkv_hbm.shape[1]
+
+    def half_grad(t, which):
+        at = pl.ds(pl.multiple_of(t * shard + which * half, half), half)
+        return (
+            dot_f32(normed_turned[at, :], dqkv_ref[...]).astype(bf16),
+            dot_f32(attn_turned[at, :], branch_ref[...]).astype(bf16),
+        )
+
+    half_sends = [remote(half_buf.at[t], attn_core.at[t], half_sems, t, links.partner) for t in range(4)]
+
+    def other_half():
+        def one(t, carry):
+            left, right = half_grad(t, 1 - core)
+            half_buf[t, :, :qkv_width] = left
+            half_buf[t, :, qkv_width:] = right
+            return carry
+
+        lax.fori_loop(0, 4, one, 0)
+        for copy in half_sends:
+            copy.start()
+        for copy in vec_comes["plane"]:
+            copy.wait_recv()
+        vec_core[core] = vec_plane[0] + vec_plane[1] + vec_plane[2] + vec_plane[3]
+        vec_copies["core"][0].start()
+
+    quarter = half // 2
+    near_x, near_y, far = links.near[1:]
+
+    def own_half():
+        for copy in half_sends:
+            copy.wait_send()
+        for t in range(4):
+            remote(attn_core.at[t], attn_core.at[t], half_sems, t, links.partner).wait_recv()
+            load = pltpu.make_async_copy(attn_core.at[t], half_load, local_sems.at[3])
+            load.start()
+            left, right = half_grad(t, core)
+            load.wait()
+            half_buf[t, :, :qkv_width] = (left.astype(f32) + half_load[:, :qkv_width].astype(f32)).astype(bf16)
+            half_buf[t, :, qkv_width:] = (right.astype(f32) + half_load[:, qkv_width:].astype(f32)).astype(bf16)
+        for copy in first_sends:
+            copy.start()
+        vec_comes["core"][0].wait_recv()
+        vec_line[line] = vec_core[0] + vec_core[1]
+        for copy in vec_copies["line"]:
+            copy.start()
+
+    low_rows, high_rows = pl.ds(0, quarter), pl.ds(quarter, quarter)
+    first_sends = [
+        remote(half_buf.at[near_y, low_rows], plane_first.at[0], plane_sems, 0, links.plane[2]),
+        remote(half_buf.at[far, low_rows], plane_first.at[1], plane_sems, 1, links.plane[2]),
+        remote(half_buf.at[near_x, high_rows], plane_first.at[2], plane_sems, 2, links.plane[1]),
+        remote(half_buf.at[far, high_rows], plane_first.at[3], plane_sems, 3, links.plane[1]),
+    ]
+    second_sends = [
+        remote(plane_send.at[0], plane_second.at[0], plane_sems, 4, links.plane[1]),
+        remote(plane_send.at[1], plane_second.at[1], plane_sems, 5, links.plane[2]),
+    ]
+
+    def plane_turn():
+        for copy in first_sends:
+            copy.wait_recv()
+        plane_send[0] = (half_buf[near_x, 0:quarter].astype(f32) + plane_first[1].astype(f32)).astype(bf16)
+        plane_send[1] = (
+            half_buf[near_y, quarter : 2 * quarter].astype(f32) + plane_first[3].astype(f32)
+        ).astype(bf16)
+        for copy in second_sends:
+            copy.start()
+
+    def plane_end():
+        for copy in second_sends + first_sends:
+            copy.wait_send()
+        for copy in second_sends:
+            copy.wait_recv()
+        for i in range(2):
+            at = slice(i * quarter, (i + 1) * quarter)
+            half_load[at, :] = (
+                half_buf[here, at].astype(f32)
+                + plane_first[2 * i].astype(f32)
+                + plane_second[i].astype(f32)
+            ).astype(bf16)
+        store = pltpu.make_async_copy(half_load, attn_own, local_sems.at[3])
+        store.start()
+        for copy in vec_comes["line"]:
+            copy.wait_recv()
+        sums_ref[...] = vec_line[0] + vec_line[1] + vec_line[2] + vec_line[3]
+        store.wait()
+
+    def heads(lo, hi):
+        return lambda: lax.fori_loop(lo, hi, head_back, 0)
+
+    chain = [
+        norm_back,
+        attn_back,
+        heads(0, 2),
+        heads(2, 4),
+        heads(4, 6),
+        heads(6, 8),
+        heads(8, 10),
+        heads(10, 12),
+        kv_send,
+        input_back,
+        other_half,
+        own_half,
+        None,
+        plane_turn,
+        None,
+        plane_end,
+    ]
+    for n in range(len(pairs) + 8):
+        service(n)
+        if n < len(chain) and chain[n] is not None:
+            chain[n]()
+
+    for swap in swaps + kv_sends + mlp_sends:
+        swap.wait_send()
+    for copy in mlp_sends:
+        copy.wait_recv()
+    for name in vec_copies:
+        for copy in vec_copies[name]:
+            copy.wait_send()
+    streams = (down, gate, up, attn)
+
+    @pl.when(is_end)
+    def _():
+        for s in streams:
+            s.close_end()
+
+    @pl.when(is_mid)
+    def _():
+        for s in streams:
+            s.close_mid()
+
+    for s in streams:
+        s.close_core()
+
+
+def epilogue(
+    lengths, starts, query, lse, trig, gains, x, cot, mid, part, normed, attn, mlp, kv, wqkv, wo, downs, gates, ups
+):
+    rows, width = x.shape
+    bf16, f32 = jnp.bfloat16, jnp.float32
+    any_space = pl.BlockSpec(memory_space=pl.ANY)
+    vmem = pl.BlockSpec(memory_space=pltpu.VMEM)
+    smem = pl.BlockSpec(memory_space=pltpu.SMEM)
+    shape = jax.ShapeDtypeStruct
+    wide = wqkv.shape[1] + width
+    half = width // 8
+    down_half = downs.shape[1]
+    cols = gates.shape[3]
+    down_size, gu_size, attn_size = 80, 16, 32
+    down_pairs = down_half // (2 * down_size)
+    gu_pairs = half // (2 * gu_size)
+    attn_pairs = half // (2 * attn_size)
+    down_chunk = (down_size, width)
+    gu_chunk = (4, gu_size, cols)
+    attn_chunk = (attn_size, wide)
+
+    def line_buffers(pairs, chunk):
+        return [shape((pairs, 2) + chunk, bf16), shape((pairs,) + chunk, bf16)]
+
+    def sems(*n):
+        return pltpu.SemaphoreType.DMA((2,) + n)
+
+    outs = [
+        shape((rows, width), f32),
+        shape((8, width), f32),
+        shape((2, down_half, width), bf16),
+        shape((2, 4, half, cols), bf16),
+        shape((2, 4, half, cols), bf16),
+        shape((2, half, wide), bf16),
+        shape((down_half, width), bf16),
+        shape((4, half, cols), bf16),
+        shape((4, half, cols), bf16),
+        shape((4, half, wide), bf16),
+        shape((half, wide), bf16),
+        shape((3, rows, width), bf16),
+    ]
+    outs += line_buffers(down_pairs, down_chunk)
+    outs += line_buffers(gu_pairs, gu_chunk) + line_buffers(gu_pairs, gu_chunk)
+    outs += line_buffers(attn_pairs, attn_chunk)
+    return pl.pallas_call(
+        epilogue_kernel,
+        name="epilogue",
+        out_shape=tuple(outs),
+        in_specs=[smem] * 2 + [vmem] * 4 + [any_space] * 13,
+        out_specs=[vmem] * 2 + [any_space] * (len(outs) - 2),
+        scratch_shapes=[
+            pltpu.VMEM((4, rows, 4 * HDIM), bf16),
+            pltpu.VMEM((KVH, HDIM, 4 * rows), bf16),
+            pltpu.VMEM((4 * rows, rows), f32),
+            pltpu.VMEM((HDIM, rows), f32),
+            pltpu.VMEM((rows, width), f32),
+            pltpu.VMEM((rows, width), bf16),
+            pltpu.VMEM((rows, width), bf16),
+            pltpu.VMEM((rows, wqkv.shape[1]), bf16),
+            pltpu.VMEM((KVH, 4 * rows, HDIM), f32),
+            pltpu.VMEM((KVH, 4 * rows, HDIM), f32),
+            pltpu.VMEM((4, rows, 4 * HDIM), bf16),
+            pltpu.VMEM((3, rows, 4 * HDIM), bf16),
+            pltpu.VMEM((width, rows), bf16),
+            pltpu.VMEM((width, rows), bf16),
+            pltpu.VMEM((4, half, wide), bf16),
+            pltpu.VMEM((half, wide), bf16),
+            pltpu.VMEM((4, half // 2, wide), bf16),
+            pltpu.VMEM((2, half // 2, wide), bf16),
+            pltpu.VMEM((2, half // 2, wide), bf16),
+            pltpu.VMEM((4, 8, width), f32),
+            pltpu.VMEM((2, 8, width), f32),
+            pltpu.VMEM((4, 8, width), f32),
+            pltpu.VMEM((8, width), f32),
+            pltpu.VMEM((4,) + down_chunk, bf16),
+            pltpu.VMEM((2, 2) + down_chunk, bf16),
+            pltpu.VMEM((4,) + gu_chunk, bf16),
+            pltpu.VMEM((2, 2) + gu_chunk, bf16),
+            pltpu.VMEM((2, 2) + gu_chunk, bf16),
+            pltpu.VMEM((4,) + attn_chunk, bf16),
+            pltpu.VMEM((2, 2) + attn_chunk, bf16),
+            pltpu.SemaphoreType.DMA((4,)),
+            pltpu.SemaphoreType.DMA((4,)),
+            sems(3),
+            pltpu.SemaphoreType.DMA((8,)),
+            sems(3),
+            sems(3),
+            sems(4),
+            sems(6),
+            sems(7),
+            sems(down_pairs, 11),
+            sems(gu_pairs, 11),
+            sems(gu_pairs, 11),
+            sems(attn_pairs, 11),
+        ],
+        compiler_params=pltpu.CompilerParams(
+            collective_id=1, has_side_effects=True, vmem_limit_bytes=63 * 2**20
+        ),
+    )(lengths, starts, query, lse, trig, gains, x, cot, mid, part, normed, attn, mlp, kv, wqkv, wo, downs, gates, ups)
+
+
 def local(
     hidden_in,
     out_grad,
@@ -1032,37 +1791,6 @@
         w_output,
         pieces,
     )
-    query_full = wqkv_full[:, :model_width]
-    key_full = wqkv_full[:, model_width : model_width + kv_width]
-    value_full = wqkv_full[:, model_width + kv_width :]
-    cosine = trig[0]
-    sine = trig[1] * jnp.where(jnp.arange(HDIM) < HDIM // 2, -1.0, 1.0)
-    local_pos = here * tok_rows + jnp.arange(tok_rows, dtype=jnp.int32)
-    query_doc, query_rel, query_piece = row_layout(local_pos, lengths, starts, PIECE)
-    key_doc, unused_rel, key_piece = row_layout(row_pos, lengths, starts, PIECE)
-    allowed = visible_pairs(query_doc, local_pos, query_piece, key_doc, row_pos, key_piece)
-    x_float = hidden_in.astype(jnp.float32)
-    inv_first = lax.rsqrt(jnp.mean(x_float * x_float, axis=1, keepdims=True) + epsilon)
-    unit_first = x_float * inv_first
-    gain_first = gains[1]
-    gain_second = gains[2]
-    inv_second = lax.rsqrt(jnp.mean(mid_state * mid_state, axis=1, keepdims=True) + epsilon)
-    unit_second = mid_state * inv_second
-    kv_rows = kv_full.reshape(row_len, 2 * kv_width)
-    query_grouped = query_rot.reshape(tok_rows, KVH, group_size, HDIM)
-    keys_grouped = kv_rows[:, :kv_width].reshape(row_len, KVH, HDIM)
-    values_grouped = kv_rows[:, kv_width:].reshape(row_len, KVH, HDIM)
-    log_total = lse[:, :HEADS].T.reshape(KVH, group_size, tok_rows, 1)
-
-    def masked_scores():
-        raw_scores = (
-            jnp.einsum(
-                "tgjd,rgd->gjtr", query_grouped, keys_grouped, preferred_element_type=jnp.float32
-            )
-            * score_scale
-        )
-        return jnp.where(allowed[None, None], raw_scores, -1e30)
-
     def whole(which, weight):
         mine = lax.dynamic_slice_in_dim(weight, here * part, part, 1)
         other = wgu[:, :, :, which].transpose(2, 0, 1, 3, 4).reshape(
@@ -1073,7 +1801,6 @@
 
     gate_part = whole(0, w_gate)
     up_part = whole(1, w_up)
-    cot_float = out_grad.astype(jnp.float32)
     cot_all = cot_all.reshape(row_len, model_width)
     normed_all = normed_all.reshape(row_len, model_width)
     gate_val = mat_dot(normed_all, gate_part)
@@ -1084,156 +1811,69 @@
     d_act = dot_right_t(cot_all, w_down)
     d_gate = (d_act * up_val * sig_gate * (1.0 + gate_val * (1.0 - sig_gate))).astype(low)
     d_up = (d_act * silu_gate).astype(low)
-    mlp_part = mat_dot(act_low, w_down).reshape(shard_count, tok_rows, model_width)
-    mlp_out = scatter_relative([pick(mlp_part, here ^ d) for d in range(shard_count)], "fsdp")
-    norm_part = (dot_right_t(d_gate, gate_part) + dot_right_t(d_up, up_part)).reshape(
-        shard_count, tok_rows, model_width
-    )
+    norm_part = (dot_right_t(d_gate, gate_part) + dot_right_t(d_up, up_part)).astype(low)
+    norm_part, act_low, d_gate, d_up = lax.optimization_barrier((norm_part, act_low, d_gate, d_up))
+    norm_part = norm_part.reshape(shard_count, tok_rows, model_width)
     partial_value = scatter_relative([pick(norm_part, here ^ d) for d in range(shard_count)], "fsdp")
-
-    def keep_half(grad):
-        mine = lax.dynamic_index_in_dim(grad, core, 1, keepdims=False)
-        other = lax.dynamic_index_in_dim(grad, 1 - core, 1, keepdims=False)
-        return (mine.astype(jnp.float32) + core_swap(other).astype(jnp.float32)).astype(low)
-
-    def both_cores(half):
-        return core_halves(half, core_swap(half), core)
-
-    down_grad = dot_left_t(act_low, cot_all).astype(low)
-    half = part // 2
-    down_half = keep_half(down_grad.reshape(1, 2, half, model_width))[0]
-    wide = model_width // line
-    down_parts = jnp.stack([down_half[:, q * wide : (q + 1) * wide] for q in range(line)])
-    down_own = line_scatter(down_parts).astype(low)
-    down_rows = line_gather(down_own)
-    down_rows = jnp.concatenate([down_rows[q] for q in range(line)], axis=1)
-    down_sums = both_cores(down_rows).reshape(part, model_width).astype(jnp.float32)
-
-    rows = model_width // shard_count
-    thin = rows // 2 // line
-
-    def column_grad(d_value):
-        grad = dot_left_t(normed_all, d_value).astype(low)
-        kept = keep_half(grad.reshape(shard_count, 2, rows // 2, part))
-        kept = kept.reshape(shard_count, line, thin, part).transpose(1, 0, 2, 3)
-        own = line_scatter(kept).astype(low)
-        got = []
-        for d in range(shard_count):
-            piece = pick(own, here ^ d)
-            got.append(piece if d == 0 else lax.ppermute(piece, "fsdp", xor_pairs(shard_count, d)))
-        got = place(got, here).transpose(1, 0, 2).reshape(thin, ff_width)
-        full = line_gather(got).reshape(rows // 2, ff_width)
-        return both_cores(full).reshape(rows, ff_width).astype(jnp.float32)
-
-    grad_gate = column_grad(d_gate)
-    grad_up = column_grad(d_up)
-    output = mid_state + mlp_out
-    d_gain_second = jnp.sum(partial_value * unit_second, axis=0)
-    scaled_second = partial_value * gain_second
-    d_mid = cot_float + inv_second * (
-        scaled_second - unit_second * jnp.mean(scaled_second * unit_second, axis=1, keepdims=True)
-    )
-    d_branch_low = d_mid.astype(jnp.bfloat16)
-    d_attn_low = dot_right_t(d_branch_low, output_full).astype(jnp.bfloat16)
-    d_attn_grouped = d_attn_low.reshape(tok_rows, KVH, group_size, HDIM)
-    scores = masked_scores()
-    soft_back = jnp.exp(scores - log_total)
-    probs_low = soft_back.astype(jnp.bfloat16)
-    prob_grad = jnp.einsum(
-        "tgjd,rgd->gjtr", d_attn_grouped, values_grouped, preferred_element_type=jnp.float32
-    )
-    row_delta = jnp.sum(soft_back * prob_grad, axis=3, keepdims=True)
-    score_grad = (soft_back * (prob_grad - row_delta)).astype(jnp.bfloat16)
-    dquery_rot = (
-        jnp.einsum("gjtr,rgd->tgjd", score_grad, keys_grouped, preferred_element_type=jnp.float32)
-        * score_scale
-    )
-    dquery_low = (
-        unrotate(dquery_rot.reshape(tok_rows, HEADS, HDIM), cosine, sine)
-        .reshape(tok_rows, model_width)
-        .astype(jnp.bfloat16)
-    )
-    key_grad = (
-        jnp.einsum("gjtr,tgjd->rgd", score_grad, query_grouped, preferred_element_type=jnp.float32)
-        * score_scale
-    )
-    value_grad = jnp.einsum(
-        "gjtr,tgjd->rgd", probs_low, d_attn_grouped, preferred_element_type=jnp.float32
-    )
-    kv_sums = lax.psum_scatter(
-        jnp.concatenate(
-            [
-                key_grad.reshape(lax.axis_size("fsdp") * tok_rows, kv_width),
-                value_grad.reshape(lax.axis_size("fsdp") * tok_rows, kv_width),
-            ],
-            axis=1,
-        ).astype(jnp.bfloat16),
-        "fsdp",
-        scatter_dimension=0,
-        tiled=True,
-    ).astype(jnp.float32)
-    dkey_low = (
-        unrotate(kv_sums[:, :kv_width].reshape(tok_rows, KVH, HDIM), cosine, sine)
-        .reshape(tok_rows, kv_width)
-        .astype(jnp.bfloat16)
-    )
-    dvalue_low = kv_sums[:, kv_width:].astype(jnp.bfloat16)
-    d_norm_first = (
-        dot_right_t(dquery_low, query_full)
-        + dot_right_t(dkey_low, key_full)
-        + dot_right_t(dvalue_low, value_full)
-    )
-    attn_grads = jnp.concatenate(
-        [
-            dot_left_t(normed_first, dquery_low).astype(low),
-            dot_left_t(normed_first, dkey_low).astype(low),
-            dot_left_t(normed_first, dvalue_low).astype(low),
-            dot_left_t(attn_low, d_branch_low).astype(low),
-        ],
-        axis=1,
-    )
-    attn_wide = attn_grads.shape[1]
-    attn_kept = keep_half(attn_grads.reshape(shard_count, 2, rows // 2, attn_wide))
-    attn_own = scatter_relative([pick(attn_kept, here ^ d) for d in range(shard_count)], "fsdp").astype(low)
-    attn_own = line_scatter(attn_own.reshape(line, thin, attn_wide)).astype(low)
-    attn_rows = line_gather(attn_own).reshape(rows // 2, attn_wide)
-    attn_sums = both_cores(attn_rows).reshape(rows, attn_wide).astype(jnp.float32)
-    d_gain_first = jnp.sum(d_norm_first * unit_first, axis=0)
-    scaled_first = d_norm_first * gain_first
-    grad_input = d_mid + inv_first * (
-        scaled_first - unit_first * jnp.mean(scaled_first * unit_first, axis=1, keepdims=True)
-    )
-    bias_query = jnp.sum(dquery_low.astype(jnp.float32), axis=0)
-    bias_key = jnp.sum(dkey_low.astype(jnp.float32), axis=0)
-    bias_value = jnp.sum(dvalue_low.astype(jnp.float32), axis=0)
-    small = (bias_query, bias_key, bias_value, d_gain_first, d_gain_second)
-    summed = lax.psum(jnp.concatenate(small), ("rep", "fsdp"))
-    outs = []
-    at = 0
-    for vector in small:
-        size = vector.shape[0] // shard_count
-        outs.append(lax.dynamic_slice_in_dim(summed, at + here * size, size, 0))
-        at += vector.shape[0]
-    bias_query, bias_key, bias_value, gain_first_sum, gain_second_sum = outs
-    grad_query = attn_sums[:, :model_width]
-    grad_key = attn_sums[:, model_width : model_width + kv_width]
-    grad_value = attn_sums[:, model_width + kv_width : model_width + 2 * kv_width]
-    grad_output = attn_sums[:, model_width + 2 * kv_width :]
+    down_part = dot_left_t(act_low, cot_all).astype(low).reshape(2, part // 2, model_width)
+    gate_grads = [
+        dot_left_t(normed_all, d_value).astype(low).reshape(shard_count, 2, shard_rows // 2, part)
+        for d_value in (d_gate, d_up)
+    ]
+    mlp_part = mat_dot(act_low, w_down).astype(low).reshape(shard_count, tok_rows, model_width)
+    results = epilogue(
+        doc_lengths,
+        piece_starts,
+        query_rot,
+        lse,
+        trig,
+        gains,
+        hidden_in,
+        out_grad,
+        mid_state,
+        partial_value,
+        normed_first,
+        attn_low,
+        mlp_part,
+        kv_full,
+        wqkv_full,
+        output_full,
+        down_part,
+        gate_grads[0],
+        gate_grads[1],
+    )
+    grad_input, sums, down_final, gate_final, up_final, attn_final = results[:6]
+    mlp_land = results[11]
+    output = mid_state + pick(mlp_part, here).astype(jnp.float32)
+    for d in range(shard_count - 1):
+        output = output + mlp_land[d].astype(jnp.float32)
+    down_sums = down_final.reshape(part, model_width).astype(jnp.float32)
+    grad_gate, grad_up = (
+        final.transpose(0, 2, 1, 3).reshape(shard_rows, ff_width).astype(jnp.float32)
+        for final in (gate_final, up_final)
+    )
+    attn_sums = attn_final.reshape(shard_rows, -1).astype(jnp.float32)
+    ends = [0, model_width, model_width + kv_width, model_width + 2 * kv_width, 2 * (model_width + kv_width)]
+    grad_query, grad_key, grad_value, grad_output = (attn_sums[:, ends[i] : ends[i + 1]] for i in range(4))
+
+    def shard_of(row, first, size):
+        return lax.dynamic_slice(sums, (row, first + here * (size // shard_count)), (1, size // shard_count))[0]
+
     return (
         output,
         grad_input,
         grad_query,
-        bias_query,
+        shard_of(0, 0, model_width),
         grad_key,
-        bias_key,
+        shard_of(3, 0, kv_width),
         grad_value,
-        bias_value,
+        shard_of(3, kv_width, kv_width),
         grad_output,
-        gain_first_sum,
+        shard_of(1, 0, model_width),
         grad_gate,
         grad_up,
         down_sums,
-        gain_second_sum,
+        shard_of(2, 0, model_width),
     )
 
 

time: 1240 us -> 843 us (0.68)
  Pallas kernels: 185 us -> 521 us
  waiting for transfers between devices: 281 us -> 0.02 us
  starting transfers between devices: 185 us -> 6.94 us
  other arithmetic: 135 us -> 44.9 us
  matrix products: 210 us -> 133 us
  local copies, waits for them, and re-layouts: 172 us -> 124 us
  blocking collectives: 37.4 us -> 0 us
  between operations: 16.7 us -> 1.57 us
    pallas_call x0 -> x1, Pallas kernels: none -> 343 us  [epilogue(): pl.pallas_call(epilogue_kernel, name='epilogue', out_shape=tuple(outs), i...]
    ppermute x62 -> x0, waiting for transfers between devices: 204 us -> none  [the longest x12 118 us: line_gather(): lax.ppermute(above[-1], 'rep', line_pairs(range(1, count - step + 1), -1))]
    ppermute x62 -> x0, starting transfers between devices: 165 us -> none  [the longest x12 70.5 us: line_scatter(): lax.ppermute(sends[0], 'rep', line_pairs(range(step), 1))]
    ppermute x18 -> x6, waiting for transfers between devices: 77.5 us -> 0.02 us  [scatter_relative(): lax.ppermute(have[d].astype(jnp.bfloat16), axis, xor_pairs(count, bit))]
    convert_element_type x7 -> x6, local copies, waits for them, and re-layouts: 27.1 us -> 86.8 us  [the longest x4 66.5 us: local_fast(): final.transpose(0, 2, 1, 3).reshape(shard_rows, ff_width)]
    dot_general x5 -> x0, matrix products: 49.7 us -> none  [the longest x1 17.9 us: masked_scores(): jnp.einsum('tgjd,rgd->gjtr', query_grouped, keys_grouped, preferred_eleme...]
    unnamed x200 -> x53, local copies, waits for them, and re-layouts: 45.7 us -> 1.54 us
    convert_element_type x25 -> x4, other arithmetic: 58.4 us -> 18.6 us  [the longest x2 8.55 us: local_fast(): final.transpose(0, 2, 1, 3).reshape(shard_rows, ff_width)]
  transfers between devices with their start and end apart: 81 -> 6, of which waited for: 26 -> 0; matrix products, arithmetic and copies ran while one was open for 30% -> 8% of each run, Pallas kernels for 0% -> 0%
where the time goes in v3:
time: 843 us; the launch traced here: 831 us
  Pallas kernels  521 us (62%)
  matrix products  133 us (16%)
  local copies, waits for them, and re-layouts  124 us (15%)
  other arithmetic  44.9 us (5%)
    pallas_call x1, Pallas kernels, epilogue(): pl.pallas_call(epilogue_kernel, name='epilogue', out_shape=tuple(outs), i...  343 us
    pallas_call x1, Pallas kernels, prologue(): pl.pallas_call(prologue_kernel, name='prologue', out_shape=(shape((shards...  178 us
    convert_element_type x4, local copies, waits for them, and re-layouts, local_fast(): final.transpose(0, 2, 1, 3).reshape(shard_rows, ff_width)  66.5 us
    dot_general x3, matrix products, mat_dot(): return jnp.dot(left, right, preferred_element_type=jnp.float32)  52.3 us
    dot_general x3, matrix products, dot_right_t(): lax.dot_general(left, right, (((1,), (1,)), ((), ())), preferred_element_...  43.3 us
    dot_general x3, matrix products, dot_left_t(): lax.dot_general(left, right, (((0,), (0,)), ((), ())), preferred_element_...  37.2 us
    convert_element_type x2, local copies, waits for them, and re-layouts, local_fast(): dot_left_t(normed_all, d_value).astype(low)  20.4 us
  transfers between devices with their start and end apart: 6, of which 0 were waited for; matrix products, arithmetic and copies ran while one was open for 8% of the time, Pallas kernels for 0%

profile of v3, /device:TPU:0, one launch (start us, length us, event | category | flops | bytes accessed | tf_op | source)
XLA Modules:
  0.0 831.5 jit_solution(13070932622761713081)
XLA Ops:
  0.7 0.7 bitcast_convert_fusion.2
  1.4 0.6 pad_maximum_fusion.7
  1.9 0.7 broadcast_in_dim.51
  2.6 0.7 broadcast_in_dim.52
  3.3 0.7 broadcast_in_dim.53
  4.0 0.1 dynamic_update_slice.20
  4.1 0.7 fusion.7
  5.0 0.6 broadcast.10.clone
  5.6 0.6 constant_dynamic-update-slice_fusion.2
  6.2 3.6 dynamic-slice_bitcast_fusion
  9.8 2.1 dynamic-slice_bitcast_fusion.13
  11.9 0.1 maximum_bitcast_fusion.1
  12.1 0.1 maximum_bitcast_fusion
  12.2 1.4 pad_maximum_fusion.5.gu_ref
  13.6 1.3 pad_maximum_fusion.6.wqkv_ref
  14.9 0.6 broadcast_in_dim.49
  15.5 1.4 concatenate.12.vec_ref
  17.0 1.2 broadcast_in_dim.50.inverse_ref
  18.2 178.4 %prologue.1 = (bf16[4,320,1536]{2,1,0:T(8,128)(2,1)}, bf16[4,320,1536]{2,1,0:T(8,128)(2,1)}, bf16[2,4,3,2,48,2240]{5,4,3,2,1,0:T(8,128)(2,1)}, bf16[1536,2048]{1...) custom-call(s32[1,8]{1,0:T(1,128)} %lengths_ref.3, ...), custom_call_target="tpu_custom_call" | custom-call | tf_op jit(solution)/shard_map/prologue/pallas_call | solution.py:605
  196.6 9.1 %slice_bitcast_fusion.1 = (bf16[3,2,4,48,2240]{4,3,0,2,1:T(8,128)(2,1)}, bf16[3,2,4,48,2240]{4,3,0,2,1:T(8,128)(2,1)}) fusion(bf16[2,4,3,2,48,2240]{5,4,3,2,1,0:T(8,128)(2,1)} %get-tuple-element.41), kind=kLoop, calls=%fused_computation.19 | loop fusion | bytes 20643840 | tf_op jit(solution)/shard_map/transpose | solution.py:1796
  205.7 5.2 fusion.10
  210.9 2.5 fusion.11
  213.4 4.3 pad_maximum_fusion
  217.7 1.2 pad_maximum_fusion.2
  218.9 0.5 constant_dynamic-slice_fusion.8
  219.4 1.7 constant_dynamic-slice_fusion.4
  221.1 2.8 pad_maximum_fusion.3
  223.8 17.0 %fusion.13 = f32[1280,2240]{0,1:T(8,128)} fusion(bf16[1280,1536]{1,0:T(8,128)(2,1)} %bitcast.150, bf16[1536,2240]{1,0:T(8,128)(2,1)S(1)} %bitcast.129), kind=kOutput, calls=%fused_computation.83 | convolution fusion | flops 8808038400 | bytes 22282240 | tf_op jit(solution)/shard_map/dot_general | solution.py:60
  240.9 15.0 %fusion.12 = f32[1280,2240]{0,1:T(8,128)} fusion(bf16[1280,1536]{1,0:T(8,128)(2,1)} %bitcast.154, bf16[2240,1536]{1,0:T(8,128)(2,1)} %param.30), kind=kOutput, calls=%fused_computation.82 | convolution fusion | flops 8808038400 | bytes 22282240 | tf_op jit(solution)/shard_map/dot_general | solution.py:64
  255.9 3.5 pad_maximum_fusion.1
  259.3 23.7 %multiply_convert_fusion = (bf16[1280,2240]{0,1:T(8,128)(2,1)}, bf16[1280,2240]{0,1:T(8,128)(2,1)}, bf16[1280,2240]{0,1:T(8,128)(2,1)}) fusion(f32[1280,2240]{0,1:T(8,128)} %fusion.13, f32[1280,2240]{0,1:T(8,128)} %fusion.12, bf16[1280,1536]{1,0:T(8,128)(2,1)} %bitcast.151, bf16[1536,2240]{1,0:T(8,128)(2,1)} %bitcast.131), kind=kOutput, calls=%fused_computation.2 | convolution fusion | flops 8851046400 | bytes 50954240 | tf_op jit(solution)/shard_map/dot_general | solution.py:60
  283.1 15.5 %fusion.14 = f32[1280,1536]{1,0:T(8,128)} fusion(bf16[1280,2240]{0,1:T(8,128)(2,1)} %get-tuple-element.53, bf16[1536,2240]{1,0:T(8,128)(2,1)} %bitcast.130), kind=kOutput, calls=%fused_computation.84 | convolution fusion | flops 8808038400 | bytes 20480000 | tf_op jit(solution)/shard_map/dot_general | solution.py:64
  298.6 12.8 %fusion.1 = bf16[1280,1536]{1,0:T(8,128)(2,1)S(1)} fusion(f32[1280,1536]{1,0:T(8,128)} %fusion.14, bf16[1280,2240]{0,1:T(8,128)(2,1)} %get-tuple-element.54, bf16[1536,2240]{1,0:T(8,128)(2,1)S(1)} %bitcast.132), kind=kOutput, calls=%fused_computation.11 | convolution fusion | flops 8811970560 | bytes 24412160 | tf_op jit(solution)/shard_map/dot_general | solution.py:64
  311.4 0.2 dynamic-slice_bitcast_fusion.8
  311.5 2.2 collective-permute-start
  313.8 2.0 collective-permute-start.4
  315.7 0.1 collective-permute-start.3
  315.8 14.2 %convolution_convert_fusion.2 = bf16[2240,1536]{1,0:T(8,128)(2,1)} fusion(bf16[1280,2240]{0,1:T(8,128)(2,1)} %get-tuple-element.42, bf16[1280,1536]{1,0:T(8,128)(2,1)} %bitcast.155), kind=kOutput, calls=%fused_computation.9 | convolution fusion | flops 8811479040 | bytes 16547840 | tf_op jit(solution)/shard_map/dot_general | solution.py:70
  330.0 11.5 %convolution_convert_fusion.1 = bf16[1536,2240]{0,1:T(8,128)(2,1)} fusion(bf16[1280,2240]{0,1:T(8,128)(2,1)S(1)} %bitcast.159, bf16[1280,1536]{1,0:T(8,128)(2,1)S(1)} %bitcast.152), kind=kOutput, calls=%fused_computation.8 | convolution fusion | flops 8811479040 | bytes 16547840 | tf_op jit(solution)/shard_map/dot_general | solution.py:70
  341.5 0.1 fusion.4
  341.7 2.6 collective-permute-start.2
  344.3 11.6 %convolution_convert_fusion = bf16[1536,2240]{0,1:T(8,128)(2,1)} fusion(bf16[1280,2240]{0,1:T(8,128)(2,1)S(1)} %bitcast.161, bf16[1280,1536]{1,0:T(8,128)(2,1)S(1)} %bitcast.153), kind=kOutput, calls=%fused_computation.7 | convolution fusion | flops 8811479040 | bytes 16547840 | tf_op jit(solution)/shard_map/dot_general | solution.py:70
  355.9 1.1 fusion.5
  357.0 11.6 %convolution_convert_fusion.3 = bf16[1280,1536]{1,0:T(8,128)(2,1)} fusion(bf16[1280,2240]{0,1:T(8,128)(2,1)S(1)} %bitcast.157, bf16[2240,1536]{1,0:T(8,128)(2,1)S(1)} %bitcast.149), kind=kOutput, calls=%fused_computation.12 | convolution fusion | flops 8810004480 | bytes 16547840 | tf_op jit(solution)/shard_map/dot_general | solution.py:60
  368.6 10.2 %copy.33 = bf16[1536,2240]{1,0:T(8,128)(2,1)} copy(bf16[1536,2240]{0,1:T(8,128)(2,1)} %convolution_convert_fusion) | data formatting | bytes 13762560 | tf_op jit(solution)/shard_map/convert_element_type | solution.py:1820
  378.8 10.2 %copy.32 = bf16[1536,2240]{1,0:T(8,128)(2,1)} copy(bf16[1536,2240]{0,1:T(8,128)(2,1)} %convolution_convert_fusion.1) | data formatting | bytes 13762560 | tf_op jit(solution)/shard_map/convert_element_type | solution.py:1820
  389.0 1.2 fusion.3
  390.2 1.4 pad_maximum_fusion.4.part_hbm
  391.6 342.6 %epilogue.1 = (f32[320,1536]{1,0:T(8,128)}, f32[8,1536]{1,0:T(8,128)}, bf16[2,1120,1536]{2,1,0:T(8,128)(2,1)}, bf16[2,4,192,2240]{3,2,1,0:T(8,128)(2,1)}, bf16[2...) custom-call(s32[1,8]{1,0:T(1,128)} %lengths_ref.3, ...), custom_call_target="tpu_custom_call" | custom-call | tf_op jit(solution)/shard_map/epilogue/pallas_call | solution.py:1356
  734.2 1.3 dynamic-slice_bitcast_fusion.18
  735.5 1.5 dynamic-slice_reduce_fusion
  736.9 2.4 bitcast_convert_fusion.1
  739.4 0.9 fusion.9
  740.4 2.7 fusion.8
  743.1 0.2 copy-done.7
  743.2 3.9 convert_add_fusion
  747.1 7.6 bitcast_convert_fusion
  754.7 4.3 convert_bitcast_fusion.1
  759.0 16.0 %copy.34 = f32[2,192,4,2240]{3,2,1,0:T(4,128)} copy(f32[2,192,4,2240]{3,1,2,0:T(8,128)S(1)} %convert_bitcast_fusion.1) | data formatting | bytes 27525120 | tf_op jit(solution)/shard_map/convert_element_type | solution.py:1852
  775.0 17.3 %reshape.123 = f32[384,8960]{1,0:T(8,128)} reshape(f32[2,192,4,2240]{3,2,1,0:T(4,128)} %copy.34) | data formatting | bytes 27525120 | tf_op jit(solution)/shard_map/convert_element_type | solution.py:1852
  792.3 4.3 convert_bitcast_fusion
  796.5 15.7 %copy.35 = f32[2,192,4,2240]{3,2,1,0:T(4,128)} copy(f32[2,192,4,2240]{3,1,2,0:T(8,128)S(1)} %convert_bitcast_fusion) | data formatting | bytes 27525120 | tf_op jit(solution)/shard_map/convert_element_type | solution.py:1852
  812.3 17.4 %reshape.124 = f32[384,8960]{1,0:T(8,128)} reshape(f32[2,192,4,2240]{3,2,1,0:T(4,128)} %copy.35) | data formatting | bytes 27525120 | tf_op jit(solution)/shard_map/convert_element_type | solution.py:1852
  829.7 1.3 copy.42
  (72 shorter events, 0.4 us)
Async XLA Ops:
  5.0 0.6 copy-start.12
  9.8 3.8 copy-start.9
  9.8 3.7 copy-start.10
  9.8 3.7 copy-start.11
  205.7 5.2 slice-start
  205.7 5.2 slice-start.1
  213.4 4.3 copy-start.3
  213.4 4.3 copy-start.4
  213.4 4.3 copy-start.5
  223.8 17.0 %copy-start.1 = (bf16[4,384,2240]{2,1,0:T(8,128)(2,1)}, bf16[4,384,2240]{2,1,0:T(8,128)(2,1)S(1)}, u32[]{:S(2)}) copy-start(bf16[4,384,2240]{2,1,0:T(8,128)(2,1)S(1)} %pad_maximum_fusion.3) | copy-start | bytes 20643844
  283.1 15.5 %copy-start.2 = (bf16[4,384,2240]{2,1,0:T(8,128)(2,1)S(1)}, bf16[4,384,2240]{2,1,0:T(8,128)(2,1)}, u32[]{:S(2)}) copy-start(bf16[4,384,2240]{2,1,0:T(8,128)(2,1)} %pad_maximum_fusion.1) | copy-start | bytes 20643844
  311.4 44.5 %copy-start.6 = (bf16[1280,1536]{1,0:T(8,128)(2,1)}, bf16[1280,1536]{1,0:T(8,128)(2,1)S(1)}, u32[]{:S(2)}) copy-start(bf16[1280,1536]{1,0:T(8,128)(2,1)S(1)} %fusion.1) | copy-start | bytes 11796484
  311.5 44.3 %collective-permute-start = (bf16[160,1536]{1,0:T(8,128)(2,1)S(1)}, bf16[160,1536]{1,0:T(8,128)(2,1)S(1)}, u32[]{:S(2)}, u32[]{:S(2)}) collective-permute-start(bf16[160,1536]{1,0:T(8,128)(2,1)S(1)} %get-tuple-element.98), channel_id=1, source_target_pairs={{0,2},{1,3},{2,0},{3,1},{4,6},{5,7},{6,4},{7,5},{8,10},{9,11},{10,... | collective-permute-start | bytes 1474568 | tf_op jit(solution)/shard_map/ppermute | solution.py:109
  313.7 27.8 %collective-permute-start.1 = (bf16[160,1536]{1,0:T(8,128)(2,1)S(1)}, bf16[160,1536]{1,0:T(8,128)(2,1)S(1)}, u32[]{:S(2)}, u32[]{:S(2)}) collective-permute-start(bf16[160,1536]{1,0:T(8,128)(2,1)S(1)} %get-tuple-element.99), channel_id=1, source_target_pairs={{0,2},{1,3},{2,0},{3,1},{4,6},{5,7},{6,4},{7,5},{8,10},{9,11},{10,... | collective-permute-start | bytes 1474568 | tf_op jit(solution)/shard_map/ppermute | solution.py:109
  313.8 42.1 %collective-permute-start.4 = (bf16[160,1536]{1,0:T(8,128)(2,1)S(1)}, bf16[160,1536]{1,0:T(8,128)(2,1)S(1)}, u32[]{:S(2)}, u32[]{:S(2)}) collective-permute-start(bf16[160,1536]{1,0:T(8,128)(2,1)S(1)} %get-tuple-element.100), channel_id=1, source_target_pairs={{0,1},{1,0},{2,3},{3,2},{4,5},{5,4},{6,7},{7,6},{8,9},{9,8},{10,11... | collective-permute-start | bytes 1474568 | tf_op jit(solution)/shard_map/ppermute | solution.py:109
  315.7 14.3 %slice-start.8 = ((s8[5734400]{0:T(1024)(128)(4,1)}), s8[4194304]{0:T(1024)(128)(4,1)S(1)}, s32[]{:S(2)}) async-start(s8[5734400]{0:T(1024)(128)(4,1)} %bitcast.158), calls=%async_computation.8 | async-start | bytes 8388608
  315.7 14.3 %copy-start.13 = (bf16[4,320,1536]{2,1,0:T(8,128)(2,1)S(1)}, bf16[4,320,1536]{2,1,0:T(8,128)(2,1)}, u32[]{:S(2)}) copy-start(bf16[4,320,1536]{2,1,0:T(8,128)(2,1)} %get-tuple-element.40) | copy-start | bytes 11796484
  315.7 14.3 %slice-start.9 = ((s8[5734400]{0:T(1024)(128)(4,1)}), s8[1540096]{0:T(1024)(128)(4,1)S(1)}, s32[]{:S(2)}) async-start(s8[5734400]{0:T(1024)(128)(4,1)} %bitcast.158), calls=%async_computation.9 | async-start | bytes 3080192
  315.7 73.3 %collective-permute-start.3 = (bf16[160,1536]{1,0:T(8,128)(2,1)S(1)}, bf16[160,1536]{1,0:T(8,128)(2,1)S(1)}, u32[]{:S(2)}, u32[]{:S(2)}) collective-permute-start(bf16[160,1536]{1,0:T(8,128)(2,1)S(1)} %get-tuple-element.101), channel_id=1, source_target_pairs={{0,1},{1,0},{2,3},{3,2},{4,5},{5,4},{6,7},{7,6},{8,9},{9,8},{10,11... | collective-permute-start | bytes 1474568 | tf_op jit(solution)/shard_map/ppermute | solution.py:109
  315.8 28.5 %slice-start.10 = ((s8[5734400]{0:T(1024)(128)(4,1)}), s8[4194304]{0:T(1024)(128)(4,1)S(1)}, s32[]{:S(2)}) async-start(s8[5734400]{0:T(1024)(128)(4,1)} %bitcast.160), calls=%async_computation.10 | async-start | bytes 8388608
  330.0 14.3 %slice-start.11 = ((s8[5734400]{0:T(1024)(128)(4,1)}), s8[1540096]{0:T(1024)(128)(4,1)S(1)}, s32[]{:S(2)}) async-start(s8[5734400]{0:T(1024)(128)(4,1)} %bitcast.160), calls=%async_computation.11 | async-start | bytes 3080192
  341.5 15.5 %slice-start.4 = ((s8[6881280]{0:T(1024)(128)(4,1)}), s8[4194304]{0:T(1024)(128)(4,1)S(1)}, s32[]{:S(2)}) async-start(s8[6881280]{0:T(1024)(128)(4,1)} %bitcast.148), calls=%async_computation.4 | async-start | bytes 8388608
  341.5 15.5 %slice-start.6 = ((s8[5734400]{0:T(1024)(128)(4,1)}), s8[4194304]{0:T(1024)(128)(4,1)S(1)}, s32[]{:S(2)}) async-start(s8[5734400]{0:T(1024)(128)(4,1)} %bitcast.156), calls=%async_computation.6 | async-start | bytes 8388608
  341.7 15.4 %slice-start.5 = ((s8[6881280]{0:T(1024)(128)(4,1)}), s8[2686976]{0:T(1024)(128)(4,1)S(1)}, s32[]{:S(2)}) async-start(s8[6881280]{0:T(1024)(128)(4,1)} %bitcast.148), calls=%async_computation.5 | async-start | bytes 5373952
  341.7 15.3 %slice-start.7 = ((s8[5734400]{0:T(1024)(128)(4,1)}), s8[1540096]{0:T(1024)(128)(4,1)S(1)}, s32[]{:S(2)}) async-start(s8[5734400]{0:T(1024)(128)(4,1)} %bitcast.156), calls=%async_computation.7 | async-start | bytes 3080192
  341.7 14.2 %collective-permute-start.2 = (bf16[160,1536]{1,0:T(8,128)(2,1)S(1)}, bf16[160,1536]{1,0:T(8,128)(2,1)S(1)}, u32[]{:S(2)}, u32[]{:S(2)}) collective-permute-start(bf16[160,1536]{1,0:T(8,128)(2,1)S(1)} %fusion.4), channel_id=1, source_target_pairs={{0,1},{1,0},{2,3},{3,2},{4,5},{5,4},{6,7},{7,6},{8,9},{9,8},{10,11... | collective-permute-start | bytes 1474568 | tf_op jit(solution)/shard_map/ppermute | solution.py:109
  357.0 32.0 %collective-permute-start.5 = (bf16[160,1536]{1,0:T(8,128)(2,1)}, bf16[160,1536]{1,0:T(8,128)(2,1)S(1)}, u32[]{:S(2)}, u32[]{:S(2)}) collective-permute-start(bf16[160,1536]{1,0:T(8,128)(2,1)} %get-tuple-element.97), channel_id=1, source_target_pairs={{0,2},{1,3},{2,0},{3,1},{4,6},{5,7},{6,4},{7,5},{8,10},{9,11},{10,... | collective-permute-start | bytes 1474568 | tf_op jit(solution)/shard_map/ppermute | solution.py:109
  739.4 3.7 copy-start
  739.4 3.8 copy-start.7
  739.4 7.7 slice-start.2
  740.4 6.7 slice-start.3
  812.3 17.4 %copy-start.8 = (f32[320,1536]{1,0:T(8,128)S(1)}, f32[320,1536]{1,0:T(8,128)}, u32[]{:S(2)}) copy-start(f32[320,1536]{1,0:T(8,128)} %get-tuple-element.125) | copy-start | bytes 5898244

commit v4 on v3

--- a/solution.py
+++ b/solution.py
@@ -290,10 +290,12 @@
     inverse_ref,
     wqkv_ref,
     wo_ref,
-    gu_ref,
+    gate_ref,
+    up_ref,
     normed_all,
     cot_all,
     wgu,
+    own_gu,
     wqkv_full,
     wo_full,
     kv_full,
@@ -310,6 +312,11 @@
     kv_buf,
     normed_buf,
     bias_ref,
+    thin_buf,
+    gu_ref,
+    wide_buf,
+    own_buf,
+    cut_sems,
     local_sems,
     vec_sems,
     qkv_sems,
@@ -430,9 +437,22 @@
                 hop.recv.wait_recv()
                 hop.swap.start()
 
-    for copy in vec_sends:
+    thin, part = gu_ref.shape[2:]
+    first_row = pl.multiple_of(core * half + line * thin, thin)
+    cuts = [
+        pltpu.make_async_copy(ref.at[pl.ds(first_row, thin)], thin_buf.at[i], cut_sems.at[i])
+        for i, ref in enumerate((gate_ref, up_ref))
+    ] + [
+        pltpu.make_async_copy(ref, wide_buf.at[i], cut_sems.at[2 + i])
+        for i, ref in enumerate((gate_ref, up_ref))
+    ]
+    for copy in vec_sends + cuts:
         copy.start()
     qkv_gather.start()
+    for copy in cuts[:2]:
+        copy.wait()
+    for t in range(4):
+        gu_ref[t] = thin_buf[:, :, t * part : (t + 1) * part]
     for copy in gu_sends:
         copy.start()
     for copy in own_copies:
@@ -505,6 +525,16 @@
         return carry
 
     lax.fori_loop(0, HEADS // 2, query_pair, 0)
+    for copy in cuts[2:]:
+        copy.wait()
+    for t in range(4):
+
+        @pl.when(here == t)
+        def _():
+            own_buf[...] = wide_buf[:, :, t * part : (t + 1) * part]
+
+    own_store = pltpu.make_async_copy(own_buf, own_gu, cut_sems.at[0])
+    own_store.start()
     wo_gather.hand_on()
     for swap in wo_swaps[:2]:
         swap.start()
@@ -567,6 +597,7 @@
     norm_gather.finish()
 
     own_copies[2].wait()
+    own_store.wait()
     full_copy.wait()
     kv_copy.wait()
     wo_copy.wait()
@@ -588,11 +619,12 @@
                 hop.swap_come.wait_recv()
 
 
-def prologue(lengths, starts, x, cot, vec, inverse, wqkv, wo, pieces):
+def prologue(lengths, starts, x, cot, vec, inverse, wqkv, wo, gate, up):
     rows, width = x.shape
     shards = lax.axis_size("fsdp")
     count = lax.axis_size("rep") // 2
-    thin, part = pieces.shape[2:]
+    shard = gate.shape[0]
+    thin, part = shard // (2 * count), gate.shape[1] // shards
     bf16, f32 = jnp.bfloat16, jnp.float32
     any_space = pl.BlockSpec(memory_space=pl.ANY)
     vmem = pl.BlockSpec(memory_space=pltpu.VMEM)
@@ -609,6 +641,7 @@
             shape((shards, rows, width), bf16),
             shape((shards, rows, width), bf16),
             shape((2, count, shards - 1, 2, thin, part), bf16),
+            shape((2, shard, part), bf16),
             shape((width, wqkv.shape[1]), bf16),
             shape((width, width), bf16),
             shape((shards, rows, 4 * HDIM), bf16),
@@ -620,8 +653,8 @@
             shape((2, rows, HDIM), f32),
             shape((8, width), f32),
         ),
-        in_specs=[smem, smem, vmem, vmem, vmem, vmem, any_space, any_space, any_space],
-        out_specs=[any_space] * 6 + [vmem] * 7,
+        in_specs=[smem, smem, vmem, vmem, vmem, vmem] + [any_space] * 4,
+        out_specs=[any_space] * 7 + [vmem] * 7,
         scratch_shapes=[
             pltpu.VMEM((shards, 8, width), f32),
             pltpu.VMEM((width, wqkv.shape[1]), bf16),
@@ -629,6 +662,11 @@
             pltpu.VMEM((shards, rows, 4 * HDIM), bf16),
             pltpu.VMEM((rows, width), bf16),
             pltpu.VMEM((rows, shards * rows), f32),
+            pltpu.VMEM((2, thin, gate.shape[1]), bf16),
+            pltpu.VMEM((shards, 2, thin, part), bf16),
+            pltpu.VMEM((2, shard, gate.shape[1]), bf16),
+            pltpu.VMEM((2, shard, part), bf16),
+            pltpu.SemaphoreType.DMA((4,)),
             pltpu.SemaphoreType.DMA((8,)),
             sems(3),
             sems(4),
@@ -648,7 +686,7 @@
         compiler_params=pltpu.CompilerParams(
             collective_id=0, has_side_effects=True, vmem_limit_bytes=60 * 2**20
         ),
-    )(lengths, starts, x, cot, vec, inverse, wqkv, wo, pieces)
+    )(lengths, starts, x, cot, vec, inverse, wqkv, wo, gate, up)
 
 
 class Stream:
@@ -1410,6 +1448,117 @@
     )(lengths, starts, query, lse, trig, gains, x, cot, mid, part, normed, attn, mlp, kv, wqkv, wo, downs, gates, ups)
 
 
+class Place:
+    def __init__(self):
+        here = lax.axis_index("fsdp")
+        self.near = [here, here + 1 - 2 * lax.rem(here, 2), lax.rem(here + 2, 4), 3 - here]
+
+
+def feed_forward_kernel(
+    x_ref, cot_ref, wgu, own_gu, down_hbm, act_ref, dgate_ref, dup_ref, norm_ref, mlp_ref, w_ref, down_ref, sems
+):
+    f32, bf16 = jnp.float32, jnp.bfloat16
+    cores, line, others, kinds, thin, part = wgu.shape
+    shard = own_gu.shape[1]
+
+    @pl.when(pl.program_id(0) == 0)
+    def _():
+        near = Place().near
+        copies = [pltpu.make_async_copy(down_hbm, down_ref, sems.at[0])]
+        for g in range(kinds):
+            at = pl.multiple_of(near[0] * shard, shard)
+            copies.append(
+                pltpu.make_async_copy(own_gu.at[g], w_ref.at[g, pl.ds(at, shard)], sems.at[1 + g])
+            )
+        n = 1 + kinds
+        for d in range(1, 4):
+            for c in range(cores):
+                for z in range(line):
+                    for g in range(kinds):
+                        at = pl.multiple_of(near[d] * shard + (c * line + z) * thin, thin)
+                        copies.append(
+                            pltpu.make_async_copy(
+                                wgu.at[c, z, d - 1, g], w_ref.at[g, pl.ds(at, thin)], sems.at[n]
+                            )
+                        )
+                        n += 1
+        for copy in copies:
+            copy.start()
+        for copy in copies:
+            copy.wait()
+
+    x, cot = x_ref[...], cot_ref[...]
+    for lo in range(0, part, 512):
+        at = slice(lo, min(lo + 512, part))
+        gate = dot_f32(x, w_ref[0, :, at])
+        up = dot_f32(x, w_ref[1, :, at])
+        d_act = dot_f32(cot, down_ref[at, :], ((1,), (1,)))
+        sig = jax.nn.sigmoid(gate)
+        silu = gate * sig
+        act_ref[:, at] = (silu * up).astype(bf16)
+        dgate_ref[:, at] = (d_act * up * sig * (1.0 + gate * (1.0 - sig))).astype(bf16)
+        dup_ref[:, at] = (d_act * silu).astype(bf16)
+    for lo in range(0, x.shape[1], 512):
+        at = slice(lo, lo + 512)
+        norm_ref[:, at] = (
+            dot_f32(dgate_ref[...], w_ref[0, at, :], ((1,), (1,)))
+            + dot_f32(dup_ref[...], w_ref[1, at, :], ((1,), (1,)))
+        ).astype(bf16)
+        mlp_ref[:, at] = dot_f32(act_ref[...], down_ref[:, at]).astype(bf16)
+
+
+def feed_forward(x, cot, wgu, own_gu, down):
+    rows, width = x.shape
+    part = down.shape[0]
+    tile = rows // 4
+    bf16 = jnp.bfloat16
+    any_space = pl.BlockSpec(memory_space=pl.ANY)
+    wide = pl.BlockSpec((tile, width), lambda i: (i, 0))
+    hidden = pl.BlockSpec((tile, part), lambda i: (i, 0))
+    shape = jax.ShapeDtypeStruct
+    return pl.pallas_call(
+        feed_forward_kernel,
+        name="feed_forward",
+        grid=(rows // tile,),
+        out_shape=[shape((rows, part), bf16)] * 3 + [shape((rows, width), bf16)] * 2,
+        in_specs=[wide, wide] + [any_space] * 3,
+        out_specs=[hidden] * 3 + [wide] * 2,
+        scratch_shapes=[
+            pltpu.VMEM((2, width, part), bf16),
+            pltpu.VMEM((part, width), bf16),
+            pltpu.SemaphoreType.DMA((3 + wgu.shape[0] * wgu.shape[1] * wgu.shape[2] * wgu.shape[3],)),
+        ],
+        compiler_params=pltpu.CompilerParams(vmem_limit_bytes=62 * 2**20),
+        cost_estimate=pl.CostEstimate(
+            flops=12 * rows * width * part, bytes_accessed=10 * width * part, transcendentals=rows * part
+        ),
+    )(x, cot, wgu, own_gu, down)
+
+
+def unfold_kernel(gate_ref, up_ref, gate_out, up_out):
+    part = gate_ref.shape[3]
+    for src, out in ((gate_ref, gate_out), (up_ref, up_out)):
+        for t in range(src.shape[1]):
+            out[:, t * part : (t + 1) * part] = src[0, t].astype(jnp.float32)
+
+
+def unfold(gate, up):
+    cores, shards, half, part = gate.shape
+    tile = 32
+    steps = half // tile
+    block = pl.BlockSpec((1, shards, tile, part), lambda c, i: (c, 0, i, 0))
+    out = pl.BlockSpec((tile, shards * part), lambda c, i: (c * steps + i, 0))
+    return pl.pallas_call(
+        unfold_kernel,
+        name="unfold",
+        grid=(cores, steps),
+        out_shape=[jax.ShapeDtypeStruct((cores * half, shards * part), jnp.float32)] * 2,
+        in_specs=[block, block],
+        out_specs=[out, out],
+        compiler_params=pltpu.CompilerParams(vmem_limit_bytes=32 * 2**20),
+    )(gate, up)
+
+
 def local(
     hidden_in,
     out_grad,
@@ -1759,17 +1908,11 @@
             jnp.zeros((4, model_width), jnp.float32),
         ]
     )
-    first_row = core * (shard_rows // 2) + line_pos * thin
-
-    def cut(weight):
-        piece = lax.dynamic_slice_in_dim(weight, first_row, thin, 0)
-        return jnp.stack([piece[:, t * part : (t + 1) * part] for t in range(shard_count)])
-
-    pieces = jnp.stack([cut(w_gate), cut(w_up)], axis=1)
     (
         normed_all,
         cot_all,
         wgu,
+        own_gu,
         wqkv_full,
         output_full,
         kv_full,
@@ -1789,29 +1932,12 @@
         inverse,
         jnp.concatenate([w_query, w_key, w_value], axis=1),
         w_output,
-        pieces,
-    )
-    def whole(which, weight):
-        mine = lax.dynamic_slice_in_dim(weight, here * part, part, 1)
-        other = wgu[:, :, :, which].transpose(2, 0, 1, 3, 4).reshape(
-            shard_count - 1, shard_rows, part
-        )
-        rows = place([mine] + [other[d] for d in range(shard_count - 1)], here)
-        return rows.reshape(model_width, part)
-
-    gate_part = whole(0, w_gate)
-    up_part = whole(1, w_up)
+        w_gate,
+        w_up,
+    )
     cot_all = cot_all.reshape(row_len, model_width)
     normed_all = normed_all.reshape(row_len, model_width)
-    gate_val = mat_dot(normed_all, gate_part)
-    up_val = mat_dot(normed_all, up_part)
-    sig_gate = jax.nn.sigmoid(gate_val)
-    silu_gate = gate_val * sig_gate
-    act_low = (silu_gate * up_val).astype(low)
-    d_act = dot_right_t(cot_all, w_down)
-    d_gate = (d_act * up_val * sig_gate * (1.0 + gate_val * (1.0 - sig_gate))).astype(low)
-    d_up = (d_act * silu_gate).astype(low)
-    norm_part = (dot_right_t(d_gate, gate_part) + dot_right_t(d_up, up_part)).astype(low)
+    act_low, d_gate, d_up, norm_part, mlp_part = feed_forward(normed_all, cot_all, wgu, own_gu, w_down)
     norm_part, act_low, d_gate, d_up = lax.optimization_barrier((norm_part, act_low, d_gate, d_up))
     norm_part = norm_part.reshape(shard_count, tok_rows, model_width)
     partial_value = scatter_relative([pick(norm_part, here ^ d) for d in range(shard_count)], "fsdp")
@@ -1820,7 +1946,7 @@
         dot_left_t(normed_all, d_value).astype(low).reshape(shard_count, 2, shard_rows // 2, part)
         for d_value in (d_gate, d_up)
     ]
-    mlp_part = mat_dot(act_low, w_down).astype(low).reshape(shard_count, tok_rows, model_width)
+    mlp_part = mlp_part.reshape(shard_count, tok_rows, model_width)
     results = epilogue(
         doc_lengths,
         piece_starts,
@@ -1848,10 +1974,7 @@
     for d in range(shard_count - 1):
         output = output + mlp_land[d].astype(jnp.float32)
     down_sums = down_final.reshape(part, model_width).astype(jnp.float32)
-    grad_gate, grad_up = (
-        final.transpose(0, 2, 1, 3).reshape(shard_rows, ff_width).astype(jnp.float32)
-        for final in (gate_final, up_final)
-    )
+    grad_gate, grad_up = unfold(gate_final, up_final)
     attn_sums = attn_final.reshape(shard_rows, -1).astype(jnp.float32)
     ends = [0, model_width, model_width + kv_width, model_width + 2 * kv_width, 2 * (model_width + kv_width)]
     grad_query, grad_key, grad_value, grad_output = (attn_sums[:, ends[i] : ends[i + 1]] for i in range(4))

time: 843 us -> 720 us (0.85)
  matrix products: 133 us -> 39 us
  local copies, waits for them, and re-layouts: 124 us -> 32.8 us
  Pallas kernels: 521 us -> 598 us
  other arithmetic: 44.9 us -> 29.6 us
    dot_general x6 -> x0, matrix products: 95.6 us -> none  [the longest x3 52.3 us: mat_dot(): return jnp.dot(left, right, preferred_element_type=jnp.float32)]
    pallas_call x0 -> x2, Pallas kernels: none -> 78.4 us  [the longest x1 67.7 us: feed_forward(): pl.pallas_call(feed_forward_kernel, name='feed_forward', grid=(rows // ti...]
    convert_element_type x4 -> x0, local copies, waits for them, and re-layouts: 66.5 us -> none  [local_fast(): final.transpose(0, 2, 1, 3).reshape(shard_rows, ff_width)]
    another operation x7 -> x0, other arithmetic: 13.3 us -> none  [the longest x2 6.21 us: place(): return jnp.stack([pick(stacked, here ^ j) for j in range(count)])]
    transpose x1 -> x0, local copies, waits for them, and re-layouts: 9.11 us -> none  [whole(): wgu[:, :, :, which].transpose(2, 0, 1, 3, 4)]
    convert_element_type x2 -> x0, other arithmetic: 8.55 us -> none  [local_fast(): final.transpose(0, 2, 1, 3).reshape(shard_rows, ff_width)]
  transfers between devices with their start and end apart: 6 -> 6, of which waited for: 0 -> 1; matrix products, arithmetic and copies ran while one was open for 8% -> 9% of each run, Pallas kernels for 0% -> 0%
where the time goes in v4:
time: 720 us; the launch traced here: 710 us
  Pallas kernels  598 us (83%)
  matrix products  39 us (5%)
  local copies, waits for them, and re-layouts  32.8 us (5%)
  other arithmetic  29.6 us (4%)
    pallas_call x1, Pallas kernels, epilogue(): pl.pallas_call(epilogue_kernel, name='epilogue', out_shape=tuple(outs), i...  342 us
    pallas_call x1, Pallas kernels, prologue(): pl.pallas_call(prologue_kernel, name='prologue', out_shape=(shape((shards...  178 us
    pallas_call x1, Pallas kernels, feed_forward(): pl.pallas_call(feed_forward_kernel, name='feed_forward', grid=(rows // ti...  67.7 us
    dot_general x3, matrix products, dot_left_t(): lax.dot_general(left, right, (((0,), (0,)), ((), ())), preferred_element_...  39 us
    convert_element_type x2, local copies, waits for them, and re-layouts, local_fast(): dot_left_t(normed_all, d_value).astype(low)  20.4 us
  transfers between devices with their start and end apart: 6, of which 1 were waited for; matrix products, arithmetic and copies ran while one was open for 9% of the time, Pallas kernels for 0%

profile of v4, /device:TPU:0, one launch (start us, length us, event | category | flops | bytes accessed | tf_op | source)
XLA Modules:
  0.0 709.8 jit_solution(6868586534418371007)
XLA Ops:
  0.7 0.7 bitcast_convert_fusion.2
  1.3 0.1 pad_maximum_fusion.2
  1.4 0.7 broadcast_in_dim.51
  2.1 0.7 broadcast_in_dim.52
  2.8 0.7 broadcast_in_dim.53
  3.5 0.1 dynamic_update_slice.20
  3.6 0.7 fusion.5
  4.3 0.1 add.74
  4.5 2.9 pad_maximum_fusion.1.wqkv_ref
  7.4 0.7 concatenate.12.vec_ref
  8.0 0.6 broadcast_in_dim.50.inverse_ref
  8.6 178.5 %prologue.1 = (bf16[4,320,1536]{2,1,0:T(8,128)(2,1)}, bf16[4,320,1536]{2,1,0:T(8,128)(2,1)}, bf16[2,4,3,2,48,2240]{5,4,3,2,1,0:T(8,128)(2,1)}, bf16[2,384,2240]{...) custom-call(s32[1,8]{1,0:T(1,128)} %lengths_ref.3, ...), custom_call_target="tpu_custom_call" | custom-call | tf_op jit(solution)/shard_map/prologue/pallas_call | solution.py:637
  187.1 67.7 %feed_forward.1 = (bf16[1280,2240]{1,0:T(8,128)(2,1)}, bf16[1280,2240]{1,0:T(8,128)(2,1)}, bf16[1280,2240]{1,0:T(8,128)(2,1)}, bf16[1280,1536]{1,0:T(8,128)(2,1)}, bf16[1280,1536]{1,0:T(8,128)(2,1)}) custom-call(bf16[1280,1536]{1,0:T(8,128)(2,1)} %bitcast.82, bf16[1280,1536]{1,0:T(8,128)(2,1)} %bitcast.85, ...), custom_call_target="tpu_custom_call" | custom-call | flops 52848230400 | bytes 34406400 | tf_op jit(solution)/shard_map/feed_forward/pallas_call | solution.py:1519
  254.9 0.0 copy-start.5
  254.9 1.8 dynamic-slice_bitcast_fusion.6
  256.7 2.2 collective-permute-start
  258.9 0.1 collective-permute-start.1
  258.9 1.9 collective-permute-start.4
  260.9 0.0 slice-start.4
  260.9 0.0 copy-start.3
  260.9 0.0 slice-start.5
  260.9 0.1 collective-permute-start.3
  261.0 0.0 copy-done.5
  261.0 13.9 %convolution_convert_fusion.2 = bf16[2240,1536]{1,0:T(8,128)(2,1)} fusion(bf16[1280,2240]{1,0:T(8,128)(2,1)} %get-tuple-element.66, bf16[1280,1536]{1,0:T(8,128)(2,1)S(1)} %bitcast.86), kind=kOutput, calls=%fused_computation.2 | convolution fusion | flops 8811479040 | bytes 16547840 | tf_op jit(solution)/shard_map/dot_general | solution.py:70
  274.9 2.8 collective-permute-done.1
  277.7 1.9 fusion.2
  279.6 1.2 collective-permute-start.2
  280.8 0.0 slice-done.4
  280.8 0.0 copy-done.3
  280.8 0.0 slice-done.5
  280.8 11.5 %convolution_convert_fusion.1 = bf16[1536,2240]{0,1:T(8,128)(2,1)} fusion(bf16[1280,1536]{1,0:T(8,128)(2,1)S(1)} %bitcast.83, bf16[1280,2240]{1,0:T(8,128)(2,1)S(1)} %bitcast.88), kind=kOutput, calls=%fused_computation.1 | convolution fusion | flops 8811479040 | bytes 16547840 | tf_op jit(solution)/shard_map/dot_general | solution.py:70
  292.3 0.0 copy-start.4
  292.3 0.0 collective-permute-done
  292.3 0.0 collective-permute-done.4
  292.3 0.0 collective-permute-done.2
  292.3 2.4 fusion.3
  294.7 0.6 collective-permute-start.5
  295.3 0.0 copy-done.4
  295.3 13.6 %convolution_convert_fusion = bf16[1536,2240]{0,1:T(8,128)(2,1)} fusion(bf16[1280,1536]{1,0:T(8,128)(2,1)S(1)} %bitcast.84, bf16[1280,2240]{1,0:T(8,128)(2,1)} %get-tuple-element.68), kind=kOutput, calls=%fused_computation | convolution fusion | flops 8811479040 | bytes 16547840 | tf_op jit(solution)/shard_map/dot_general | solution.py:70
  308.9 10.2 %copy.31 = bf16[1536,2240]{1,0:T(8,128)(2,1)} copy(bf16[1536,2240]{0,1:T(8,128)(2,1)} %convolution_convert_fusion) | data formatting | bytes 13762560 | tf_op jit(solution)/shard_map/convert_element_type | solution.py:1946
  319.1 10.2 %copy.30 = bf16[1536,2240]{1,0:T(8,128)(2,1)} copy(bf16[1536,2240]{0,1:T(8,128)(2,1)} %convolution_convert_fusion.1) | data formatting | bytes 13762560 | tf_op jit(solution)/shard_map/convert_element_type | solution.py:1946
  329.3 0.0 collective-permute-done.3
  329.3 0.0 collective-permute-done.5
  329.3 1.2 fusion.1
  330.5 1.4 pad_maximum_fusion.part_hbm
  331.9 341.6 %epilogue.1 = (f32[320,1536]{1,0:T(8,128)}, f32[8,1536]{1,0:T(8,128)}, bf16[2,1120,1536]{2,1,0:T(8,128)(2,1)}, bf16[2,4,192,2240]{3,2,1,0:T(8,128)(2,1)}, bf16[2...) custom-call(s32[1,8]{1,0:T(1,128)} %lengths_ref.3, ...), custom_call_target="tpu_custom_call" | custom-call | tf_op jit(solution)/shard_map/epilogue/pallas_call | solution.py:1394
  673.5 1.3 dynamic-slice_bitcast_fusion.8
  674.7 1.5 dynamic-slice_reduce_fusion
  676.2 2.4 bitcast_convert_fusion.1
  678.7 0.9 fusion.7
  679.6 0.0 copy-start
  679.6 2.7 fusion.6
  682.3 0.0 copy-done
  682.3 1.4 copy-done.1
  683.7 3.1 convert_add_fusion
  686.8 10.8 %bitcast_convert_fusion = f32[2240,1536]{1,0:T(8,128)} fusion(bf16[2,1120,1536]{2,1,0:T(8,128)(2,1)} %get-tuple-element.77), kind=kLoop, calls=%fused_computation.3 | loop fusion | flops 3440640 | bytes 20643840 | tf_op jit(solution)/shard_map/convert_element_type | solution.py:1976
  697.6 0.0 slice-done
  697.6 0.0 slice-done.2
  697.6 0.0 slice-done.1
  697.6 0.0 slice-done.3
  697.6 0.0 copy-start.2
  697.7 10.6 %unfold.1 = (f32[384,8960]{1,0:T(8,128)}, f32[384,8960]{1,0:T(8,128)}) custom-call(bf16[2,4,192,2240]{3,2,1,0:T(8,128)(2,1)S(1)} %bitcast.70, bf16[2,4,192,2240]{3,2,1,0:T(8,128)(2,1)S(1)} %bitcast.72), custom_call_target="tpu_custom_call" | custom-call | tf_op jit(solution)/shard_map/unfold/pallas_call | solution.py:1551
  708.3 0.0 copy-done.2
  708.3 1.3 copy.38
  (17 shorter events, 0.1 us)
Async XLA Ops:
  254.9 6.1 copy-start.5
  256.7 35.6 %collective-permute-start = (bf16[160,1536]{1,0:T(8,128)(2,1)S(1)}, bf16[160,1536]{1,0:T(8,128)(2,1)S(1)}, u32[]{:S(2)}, u32[]{:S(2)}) collective-permute-start(bf16[160,1536]{1,0:T(8,128)(2,1)S(1)} %get-tuple-element.87), channel_id=1, source_target_pairs={{0,2},{1,3},{2,0},{3,1},{4,6},{5,7},{6,4},{7,5},{8,10},{9,11},{10,... | collective-permute-start | bytes 1474568 | tf_op jit(solution)/shard_map/ppermute | solution.py:109
  258.9 18.9 %collective-permute-start.1 = (bf16[160,1536]{1,0:T(8,128)(2,1)S(1)}, bf16[160,1536]{1,0:T(8,128)(2,1)S(1)}, u32[]{:S(2)}, u32[]{:S(2)}) collective-permute-start(bf16[160,1536]{1,0:T(8,128)(2,1)S(1)} %get-tuple-element.88), channel_id=1, source_target_pairs={{0,2},{1,3},{2,0},{3,1},{4,6},{5,7},{6,4},{7,5},{8,10},{9,11},{10,... | collective-permute-start | bytes 1474568 | tf_op jit(solution)/shard_map/ppermute | solution.py:109
  258.9 33.4 %collective-permute-start.4 = (bf16[160,1536]{1,0:T(8,128)(2,1)S(1)}, bf16[160,1536]{1,0:T(8,128)(2,1)S(1)}, u32[]{:S(2)}, u32[]{:S(2)}) collective-permute-start(bf16[160,1536]{1,0:T(8,128)(2,1)S(1)} %get-tuple-element.89), channel_id=1, source_target_pairs={{0,1},{1,0},{2,3},{3,2},{4,5},{5,4},{6,7},{7,6},{8,9},{9,8},{10,11... | collective-permute-start | bytes 1474568 | tf_op jit(solution)/shard_map/ppermute | solution.py:109
  260.9 20.0 %slice-start.4 = ((s8[5898240]{0:T(1024)(128)(4,1)}), s8[4194304]{0:T(1024)(128)(4,1)S(1)}, s32[]{:S(2)}) async-start(s8[5898240]{0:T(1024)(128)(4,1)} %bitcast.87), calls=%async_computation.4 | async-start | bytes 8388608
  260.9 20.0 %copy-start.3 = (bf16[4,320,1536]{2,1,0:T(8,128)(2,1)S(1)}, bf16[4,320,1536]{2,1,0:T(8,128)(2,1)}, u32[]{:S(2)}) copy-start(bf16[4,320,1536]{2,1,0:T(8,128)(2,1)} %get-tuple-element.47) | copy-start | bytes 11796484
  260.9 20.0 %slice-start.5 = ((s8[5898240]{0:T(1024)(128)(4,1)}), s8[1703936]{0:T(1024)(128)(4,1)S(1)}, s32[]{:S(2)}) async-start(s8[5898240]{0:T(1024)(128)(4,1)} %bitcast.87), calls=%async_computation.5 | async-start | bytes 3407872
  260.9 68.4 %collective-permute-start.3 = (bf16[160,1536]{1,0:T(8,128)(2,1)S(1)}, bf16[160,1536]{1,0:T(8,128)(2,1)S(1)}, u32[]{:S(2)}, u32[]{:S(2)}) collective-permute-start(bf16[160,1536]{1,0:T(8,128)(2,1)S(1)} %get-tuple-element.90), channel_id=1, source_target_pairs={{0,1},{1,0},{2,3},{3,2},{4,5},{5,4},{6,7},{7,6},{8,9},{9,8},{10,11... | collective-permute-start | bytes 1474568 | tf_op jit(solution)/shard_map/ppermute | solution.py:109
  279.6 12.7 %collective-permute-start.2 = (bf16[160,1536]{1,0:T(8,128)(2,1)}, bf16[160,1536]{1,0:T(8,128)(2,1)S(1)}, u32[]{:S(2)}, u32[]{:S(2)}) collective-permute-start(bf16[160,1536]{1,0:T(8,128)(2,1)} %fusion.2), channel_id=1, source_target_pairs={{0,1},{1,0},{2,3},{3,2},{4,5},{5,4},{6,7},{7,6},{8,9},{9,8},{10,11... | collective-permute-start | bytes 1474568 | tf_op jit(solution)/shard_map/ppermute | solution.py:109
  292.3 3.0 copy-start.4
  294.7 34.6 %collective-permute-start.5 = (bf16[160,1536]{1,0:T(8,128)(2,1)}, bf16[160,1536]{1,0:T(8,128)(2,1)S(1)}, u32[]{:S(2)}, u32[]{:S(2)}) collective-permute-start(bf16[160,1536]{1,0:T(8,128)(2,1)} %get-tuple-element.86), channel_id=1, source_target_pairs={{0,2},{1,3},{2,0},{3,1},{4,6},{5,7},{6,4},{7,5},{8,10},{9,11},{10,... | collective-permute-start | bytes 1474568 | tf_op jit(solution)/shard_map/ppermute | solution.py:109
  679.6 2.7 copy-start
  679.6 4.1 copy-start.1
  686.8 10.8 %slice-start = ((s8[7077888]{0:T(1024)(128)(4,1)}), s8[4194304]{0:T(1024)(128)(4,1)S(1)}, s32[]{:S(2)}) async-start(s8[7077888]{0:T(1024)(128)(4,1)} %bitcast.69), calls=%async_computation | async-start | bytes 8388608
  686.8 10.8 %slice-start.2 = ((s8[7077888]{0:T(1024)(128)(4,1)}), s8[4194304]{0:T(1024)(128)(4,1)S(1)}, s32[]{:S(2)}) async-start(s8[7077888]{0:T(1024)(128)(4,1)} %bitcast.71), calls=%async_computation.2 | async-start | bytes 8388608
  686.8 10.8 %slice-start.1 = ((s8[7077888]{0:T(1024)(128)(4,1)}), s8[2883584]{0:T(1024)(128)(4,1)S(1)}, s32[]{:S(2)}) async-start(s8[7077888]{0:T(1024)(128)(4,1)} %bitcast.69), calls=%async_computation.1 | async-start | bytes 5767168
  686.8 10.8 %slice-start.3 = ((s8[7077888]{0:T(1024)(128)(4,1)}), s8[2883584]{0:T(1024)(128)(4,1)S(1)}, s32[]{:S(2)}) async-start(s8[7077888]{0:T(1024)(128)(4,1)} %bitcast.71), calls=%async_computation.3 | async-start | bytes 5767168
  697.6 10.6 %copy-start.2 = (f32[320,1536]{1,0:T(8,128)S(1)}, f32[320,1536]{1,0:T(8,128)}, u32[]{:S(2)}) copy-start(f32[320,1536]{1,0:T(8,128)} %get-tuple-element.108) | copy-start | bytes 5898244

commit v5 on v4

--- a/solution.py
+++ b/solution.py
@@ -453,11 +453,8 @@
         copy.wait()
     for t in range(4):
         gu_ref[t] = thin_buf[:, :, t * part : (t + 1) * part]
-    for copy in gu_sends:
-        copy.start()
     for copy in own_copies:
         copy.start()
-    wo_gather.start()
 
     bias, query_rel = mask_bias(here, rows, kv_buf.shape[0] * rows, lengths_ref, starts_ref)
     bias_ref[...] = bias
@@ -480,12 +477,9 @@
     for swap in qkv_swaps[:2]:
         swap.start()
     for copy in gu_sends:
-        copy.wait_recv()
-    start_hop(1)
-    own_swap.start()
+        copy.start()
     qkv_gather.finish()
     qkv_swaps[2].start()
-    cot_gather.start()
     own_copies[0].wait()
     for copy in qkv_comes:
         copy.wait_recv()
@@ -515,6 +509,7 @@
     ]
     for copy in kv_sends:
         copy.start()
+    wo_gather.start()
 
     def query_pair(pair, carry):
         columns = pl.ds(pl.multiple_of(pair * 2 * HDIM, 2 * HDIM), 2 * HDIM)
@@ -535,9 +530,10 @@
 
     own_store = pltpu.make_async_copy(own_buf, own_gu, cut_sems.at[0])
     own_store.start()
-    wo_gather.hand_on()
-    for swap in wo_swaps[:2]:
-        swap.start()
+    for copy in gu_sends:
+        copy.wait_recv()
+    start_hop(1)
+    own_swap.start()
     for copy in kv_comes:
         copy.wait_recv()
     kv_copy = pltpu.make_async_copy(kv_buf, kv_full, local_sems.at[5])
@@ -562,15 +558,16 @@
         attn_ref[:, columns] = mixed.astype(jnp.bfloat16)
         return jnp.where(head_lane == h, peak + jnp.log(total), lse)
 
-    lse = lax.fori_loop(0, HEADS // 2, head_step, jnp.zeros((rows, HDIM), jnp.float32))
+    lse = lax.fori_loop(0, 2 * HEADS // 3, head_step, jnp.zeros((rows, HDIM), jnp.float32))
+    wo_gather.hand_on()
+    for swap in wo_swaps[:2]:
+        swap.start()
+    cot_gather.start()
+    lse_ref[...] = lax.fori_loop(2 * HEADS // 3, HEADS, head_step, lse)
+    take_hop(1)
+    start_hop(2)
     wo_gather.finish()
     wo_swaps[2].start()
-    take_hop(1)
-    start_hop(2)
-    lse_ref[...] = lax.fori_loop(HEADS // 2, HEADS, head_step, lse)
-    cot_gather.hand_on()
-    take_hop(2)
-    start_hop(3)
     own_copies[1].wait()
     for copy in wo_comes:
         copy.wait_recv()
@@ -591,6 +588,9 @@
     norm_gather.start()
     norm_copy = pltpu.make_async_copy(normed_buf, normed_all.at[here], local_sems.at[7])
     norm_copy.start()
+    cot_gather.hand_on()
+    take_hop(2)
+    start_hop(3)
     norm_gather.hand_on()
     cot_gather.finish()
     take_hop(3)
@@ -712,18 +712,23 @@
             device_id_type=MESH,
         )
 
-    def total(self, refs):
+    def load(self, refs, first):
         copies = [
-            pltpu.make_async_copy(ref, self.loads.at[i], self.local_sems.at[i]) for i, ref in enumerate(refs)
+            pltpu.make_async_copy(ref, self.loads.at[first + i], self.local_sems.at[first + i])
+            for i, ref in enumerate(refs)
         ]
         for copy in copies:
             copy.start()
-        for copy in copies:
-            copy.wait()
-        out = self.loads[0].astype(jnp.float32)
-        for i in range(1, len(refs)):
-            out = out + self.loads[i].astype(jnp.float32)
-        return out.astype(jnp.bfloat16)
+
+        def total():
+            for copy in copies:
+                copy.wait()
+            out = self.loads[first].astype(jnp.float32)
+            for i in range(1, len(refs)):
+                out = out + self.loads[first + i].astype(jnp.float32)
+            return out.astype(jnp.bfloat16)
+
+        return total
 
     def free(self, role, which, p):
         for copy in self.busy.pop((role, which, p % 2), list)():
@@ -753,9 +758,12 @@
         ]
 
     def end_send(self, p):
-        for which, kind in ((0, self.far), (1, self.near)):
+        totals = [
+            self.load(self.own(self.rows(kind, p)), first) for first, kind in ((0, self.far), (2, self.near))
+        ]
+        for which in range(2):
             self.free("end", which, p)
-            self.stage[which, p % 2] = self.total(self.own(self.rows(kind, p)))
+            self.stage[which, p % 2] = totals[which]()
             self.hold(
                 "end",
                 which,
@@ -767,10 +775,13 @@
                 ],
             )
 
-    def mid_pass(self, p):
+    def pass_load(self, p):
+        self.copy(self.land_end.at[p, 0], self.land_end.at[p, 0], p, 0, self.links.away).wait_recv()
+        return self.load(self.own(self.rows(self.far, p)) + [self.land_end.at[p, 0]], 4)
+
+    def mid_pass(self, p, total):
         self.free("mid", 0, p)
-        self.copy(self.land_end.at[p, 0], self.land_end.at[p, 0], p, 0, self.links.away).wait_recv()
-        self.stage[0, p % 2] = self.total(self.own(self.rows(self.far, p)) + [self.land_end.at[p, 0]])
+        self.stage[0, p % 2] = total()
         self.hold(
             "mid",
             0,
@@ -778,13 +789,17 @@
             lambda: [self.copy(self.stage.at[0, p % 2], self.land_mid.at[p], p, 2, self.links.toward)],
         )
 
-    def mid_sum(self, p):
+    def sum_load(self, p):
         links = self.links
-        self.free("mid", 1, p)
         self.copy(self.land_end.at[p, 1], self.land_end.at[p, 1], p, 1, links.away).wait_recv()
         self.copy(self.land_mid.at[p], self.land_mid.at[p], p, 2, links.toward).wait_recv()
         near = self.rows(self.near, p)
-        self.stage[1, p % 2] = self.total(self.own(near) + [self.land_end.at[p, 1], self.land_mid.at[p]])
+        return self.load(self.own(near) + [self.land_end.at[p, 1], self.land_mid.at[p]], 0)
+
+    def mid_sum(self, p, total):
+        links = self.links
+        self.free("mid", 1, p)
+        self.stage[1, p % 2] = total()
         self.own_copy(p).start()
 
         def sends():
@@ -810,7 +825,7 @@
         final = self.final(links.core, near)
         if self.targets:
             buf, final = buf.at[links.here], self.target(links.core, near, links.here)
-        return pltpu.make_async_copy(buf, final, self.local_sems.at[6 + p % 2])
+        return pltpu.make_async_copy(buf, final, self.local_sems.at[7 + p % 2])
 
     def target(self, core, rows, source):
         return self.final(core, rows).at[source]
@@ -862,6 +877,83 @@
                 self.copy(ref, ref, p, index, self.links.partner).wait_recv()
 
 
+class WeightSum:
+    def __init__(self, links, product, land, own, half_buf, load_buf, first, second, send, half_sems, plane_sems, sem):
+        self.links, self.product, self.land, self.own = links, product, land, own
+        self.half_buf, self.load_buf, self.first, self.second, self.send = half_buf, load_buf, first, second, send
+        self.half_sems, self.sem = half_sems, sem
+        self.quarter = half_buf.shape[1] // 2
+        near_x, near_y, far = links.near[1:]
+        low, high = pl.ds(0, self.quarter), pl.ds(self.quarter, self.quarter)
+        self.first_sends = [
+            remote(half_buf.at[near_y, low], first.at[0], plane_sems, 0, links.plane[2]),
+            remote(half_buf.at[far, low], first.at[1], plane_sems, 1, links.plane[2]),
+            remote(half_buf.at[near_x, high], first.at[2], plane_sems, 2, links.plane[1]),
+            remote(half_buf.at[far, high], first.at[3], plane_sems, 3, links.plane[1]),
+        ]
+        self.second_sends = [
+            remote(send.at[0], second.at[0], plane_sems, 4, links.plane[1]),
+            remote(send.at[1], second.at[1], plane_sems, 5, links.plane[2]),
+        ]
+        self.half_sends = [
+            remote(half_buf.at[t], land.at[t], half_sems, t, links.partner) for t in range(4)
+        ]
+
+    def other_half(self):
+        def one(t, carry):
+            self.half_buf[t] = self.product(t, 1 - self.links.core).astype(jnp.bfloat16)
+            return carry
+
+        lax.fori_loop(0, 4, one, 0)
+        for copy in self.half_sends:
+            copy.start()
+
+    def own_half(self):
+        for copy in self.half_sends:
+            copy.wait_send()
+            copy.wait_recv()
+
+        def one(t, carry):
+            load = pltpu.make_async_copy(self.land.at[t], self.load_buf, self.sem)
+            load.start()
+            got = self.product(t, self.links.core)
+            load.wait()
+            self.half_buf[t] = (got + self.load_buf[...].astype(jnp.float32)).astype(jnp.bfloat16)
+            return carry
+
+        lax.fori_loop(0, 4, one, 0)
+        for copy in self.first_sends:
+            copy.start()
+
+    def plane_turn(self):
+        for copy in self.first_sends:
+            copy.wait_recv()
+        near_x, near_y, far = self.links.near[1:]
+        for i, near in ((0, near_x), (1, near_y)):
+            at = slice(i * self.quarter, (i + 1) * self.quarter)
+            self.send[i] = (
+                self.half_buf[near, at].astype(jnp.float32) + self.first[2 * i + 1].astype(jnp.float32)
+            ).astype(jnp.bfloat16)
+        for copy in self.second_sends:
+            copy.start()
+
+    def plane_end(self):
+        for copy in self.second_sends + self.first_sends:
+            copy.wait_send()
+        for copy in self.second_sends:
+            copy.wait_recv()
+        for i in range(2):
+            at = slice(i * self.quarter, (i + 1) * self.quarter)
+            self.load_buf[at, :] = (
+                self.half_buf[self.links.here, at].astype(jnp.float32)
+                + self.first[2 * i].astype(jnp.float32)
+                + self.second[i].astype(jnp.float32)
+            ).astype(jnp.bfloat16)
+        store = pltpu.make_async_copy(self.load_buf, self.own, self.sem)
+        store.start()
+        store.wait()
+
+
 def epilogue_kernel(
     lengths_ref,
     starts_ref,
@@ -872,36 +964,50 @@
     x_hbm,
     cot_hbm,
     mid_hbm,
-    part_hbm,
     normed_hbm,
     attn_hbm,
-    mlp_hbm,
     kv_hbm,
     wqkv_hbm,
     wo_hbm,
-    down_part,
-    gate_part,
-    up_part,
+    act_hbm,
+    dgate_hbm,
+    dup_hbm,
+    normed_all,
+    cot_all,
+    w_hbm,
+    down_hbm,
     grad_input_ref,
     sums_ref,
     down_final,
     gate_final,
     up_final,
-    attn_final,
+    out_final,
+    qkv_final,
     down_core,
     gate_core,
     up_core,
-    attn_core,
-    attn_own,
+    out_core,
+    qkv_core,
+    out_own,
+    qkv_own,
     mlp_land,
+    mlp_own,
+    norm_land,
+    norm_parts,
+    mlp_parts,
+    down_own,
+    gate_own,
+    up_own,
     down_end,
     down_mid,
     gate_end,
     gate_mid,
     up_end,
     up_mid,
-    attn_end,
-    attn_mid,
+    out_end,
+    out_mid,
+    qkv_end,
+    qkv_mid,
     kv_buf,
     key_turned,
     bias_ref,
@@ -916,35 +1022,46 @@
     kv_land,
     normed_turned,
     attn_turned,
-    half_buf,
-    half_load,
-    plane_first,
-    plane_second,
-    plane_send,
+    out_half,
+    out_load,
+    out_first,
+    out_second,
+    out_send,
+    qkv_half,
+    qkv_load,
+    qkv_first,
+    qkv_second,
+    qkv_send,
     vec_plane,
     vec_core,
     vec_line,
     vec_send,
+    norm_own,
     down_loads,
     down_stage,
     gu_loads,
     gate_stage,
-    up_stage,
-    attn_loads,
-    attn_stage,
+    out_loads,
+    out_stage,
+    qkv_loads,
+    qkv_stage,
     local_sems,
     scope_sems,
+    norm_sems,
     mlp_sems,
     load_sems,
     core_sems,
     kv_sems,
     half_sems,
     plane_sems,
+    qkv_half_sems,
+    qkv_plane_sems,
     vec_sems,
     down_sems,
     gate_sems,
     up_sems,
-    attn_sems,
+    out_sems,
+    qkv_sems,
 ):
     links = Links()
     here, core, line = links.here, links.core, links.line
@@ -965,21 +1082,11 @@
         pl.semaphore_signal(barrier, inc=1, device_id=other, device_id_type=MESH)
     pl.semaphore_wait(barrier, len(others))
 
-    swaps = [
-        remote(down_part.at[1 - core], down_core, core_sems, 0, links.partner),
-        remote(gate_part.at[:, 1 - core], gate_core, core_sems, 1, links.partner),
-        remote(up_part.at[:, 1 - core], up_core, core_sems, 2, links.partner),
+    fetches = [pltpu.make_async_copy(kv_hbm, kv_buf, local_sems.at[1])]
+    fetches[0].start()
+    core_comes = [
+        remote(ref, ref, core_sems, i, links.partner) for i, ref in enumerate((down_core, gate_core, up_core))
     ]
-    for swap in swaps:
-        swap.start()
-    fetches = [pltpu.make_async_copy(kv_hbm, kv_buf, local_sems.at[1])]
-    mlp_sends = [
-        remote(mlp_hbm.at[links.near[d]], mlp_land.at[d - 1], mlp_sems, d - 1, links.plane[d]) for d in (1, 2, 3)
-    ]
-    for copy in mlp_sends:
-        copy.start()
-    for fetch in fetches:
-        fetch.start()
 
     def stream(size, total, own, end, mid, final, loads, stage, sems, targets=False):
         return Stream(
@@ -989,7 +1096,7 @@
     down = stream(
         down_stage.shape[2],
         down_core.shape[0],
-        lambda r: [down_part.at[core, r], down_core.at[r]],
+        lambda r: [down_own.at[r], down_core.at[r]],
         down_end,
         down_mid,
         lambda c, r: down_final.at[c, r],
@@ -1000,7 +1107,7 @@
     gate = stream(
         gate_stage.shape[3],
         gate_core.shape[1],
-        lambda r: [gate_part.at[:, core, r], gate_core.at[:, r]],
+        lambda r: [gate_own.at[:, r], gate_core.at[:, r]],
         gate_end,
         gate_mid,
         lambda c, r: gate_final.at[c, :, r],
@@ -1010,49 +1117,81 @@
         True,
     )
     up = stream(
-        up_stage.shape[3],
+        gate_stage.shape[3],
         up_core.shape[1],
-        lambda r: [up_part.at[:, core, r], up_core.at[:, r]],
+        lambda r: [up_own.at[:, r], up_core.at[:, r]],
         up_end,
         up_mid,
         lambda c, r: up_final.at[c, :, r],
         gu_loads,
-        up_stage,
+        gate_stage,
         up_sems,
         True,
     )
-    attn = stream(
-        attn_stage.shape[2],
-        attn_own.shape[0],
-        lambda r: [attn_own.at[r]],
-        attn_end,
-        attn_mid,
-        lambda c, r: attn_final.at[c, r],
-        attn_loads,
-        attn_stage,
-        attn_sems,
-    )
-    pairs = [(s, p) for s in (down, gate, up, attn) for p in range(s.pairs)]
+    up.busy = gate.busy
+    out = stream(
+        out_stage.shape[2],
+        out_own.shape[0],
+        lambda r: [out_own.at[r]],
+        out_end,
+        out_mid,
+        lambda c, r: out_final.at[c, r],
+        out_loads,
+        out_stage,
+        out_sems,
+    )
+    qkv = stream(
+        qkv_stage.shape[2],
+        qkv_own.shape[0],
+        lambda r: [qkv_own.at[r]],
+        qkv_end,
+        qkv_mid,
+        lambda c, r: qkv_final.at[c, r],
+        qkv_loads,
+        qkv_stage,
+        qkv_sems,
+    )
+    streams = (down, gate, up, out, qkv)
+    pairs = [(s, p) for s in streams for p in range(s.pairs)]
+
+    def when(i):
+        far = i + (4 if pairs[i][0].targets else 3)
+        return {
+            "end_send": i,
+            "mid_pass": i + 1,
+            "mid_sum": i + 2,
+            "mid_out": i + 3,
+            "mid_far": far,
+            "end_take": far + 1,
+        }
 
     def service(n):
-        def at(back):
-            return pairs[n - back] if 0 <= n - back < len(pairs) else None
+        def due(action):
+            return [pairs[i] for i in range(len(pairs)) if when(i)[action] == n]
 
         first = {0: down, down.pairs: gate, down.pairs + gate.pairs: up}
         if n in first:
-            swaps[list(first).index(n)].wait_recv()
+            core_comes[list(first).index(n)].wait_recv()
 
         @pl.when(is_end)
         def _():
-            for back, action in ((7, "end_take"), (0, "end_send")):
-                if at(back):
-                    getattr(at(back)[0], action)(at(back)[1])
+            for s, p in due("end_take"):
+                s.end_take(p)
+            for s, p in due("end_send"):
+                s.end_send(p)
 
         @pl.when(is_mid)
         def _():
-            for back, action in ((4, "mid_far"), (3, "mid_out"), (2, "mid_sum"), (1, "mid_pass")):
-                if at(back):
-                    getattr(at(back)[0], action)(at(back)[1])
+            for s, p in due("mid_far"):
+                s.mid_far(p)
+            for s, p in due("mid_out"):
+                s.mid_out(p)
+            sums = [(s, p, s.sum_load(p)) for s, p in due("mid_sum")]
+            passes = [(s, p, s.pass_load(p)) for s, p in due("mid_pass")]
+            for s, p, total in sums:
+                s.mid_sum(p, total)
+            for s, p, total in passes:
+                s.mid_pass(p, total)
 
     def scoped(refs, body):
         def inner(*bufs):
@@ -1066,13 +1205,17 @@
         pl.run_scoped(inner, *[pltpu.VMEM(r.shape, r.dtype) for r in refs])
 
     def norm_back():
-        scoped((mid_hbm, part_hbm, cot_hbm), norm_body)
-
-    def norm_body(mid_ref, part_ref, cot_ref):
+        for d in range(3):
+            remote(norm_land.at[d], norm_land.at[d], norm_sems, d, links.plane[d + 1]).wait_recv()
+        scoped((mid_hbm, norm_land, cot_hbm), norm_body)
+
+    def norm_body(mid_ref, land_ref, cot_ref):
         mid = mid_ref[...]
         inv = lax.rsqrt(jnp.mean(mid * mid, axis=1, keepdims=True) + epsilon)
         unit = mid * inv
-        part = part_ref[...]
+        part = norm_own[...]
+        for d in range(3):
+            part = part + land_ref[d].astype(f32)
         vec_send[2:3, :] = jnp.sum(part * unit, axis=0, keepdims=True)
         scaled = part * gains_ref[2:3, :]
         d_mid = cot_ref[...].astype(f32) + inv * (
@@ -1094,6 +1237,8 @@
         scoped((wo_hbm,), attn_body)
 
     def attn_body(wo_buf):
+        scoped((normed_hbm, attn_hbm), turn_body)
+
         def tile(i, carry):
             columns = pl.ds(pl.multiple_of(i * 256, 256), 256)
             dattn_ref[:, columns] = dot_f32(branch_ref[...], wo_buf[columns, :], ((1,), (1,))).astype(bf16)
@@ -1177,7 +1322,6 @@
             dqkv_ref[:, width + g * HDIM : width + (g + 1) * HDIM] = d_key.astype(bf16)
         dqkv_ref[:, width + KVH * HDIM :] = kv[:, KVH * HDIM :].astype(bf16)
         scoped((wqkv_hbm, x_hbm), input_body)
-        scoped((normed_hbm, attn_hbm), turn_body)
 
     def turn_body(normed_ref, attn_ref):
         normed_turned[...] = normed_ref[...].T
@@ -1210,128 +1354,252 @@
 
     shard = width // 4
     half = shard // 2
-    qkv_width = wqkv_hbm.shape[1]
-
-    def half_grad(t, which):
-        at = pl.ds(pl.multiple_of(t * shard + which * half, half), half)
-        return (
-            dot_f32(normed_turned[at, :], dqkv_ref[...]).astype(bf16),
-            dot_f32(attn_turned[at, :], branch_ref[...]).astype(bf16),
-        )
-
-    half_sends = [remote(half_buf.at[t], attn_core.at[t], half_sems, t, links.partner) for t in range(4)]
-
-    def other_half():
-        def one(t, carry):
-            left, right = half_grad(t, 1 - core)
-            half_buf[t, :, :qkv_width] = left
-            half_buf[t, :, qkv_width:] = right
-            return carry
-
-        lax.fori_loop(0, 4, one, 0)
-        for copy in half_sends:
-            copy.start()
+
+    def row_block(t, which):
+        return pl.ds(pl.multiple_of(t * shard + which * half, half), half)
+
+    out_sum = WeightSum(
+        links,
+        lambda t, which: dot_f32(attn_turned[row_block(t, which), :], branch_ref[...]),
+        out_core,
+        out_own,
+        out_half,
+        out_load,
+        out_first,
+        out_second,
+        out_send,
+        half_sems,
+        plane_sems,
+        local_sems.at[3],
+    )
+    qkv_sum = WeightSum(
+        links,
+        lambda t, which: dot_f32(normed_turned[row_block(t, which), :], dqkv_ref[...]),
+        qkv_core,
+        qkv_own,
+        qkv_half,
+        qkv_load,
+        qkv_first,
+        qkv_second,
+        qkv_send,
+        qkv_half_sems,
+        qkv_plane_sems,
+        local_sems.at[3],
+    )
+
+    def vec_core_step():
         for copy in vec_comes["plane"]:
             copy.wait_recv()
         vec_core[core] = vec_plane[0] + vec_plane[1] + vec_plane[2] + vec_plane[3]
         vec_copies["core"][0].start()
 
-    quarter = half // 2
-    near_x, near_y, far = links.near[1:]
-
-    def own_half():
-        for copy in half_sends:
-            copy.wait_send()
-        for t in range(4):
-            remote(attn_core.at[t], attn_core.at[t], half_sems, t, links.partner).wait_recv()
-            load = pltpu.make_async_copy(attn_core.at[t], half_load, local_sems.at[3])
-            load.start()
-            left, right = half_grad(t, core)
-            load.wait()
-            half_buf[t, :, :qkv_width] = (left.astype(f32) + half_load[:, :qkv_width].astype(f32)).astype(bf16)
-            half_buf[t, :, qkv_width:] = (right.astype(f32) + half_load[:, qkv_width:].astype(f32)).astype(bf16)
-        for copy in first_sends:
-            copy.start()
+    def vec_line_step():
         vec_comes["core"][0].wait_recv()
         vec_line[line] = vec_core[0] + vec_core[1]
         for copy in vec_copies["line"]:
             copy.start()
 
-    low_rows, high_rows = pl.ds(0, quarter), pl.ds(quarter, quarter)
-    first_sends = [
-        remote(half_buf.at[near_y, low_rows], plane_first.at[0], plane_sems, 0, links.plane[2]),
-        remote(half_buf.at[far, low_rows], plane_first.at[1], plane_sems, 1, links.plane[2]),
-        remote(half_buf.at[near_x, high_rows], plane_first.at[2], plane_sems, 2, links.plane[1]),
-        remote(half_buf.at[far, high_rows], plane_first.at[3], plane_sems, 3, links.plane[1]),
-    ]
-    second_sends = [
-        remote(plane_send.at[0], plane_second.at[0], plane_sems, 4, links.plane[1]),
-        remote(plane_send.at[1], plane_second.at[1], plane_sems, 5, links.plane[2]),
-    ]
-
-    def plane_turn():
-        for copy in first_sends:
-            copy.wait_recv()
-        plane_send[0] = (half_buf[near_x, 0:quarter].astype(f32) + plane_first[1].astype(f32)).astype(bf16)
-        plane_send[1] = (
-            half_buf[near_y, quarter : 2 * quarter].astype(f32) + plane_first[3].astype(f32)
-        ).astype(bf16)
-        for copy in second_sends:
-            copy.start()
-
-    def plane_end():
-        for copy in second_sends + first_sends:
-            copy.wait_send()
-        for copy in second_sends:
-            copy.wait_recv()
-        for i in range(2):
-            at = slice(i * quarter, (i + 1) * quarter)
-            half_load[at, :] = (
-                half_buf[here, at].astype(f32)
-                + plane_first[2 * i].astype(f32)
-                + plane_second[i].astype(f32)
-            ).astype(bf16)
-        store = pltpu.make_async_copy(half_load, attn_own, local_sems.at[3])
-        store.start()
+    def vec_end():
         for copy in vec_comes["line"]:
             copy.wait_recv()
         sums_ref[...] = vec_line[0] + vec_line[1] + vec_line[2] + vec_line[3]
-        store.wait()
-
-    def heads(lo, hi):
-        return lambda: lax.fori_loop(lo, hi, head_back, 0)
-
-    chain = [
-        norm_back,
-        attn_back,
-        heads(0, 2),
-        heads(2, 4),
-        heads(4, 6),
-        heads(6, 8),
-        heads(8, 10),
-        heads(10, 12),
-        kv_send,
-        input_back,
-        other_half,
-        own_half,
-        None,
-        plane_turn,
-        None,
-        plane_end,
-    ]
-    for n in range(len(pairs) + 8):
-        service(n)
-        if n < len(chain) and chain[n] is not None:
-            chain[n]()
-
-    for swap in swaps + kv_sends + mlp_sends:
-        swap.wait_send()
-    for copy in mlp_sends:
-        copy.wait_recv()
+
+    done = [0]
+
+    def tick():
+        service(done[0])
+        done[0] += 1
+
+    def fetch(src, dst, i):
+        return pltpu.make_async_copy(src, dst, scope_sems.at[i])
+
+    def down_grads(act_buf, cot_buf, send_buf, keep_buf):
+        loads = [fetch(act_hbm, act_buf, 0), fetch(cot_all, cot_buf, 1)]
+        for load in loads:
+            load.start()
+        for load in loads:
+            load.wait()
+        units, cols = keep_buf.shape
+
+        def product(which, out):
+            at = pl.ds(pl.multiple_of(which * cols, cols), cols)
+            for lo in range(0, units, 768):
+                part = slice(lo, min(lo + 768, units))
+                out[part, :] = dot_f32(act_buf[:, part], cot_buf[:, at], ((0,), (0,))).astype(bf16)
+
+        product(1 - core, send_buf)
+        send = remote(send_buf, down_core, core_sems, 0, links.partner)
+        send.start()
+        product(core, keep_buf)
+        keep = fetch(keep_buf, down_own, 0)
+        keep.start()
+        keep.wait()
+        send.wait_send()
+
+    def column_grads(turned, value_buf, send_buf, keep_buf):
+        def turn(normed_buf):
+            load = fetch(normed_all, normed_buf, 1)
+            load.start()
+            load.wait()
+            turned[...] = normed_buf[...].T.reshape(turned.shape)
+
+        def product(which, out):
+            left = turned[:, which].reshape(width // 2, turned.shape[3])
+            cols = value_buf.shape[1]
+            for lo in range(0, cols, 512):
+                at = slice(lo, min(lo + 512, cols))
+                out[:, :, at] = dot_f32(left, value_buf[:, at]).astype(bf16).reshape(4, width // 8, -1)
+
+        load = fetch(dgate_hbm, value_buf, 0)
+        load.start()
+        pl.run_scoped(turn, pltpu.VMEM(normed_all.shape, bf16))
+        for i, (land, own) in enumerate(((gate_core, gate_own), (up_core, up_own))):
+            load.wait()
+            send = remote(send_buf, land, core_sems, 1 + i, links.partner)
+            product(1 - core, send_buf)
+            send.start()
+            tick()
+            product(core, keep_buf)
+            if i == 0:
+                load = fetch(dup_hbm, value_buf, 0)
+                load.start()
+            keep = fetch(keep_buf, own, 1)
+            keep.start()
+            tick()
+            keep.wait()
+            send.wait_send()
+
+    order = (1, 2, 3, 0)
+
+    def token_sends(parts, land, sems):
+        return [
+            remote(parts.at[i], land.at[order[i] - 1], sems, order[i] - 1, links.plane[order[i]]) for i in range(3)
+        ]
+
+    def token_blocks(inputs, weights, product, sems, parts, land, keep, store, ticks):
+        depth = 3 - len(inputs)
+
+        def body(weight_buf, block_buf, send_buf):
+            def block_loads(i):
+                return [
+                    fetch(ref.at[links.near[order[i]]], block_buf.at[i % depth, j], 2 * (i % depth) + j)
+                    for j, ref in enumerate(inputs)
+                ]
+
+            load = pltpu.make_async_copy(weights, weight_buf, local_sems.at[2])
+            load.start()
+            for copy in block_loads(0):
+                copy.start()
+            load.wait()
+            sends = token_sends(parts, land, sems)
+            for i, d in enumerate(order):
+                if i < 3 and depth > 1:
+                    for copy in block_loads(i + 1):
+                        copy.start()
+                for copy in block_loads(i):
+                    copy.wait()
+                for lo in range(0, width, 512):
+                    at = slice(lo, lo + 512)
+                    got = product(block_buf.at[i % depth], weight_buf, at)
+                    if d == 0 and store is None:
+                        keep[:, at] = got
+                    else:
+                        send_buf[i % 2, :, at] = got.astype(bf16)
+                if d or store is not None:
+                    copy = fetch(send_buf.at[i % 2], parts.at[i] if d else store, 3)
+                    copy.start()
+                    copy.wait()
+                if d:
+                    sends[i].start()
+                if i < 3 and depth == 1:
+                    for copy in block_loads(i + 1):
+                        copy.start()
+                if i in ticks:
+                    tick()
+
+        pl.run_scoped(
+            body,
+            pltpu.VMEM(weights.shape, bf16),
+            pltpu.VMEM((depth, len(inputs)) + inputs[0].shape[1:], bf16),
+            pltpu.VMEM((2, rows, width), bf16),
+        )
+
+    def norm_product(block, weight, at):
+        return dot_f32(block[0], weight[0, at, :], ((1,), (1,))) + dot_f32(
+            block[1], weight[1, at, :], ((1,), (1,))
+        )
+
+    def mlp_product(block, weight, at):
+        return dot_f32(block[0], weight[:, at])
+
+    units = act_hbm.shape[1]
+
+    def by_block(ref):
+        return ref.reshape(4, rows, units)
+
+    pl.run_scoped(
+        down_grads,
+        pltpu.VMEM(act_hbm.shape, bf16),
+        pltpu.VMEM(cot_all.shape, bf16),
+        pltpu.VMEM(down_own.shape, bf16),
+        pltpu.VMEM(down_own.shape, bf16),
+    )
+    tick()
+    token_blocks(
+        (by_block(dgate_hbm), by_block(dup_hbm)), w_hbm, norm_product, norm_sems, norm_parts, norm_land, norm_own, None, (0, 1, 2, 3)
+    )
+    pl.run_scoped(
+        column_grads,
+        pltpu.VMEM((4, 2, width // 8, normed_all.shape[0]), bf16),
+        pltpu.VMEM(dgate_hbm.shape, bf16),
+        pltpu.VMEM(gate_own.shape, bf16),
+        pltpu.VMEM(gate_own.shape, bf16),
+    )
+    norm_back()
+    tick()
+    attn_back()
+    tick()
+    out_sum.other_half()
+    lax.fori_loop(0, 2, head_back, 0)
+    tick()
+    out_sum.own_half()
+    lax.fori_loop(2, 4, head_back, 0)
+    tick()
+    lax.fori_loop(4, 7, head_back, 0)
+    tick()
+    out_sum.plane_turn()
+    lax.fori_loop(7, 10, head_back, 0)
+    tick()
+    lax.fori_loop(10, 12, head_back, 0)
+    kv_send()
+    tick()
+    out_sum.plane_end()
+    tick()
+    input_back()
+    tick()
+    qkv_sum.other_half()
+    vec_core_step()
+    tick()
+    qkv_sum.own_half()
+    vec_line_step()
+    tick()
+    qkv_sum.plane_turn()
+    vec_end()
+    tick()
+    qkv_sum.plane_end()
+    assert down.pairs + gate.pairs + up.pairs + out.pairs >= done[0]
+    tick()
+    token_blocks((by_block(act_hbm),), down_hbm, mlp_product, mlp_sems, mlp_parts, mlp_land, None, mlp_own, (0, 1, 2, 3))
+    while done[0] <= len(pairs) + 3:
+        tick()
+
+    for copy in kv_sends + token_sends(norm_parts, norm_land, norm_sems) + token_sends(mlp_parts, mlp_land, mlp_sems):
+        copy.wait_send()
+    for d in range(3):
+        remote(mlp_land.at[d], mlp_land.at[d], mlp_sems, d, links.plane[d + 1]).wait_recv()
     for name in vec_copies:
         for copy in vec_copies[name]:
             copy.wait_send()
-    streams = (down, gate, up, attn)
 
     @pl.when(is_end)
     def _():
@@ -1347,55 +1615,71 @@
         s.close_core()
 
 
-def epilogue(
-    lengths, starts, query, lse, trig, gains, x, cot, mid, part, normed, attn, mlp, kv, wqkv, wo, downs, gates, ups
-):
+def epilogue(lengths, starts, query, lse, trig, gains, *others):
+    x, wqkv, act, normed_all, w_full = others[0], others[6], others[8], others[11], others[13]
     rows, width = x.shape
     bf16, f32 = jnp.bfloat16, jnp.float32
     any_space = pl.BlockSpec(memory_space=pl.ANY)
     vmem = pl.BlockSpec(memory_space=pltpu.VMEM)
     smem = pl.BlockSpec(memory_space=pltpu.SMEM)
     shape = jax.ShapeDtypeStruct
-    wide = wqkv.shape[1] + width
     half = width // 8
-    down_half = downs.shape[1]
-    cols = gates.shape[3]
-    down_size, gu_size, attn_size = 80, 16, 32
-    down_pairs = down_half // (2 * down_size)
+    cols = act.shape[1]
+    down_size, gu_size, attn_size = 160, 16, 32
+    down_pairs = cols // (2 * down_size)
     gu_pairs = half // (2 * gu_size)
     attn_pairs = half // (2 * attn_size)
-    down_chunk = (down_size, width)
+    down_chunk = (down_size, width // 2)
     gu_chunk = (4, gu_size, cols)
-    attn_chunk = (attn_size, wide)
+    out_chunk, qkv_chunk = (attn_size, width), (attn_size, wqkv.shape[1])
 
     def line_buffers(pairs, chunk):
         return [shape((pairs, 2) + chunk, bf16), shape((pairs,) + chunk, bf16)]
 
     def sems(*n):
         return pltpu.SemaphoreType.DMA((2,) + n)
+
+    def weight_buffers(cols):
+        return [
+            pltpu.VMEM((4, half, cols), bf16),
+            pltpu.VMEM((half, cols), bf16),
+            pltpu.VMEM((4, half // 2, cols), bf16),
+            pltpu.VMEM((2, half // 2, cols), bf16),
+            pltpu.VMEM((2, half // 2, cols), bf16),
+        ]
 
     outs = [
         shape((rows, width), f32),
         shape((8, width), f32),
-        shape((2, down_half, width), bf16),
+        shape((2, cols, width // 2), bf16),
         shape((2, 4, half, cols), bf16),
         shape((2, 4, half, cols), bf16),
-        shape((2, half, wide), bf16),
-        shape((down_half, width), bf16),
+        shape((2, half, width), bf16),
+        shape((2, half, wqkv.shape[1]), bf16),
+        shape((cols, width // 2), bf16),
         shape((4, half, cols), bf16),
         shape((4, half, cols), bf16),
-        shape((4, half, wide), bf16),
-        shape((half, wide), bf16),
+        shape((4, half, width), bf16),
+        shape((4, half, wqkv.shape[1]), bf16),
+        shape((half, width), bf16),
+        shape((half, wqkv.shape[1]), bf16),
         shape((3, rows, width), bf16),
+        shape((rows, width), bf16),
+        shape((3, rows, width), bf16),
+        shape((3, rows, width), bf16),
+        shape((3, rows, width), bf16),
+        shape((cols, width // 2), bf16),
+        shape((4, half, cols), bf16),
+        shape((4, half, cols), bf16),
     ]
     outs += line_buffers(down_pairs, down_chunk)
     outs += line_buffers(gu_pairs, gu_chunk) + line_buffers(gu_pairs, gu_chunk)
-    outs += line_buffers(attn_pairs, attn_chunk)
+    outs += line_buffers(attn_pairs, out_chunk) + line_buffers(attn_pairs, qkv_chunk)
     return pl.pallas_call(
         epilogue_kernel,
         name="epilogue",
         out_shape=tuple(outs),
-        in_specs=[smem] * 2 + [vmem] * 4 + [any_space] * 13,
+        in_specs=[smem] * 2 + [vmem] * 4 + [any_space] * len(others),
         out_specs=[vmem] * 2 + [any_space] * (len(outs) - 2),
         scratch_shapes=[
             pltpu.VMEM((4, rows, 4 * HDIM), bf16),
@@ -1412,28 +1696,30 @@
             pltpu.VMEM((3, rows, 4 * HDIM), bf16),
             pltpu.VMEM((width, rows), bf16),
             pltpu.VMEM((width, rows), bf16),
-            pltpu.VMEM((4, half, wide), bf16),
-            pltpu.VMEM((half, wide), bf16),
-            pltpu.VMEM((4, half // 2, wide), bf16),
-            pltpu.VMEM((2, half // 2, wide), bf16),
-            pltpu.VMEM((2, half // 2, wide), bf16),
+            *weight_buffers(width),
+            *weight_buffers(wqkv.shape[1]),
             pltpu.VMEM((4, 8, width), f32),
             pltpu.VMEM((2, 8, width), f32),
             pltpu.VMEM((4, 8, width), f32),
             pltpu.VMEM((8, width), f32),
-            pltpu.VMEM((4,) + down_chunk, bf16),
+            pltpu.VMEM((rows, width), f32),
+            pltpu.VMEM((7,) + down_chunk, bf16),
             pltpu.VMEM((2, 2) + down_chunk, bf16),
-            pltpu.VMEM((4,) + gu_chunk, bf16),
+            pltpu.VMEM((7,) + gu_chunk, bf16),
             pltpu.VMEM((2, 2) + gu_chunk, bf16),
-            pltpu.VMEM((2, 2) + gu_chunk, bf16),
-            pltpu.VMEM((4,) + attn_chunk, bf16),
-            pltpu.VMEM((2, 2) + attn_chunk, bf16),
+            pltpu.VMEM((7,) + out_chunk, bf16),
+            pltpu.VMEM((2, 2) + out_chunk, bf16),
+            pltpu.VMEM((7,) + qkv_chunk, bf16),
+            pltpu.VMEM((2, 2) + qkv_chunk, bf16),
             pltpu.SemaphoreType.DMA((4,)),
             pltpu.SemaphoreType.DMA((4,)),
             sems(3),
-            pltpu.SemaphoreType.DMA((8,)),
+            sems(3),
+            pltpu.SemaphoreType.DMA((9,)),
             sems(3),
             sems(3),
+            sems(4),
+            sems(6),
             sems(4),
             sems(6),
             sems(7),
@@ -1441,11 +1727,12 @@
             sems(gu_pairs, 11),
             sems(gu_pairs, 11),
             sems(attn_pairs, 11),
+            sems(attn_pairs, 11),
         ],
         compiler_params=pltpu.CompilerParams(
             collective_id=1, has_side_effects=True, vmem_limit_bytes=63 * 2**20
         ),
-    )(lengths, starts, query, lse, trig, gains, x, cot, mid, part, normed, attn, mlp, kv, wqkv, wo, downs, gates, ups)
+    )(lengths, starts, query, lse, trig, gains, *others)
 
 
 class Place:
@@ -1455,7 +1742,7 @@
 
 
 def feed_forward_kernel(
-    x_ref, cot_ref, wgu, own_gu, down_hbm, act_ref, dgate_ref, dup_ref, norm_ref, mlp_ref, w_ref, down_ref, sems
+    x_ref, cot_ref, wgu, own_gu, down_hbm, act_ref, dgate_ref, dup_ref, w_hbm, w_ref, down_ref, sems
 ):
     f32, bf16 = jnp.float32, jnp.bfloat16
     cores, line, others, kinds, thin, part = wgu.shape
@@ -1486,6 +1773,7 @@
             copy.start()
         for copy in copies:
             copy.wait()
+        pltpu.make_async_copy(w_ref, w_hbm, sems.at[0]).start()
 
     x, cot = x_ref[...], cot_ref[...]
     for lo in range(0, part, 512):
@@ -1498,13 +1786,10 @@
         act_ref[:, at] = (silu * up).astype(bf16)
         dgate_ref[:, at] = (d_act * up * sig * (1.0 + gate * (1.0 - sig))).astype(bf16)
         dup_ref[:, at] = (d_act * silu).astype(bf16)
-    for lo in range(0, x.shape[1], 512):
-        at = slice(lo, lo + 512)
-        norm_ref[:, at] = (
-            dot_f32(dgate_ref[...], w_ref[0, at, :], ((1,), (1,)))
-            + dot_f32(dup_ref[...], w_ref[1, at, :], ((1,), (1,)))
-        ).astype(bf16)
-        mlp_ref[:, at] = dot_f32(act_ref[...], down_ref[:, at]).astype(bf16)
+
+    @pl.when(pl.program_id(0) == pl.num_programs(0) - 1)
+    def _():
+        pltpu.make_async_copy(w_ref, w_hbm, sems.at[0]).wait()
 
 
 def feed_forward(x, cot, wgu, own_gu, down):
@@ -1520,9 +1805,9 @@
         feed_forward_kernel,
         name="feed_forward",
         grid=(rows // tile,),
-        out_shape=[shape((rows, part), bf16)] * 3 + [shape((rows, width), bf16)] * 2,
+        out_shape=[shape((rows, part), bf16)] * 3 + [shape((2, width, part), bf16)],
         in_specs=[wide, wide] + [any_space] * 3,
-        out_specs=[hidden] * 3 + [wide] * 2,
+        out_specs=[hidden] * 3 + [any_space],
         scratch_shapes=[
             pltpu.VMEM((2, width, part), bf16),
             pltpu.VMEM((part, width), bf16),
@@ -1530,33 +1815,64 @@
         ],
         compiler_params=pltpu.CompilerParams(vmem_limit_bytes=62 * 2**20),
         cost_estimate=pl.CostEstimate(
-            flops=12 * rows * width * part, bytes_accessed=10 * width * part, transcendentals=rows * part
+            flops=6 * rows * width * part, bytes_accessed=10 * width * part, transcendentals=rows * part
         ),
     )(x, cot, wgu, own_gu, down)
 
 
-def unfold_kernel(gate_ref, up_ref, gate_out, up_out):
+def unfold_kernel(gate_ref, up_ref, out_ref, qkv_ref, gate_out, up_out, out_out, query_out, key_out, value_out):
     part = gate_ref.shape[3]
     for src, out in ((gate_ref, gate_out), (up_ref, up_out)):
         for t in range(src.shape[1]):
             out[:, t * part : (t + 1) * part] = src[0, t].astype(jnp.float32)
-
-
-def unfold(gate, up):
+    out_out[...] = out_ref[0].astype(jnp.float32)
+    first = 0
+    for out in (query_out, key_out, value_out):
+        out[...] = qkv_ref[0, :, first : first + out.shape[1]].astype(jnp.float32)
+        first += out.shape[1]
+
+
+def unfold(gate, up, out, qkv):
     cores, shards, half, part = gate.shape
+    width = out.shape[2]
+    narrow = KVH * HDIM
     tile = 32
     steps = half // tile
+    wides = [shards * part] * 2 + [width, width, narrow, narrow]
     block = pl.BlockSpec((1, shards, tile, part), lambda c, i: (c, 0, i, 0))
-    out = pl.BlockSpec((tile, shards * part), lambda c, i: (c * steps + i, 0))
+
+    def flat(cols):
+        return pl.BlockSpec((1, tile, cols), lambda c, i: (c, i, 0))
+
     return pl.pallas_call(
         unfold_kernel,
         name="unfold",
         grid=(cores, steps),
-        out_shape=[jax.ShapeDtypeStruct((cores * half, shards * part), jnp.float32)] * 2,
-        in_specs=[block, block],
-        out_specs=[out, out],
+        out_shape=[jax.ShapeDtypeStruct((cores * half, wide), jnp.float32) for wide in wides],
+        in_specs=[block, block, flat(width), flat(qkv.shape[2])],
+        out_specs=[pl.BlockSpec((tile, wide), lambda c, i: (c * steps + i, 0)) for wide in wides],
         compiler_params=pltpu.CompilerParams(vmem_limit_bytes=32 * 2**20),
-    )(gate, up)
+    )(gate, up, out, qkv)
+
+
+def join_kernel(down_ref, out):
+    cols = down_ref.shape[2]
+    for c in range(2):
+        out[:, c * cols : (c + 1) * cols] = down_ref[c].astype(jnp.float32)
+
+
+def join(down):
+    cores, rows, cols = down.shape
+    tile = rows // 7
+    return pl.pallas_call(
+        join_kernel,
+        name="join",
+        grid=(rows // tile,),
+        out_shape=jax.ShapeDtypeStruct((rows, cores * cols), jnp.float32),
+        in_specs=[pl.BlockSpec((cores, tile, cols), lambda i: (0, i, 0))],
+        out_specs=pl.BlockSpec((tile, cores * cols), lambda i: (i, 0)),
+        compiler_params=pltpu.CompilerParams(vmem_limit_bytes=32 * 2**20),
+    )(down)
 
 
 def local(
@@ -1937,16 +2253,7 @@
     )
     cot_all = cot_all.reshape(row_len, model_width)
     normed_all = normed_all.reshape(row_len, model_width)
-    act_low, d_gate, d_up, norm_part, mlp_part = feed_forward(normed_all, cot_all, wgu, own_gu, w_down)
-    norm_part, act_low, d_gate, d_up = lax.optimization_barrier((norm_part, act_low, d_gate, d_up))
-    norm_part = norm_part.reshape(shard_count, tok_rows, model_width)
-    partial_value = scatter_relative([pick(norm_part, here ^ d) for d in range(shard_count)], "fsdp")
-    down_part = dot_left_t(act_low, cot_all).astype(low).reshape(2, part // 2, model_width)
-    gate_grads = [
-        dot_left_t(normed_all, d_value).astype(low).reshape(shard_count, 2, shard_rows // 2, part)
-        for d_value in (d_gate, d_up)
-    ]
-    mlp_part = mlp_part.reshape(shard_count, tok_rows, model_width)
+    act_low, d_gate, d_up, w_full = feed_forward(normed_all, cot_all, wgu, own_gu, w_down)
     results = epilogue(
         doc_lengths,
         piece_starts,
@@ -1957,28 +2264,28 @@
         hidden_in,
         out_grad,
         mid_state,
-        partial_value,
         normed_first,
         attn_low,
-        mlp_part,
         kv_full,
         wqkv_full,
         output_full,
-        down_part,
-        gate_grads[0],
-        gate_grads[1],
-    )
-    grad_input, sums, down_final, gate_final, up_final, attn_final = results[:6]
-    mlp_land = results[11]
-    output = mid_state + pick(mlp_part, here).astype(jnp.float32)
+        act_low,
+        d_gate,
+        d_up,
+        normed_all,
+        cot_all,
+        w_full,
+        w_down,
+    )
+    grad_input, sums, down_final, gate_final, up_final, out_final, qkv_final = results[:7]
+    mlp_land = results[14]
+    output = mid_state + results[15].astype(jnp.float32)
     for d in range(shard_count - 1):
         output = output + mlp_land[d].astype(jnp.float32)
-    down_sums = down_final.reshape(part, model_width).astype(jnp.float32)
-    grad_gate, grad_up = unfold(gate_final, up_final)
-    attn_sums = attn_final.reshape(shard_rows, -1).astype(jnp.float32)
-    ends = [0, model_width, model_width + kv_width, model_width + 2 * kv_width, 2 * (model_width + kv_width)]
-    grad_query, grad_key, grad_value, grad_output = (attn_sums[:, ends[i] : ends[i + 1]] for i in range(4))
-
+    down_sums = join(down_final)
+    grad_gate, grad_up, grad_output, grad_query, grad_key, grad_value = unfold(
+        gate_final, up_final, out_final, qkv_final
+    )
     def shard_of(row, first, size):
         return lax.dynamic_slice(sums, (row, first + here * (size // shard_count)), (1, size // shard_count))[0]
 

time: 720 us -> 578 us (0.80)
  Pallas kernels: 598 us -> 551 us
  matrix products: 39 us -> 0 us
  local copies, waits for them, and re-layouts: 32.8 us -> 7.53 us
  other arithmetic: 29.6 us -> 11.1 us
    dot_general x3 -> x0, matrix products: 39 us -> none  [dot_left_t(): lax.dot_general(left, right, (((0,), (0,)), ((), ())), preferred_element_...]
    pallas_call x1, Pallas kernels: 67.7 us -> 41.1 us  [feed_forward(): pl.pallas_call(feed_forward_kernel, name='feed_forward', grid=(rows // ti...]
    pallas_call x1, Pallas kernels: 178 us -> 157 us  [prologue(): pl.pallas_call(prologue_kernel, name='prologue', out_shape=(shape((shards...]
    convert_element_type x2 -> x0, local copies, waits for them, and re-layouts: 20.4 us -> none  [local_fast(): dot_left_t(normed_all, d_value).astype(low)]
    convert_element_type x3 -> x0, other arithmetic: 15.2 us -> none  [the longest x1 10.8 us: local_fast(): down_sums = down_final.reshape(part, model_width).astype(jnp.float32)]
  transfers between devices with their start and end apart: 6 -> 0, of which waited for: 1 -> 0; matrix products, arithmetic and copies ran while one was open for 9% -> 0% of each run, Pallas kernels for 0% -> 0%
where the time goes in v5:
time: 578 us; the launch traced here: 571 us
  Pallas kernels  551 us (95%)
  other arithmetic  11.1 us (2%)
  local copies, waits for them, and re-layouts  7.53 us (1%)
    pallas_call x1, Pallas kernels, epilogue(): pl.pallas_call(epilogue_kernel, name='epilogue', out_shape=tuple(outs), i...  334 us
    pallas_call x1, Pallas kernels, prologue(): pl.pallas_call(prologue_kernel, name='prologue', out_shape=(shape((shards...  157 us
    pallas_call x1, Pallas kernels, feed_forward(): pl.pallas_call(feed_forward_kernel, name='feed_forward', grid=(rows // ti...  41.1 us

profile of v5, /device:TPU:0, one launch (start us, length us, event | category | flops | bytes accessed | tf_op | source)
XLA Modules:
  0.0 570.8 jit_solution(8674854094551667153)
XLA Ops:
  0.7 0.7 bitcast_convert_fusion
  1.3 0.1 pad_maximum_fusion.1
  1.4 0.7 broadcast_in_dim.51
  2.1 0.7 broadcast_in_dim.52
  2.8 0.7 broadcast_in_dim.53
  3.4 0.6 broadcast_in_dim.50.inverse_ref
  4.1 0.2 dynamic_update_slice.20
  4.3 0.7 fusion.2
  5.0 0.1 add.42
  5.1 0.7 concatenate.9.vec_ref
  5.8 2.9 pad_maximum_fusion.wqkv_ref
  8.7 157.0 %prologue.1 = (bf16[4,320,1536]{2,1,0:T(8,128)(2,1)}, bf16[4,320,1536]{2,1,0:T(8,128)(2,1)}, bf16[2,4,3,2,48,2240]{5,4,3,2,1,0:T(8,128)(2,1)}, bf16[2,384,2240]{...) custom-call(s32[1,8]{1,0:T(1,128)} %lengths_ref.3, ...), custom_call_target="tpu_custom_call" | custom-call | tf_op jit(solution)/shard_map/prologue/pallas_call | solution.py:637
  165.7 41.1 %feed_forward.1 = (bf16[1280,2240]{1,0:T(8,128)(2,1)}, bf16[1280,2240]{1,0:T(8,128)(2,1)}, bf16[1280,2240]{1,0:T(8,128)(2,1)}, bf16[2,1536,2240]{2,1,0:T(8,128)(2,1)}) custom-call(bf16[1280,1536]{1,0:T(8,128)(2,1)} %bitcast.25, bf16[1280,1536]{1,0:T(8,128)(2,1)} %bitcast.27, bf16[2,4,3,2,48,2240]{5,4,3,2,1,0:T(8,128)(2,1)} %get-tuple-element.59.wgu, ...), custom_call_target="tpu_custom_call" | custom-call | flops 26424115200 | bytes 34406400 | tf_op jit(solution)/shard_map/feed_forward/pallas_call | solution.py:1804
  206.8 334.4 %epilogue.1 = (f32[320,1536]{1,0:T(8,128)}, f32[8,1536]{1,0:T(8,128)}, bf16[2,2240,768]{2,1,0:T(8,128)(2,1)}, bf16[2,4,192,2240]{3,2,1,0:T(8,128)(2,1)}, bf16[2,...) custom-call(s32[1,8]{1,0:T(1,128)} %lengths_ref.3, ...), custom_call_target="tpu_custom_call" | custom-call | tf_op jit(solution)/shard_map/epilogue/pallas_call | solution.py:1678
  541.2 0.0 copy-start
  541.2 0.0 slice-start
  541.2 0.0 slice-start.2
  541.2 4.7 convert_add_fusion
  545.9 2.1 fusion.1
  548.0 1.5 dynamic-slice_reduce_fusion
  549.5 0.0 copy-done
  549.5 0.0 slice-start.1
  549.5 0.0 slice-start.3
  549.5 0.0 copy-start.1
  549.5 0.0 copy-start.2
  549.5 7.0 %join.1 = f32[2240,1536]{1,0:T(8,128)} custom-call(bf16[2,2240,768]{2,1,0:T(8,128)(2,1)S(1)} %copy-done), custom_call_target="tpu_custom_call" | custom-call | tf_op jit(solution)/shard_map/join/pallas_call | solution.py:1867
  556.5 0.0 slice-done
  556.6 0.0 slice-done.2
  556.6 0.0 slice-done.1
  556.6 0.0 slice-done.3
  556.6 0.5 copy-done.1
  557.0 0.6 copy-done.2
  557.7 0.0 copy-start.3
  557.7 11.4 %unfold.1 = (f32[384,8960]{1,0:T(8,128)}, f32[384,8960]{1,0:T(8,128)}, f32[384,1536]{1,0:T(8,128)}, f32[384,1536]{1,0:T(8,128)}, f32[384,256]{1,0:T(8,128)}, /*index=5*/f32[384,256]{1,0:T(8,128)}) custom-call(bf16[2,4,192,2240]{3,2,1,0:T(8,128)(2,1)S(1)} %bitcast.22, bf16[2,4,192,2240]{3,2,1,0:T(8,128)(2,1)S(1)} %bitcast.24, ...), custom_call_target="tpu_custom_call" | custom-call | tf_op jit(solution)/shard_map/unfold/pallas_call | solution.py:1847
  569.1 0.0 copy-done.3
  569.1 1.3 copy.36
  (11 shorter events, 0.1 us)
Async XLA Ops:
  541.2 8.3 %copy-start = (bf16[2,2240,768]{2,1,0:T(8,128)(2,1)S(1)}, bf16[2,2240,768]{2,1,0:T(8,128)(2,1)}, u32[]{:S(2)}) copy-start(bf16[2,2240,768]{2,1,0:T(8,128)(2,1)} %get-tuple-element.79.down_ref) | copy-start | bytes 20643844
  541.2 15.3 %slice-start = ((s8[7077888]{0:T(1024)(128)(4,1)}), s8[4194304]{0:T(1024)(128)(4,1)S(1)}, s32[]{:S(2)}) async-start(s8[7077888]{0:T(1024)(128)(4,1)} %bitcast.21), calls=%async_computation | async-start | bytes 8388608
  541.2 15.3 %slice-start.2 = ((s8[7077888]{0:T(1024)(128)(4,1)}), s8[4194304]{0:T(1024)(128)(4,1)S(1)}, s32[]{:S(2)}) async-start(s8[7077888]{0:T(1024)(128)(4,1)} %bitcast.23), calls=%async_computation.2 | async-start | bytes 8388608
  549.5 7.1 %slice-start.1 = ((s8[7077888]{0:T(1024)(128)(4,1)}), s8[2883584]{0:T(1024)(128)(4,1)S(1)}, s32[]{:S(2)}) async-start(s8[7077888]{0:T(1024)(128)(4,1)} %bitcast.21), calls=%async_computation.1 | async-start | bytes 5767168
  549.5 7.1 %slice-start.3 = ((s8[7077888]{0:T(1024)(128)(4,1)}), s8[2883584]{0:T(1024)(128)(4,1)S(1)}, s32[]{:S(2)}) async-start(s8[7077888]{0:T(1024)(128)(4,1)} %bitcast.23), calls=%async_computation.3 | async-start | bytes 5767168
  549.5 7.5 %copy-start.1 = (bf16[2,192,2048]{2,1,0:T(8,128)(2,1)S(1)}, bf16[2,192,2048]{2,1,0:T(8,128)(2,1)}, u32[]{:S(2)}) copy-start(bf16[2,192,2048]{2,1,0:T(8,128)(2,1)} %get-tuple-element.71.qkv_ref) | copy-start | bytes 4718596
  549.5 8.2 %copy-start.2 = (bf16[2,192,1536]{2,1,0:T(8,128)(2,1)S(1)}, bf16[2,192,1536]{2,1,0:T(8,128)(2,1)}, u32[]{:S(2)}) copy-start(bf16[2,192,1536]{2,1,0:T(8,128)(2,1)} %get-tuple-element.70.out_ref) | copy-start | bytes 3538948
  557.7 11.4 %copy-start.3 = (f32[320,1536]{1,0:T(8,128)S(1)}, f32[320,1536]{1,0:T(8,128)}, u32[]{:S(2)}) copy-start(f32[320,1536]{1,0:T(8,128)} %get-tuple-element.100) | copy-start | bytes 5898244

commit v6 on v5

--- a/solution.py
+++ b/solution.py
@@ -1,5 +1,6 @@
 import jax
 import jax.numpy as jnp
+import numpy as np
 from jax import lax
 from jax.experimental import pallas as pl
 from jax.experimental.pallas import tpu as pltpu
@@ -1742,16 +1743,15 @@
 
 
 def feed_forward_kernel(
-    x_ref, cot_ref, wgu, own_gu, down_hbm, act_ref, dgate_ref, dup_ref, w_hbm, w_ref, down_ref, sems
+    x_ref, cot_ref, wgu, own_gu, down_hbm, act_ref, dgate_ref, dup_ref, w_hbm, w_ref, down_ref, d_act_ref, sems
 ):
     f32, bf16 = jnp.float32, jnp.bfloat16
     cores, line, others, kinds, thin, part = wgu.shape
     shard = own_gu.shape[1]
 
-    @pl.when(pl.program_id(0) == 0)
-    def _():
+    def weight_copies():
         near = Place().near
-        copies = [pltpu.make_async_copy(down_hbm, down_ref, sems.at[0])]
+        copies = []
         for g in range(kinds):
             at = pl.multiple_of(near[0] * shard, shard)
             copies.append(
@@ -1769,18 +1769,31 @@
                             )
                         )
                         n += 1
-        for copy in copies:
+        return copies
+
+    @pl.when(pl.program_id(0) == 0)
+    def _():
+        down_copy = pltpu.make_async_copy(down_hbm, down_ref, sems.at[0])
+        down_copy.start()
+        for copy in weight_copies():
             copy.start()
-        for copy in copies:
+        down_copy.wait()
+
+    x, cot = x_ref[...], cot_ref[...]
+    pieces = [slice(lo, min(lo + 512, part)) for lo in range(0, part, 512)]
+    for at in pieces:
+        d_act_ref[:, at] = dot_f32(cot, down_ref[at, :], ((1,), (1,)))
+
+    @pl.when(pl.program_id(0) == 0)
+    def _():
+        for copy in weight_copies():
             copy.wait()
         pltpu.make_async_copy(w_ref, w_hbm, sems.at[0]).start()
 
-    x, cot = x_ref[...], cot_ref[...]
-    for lo in range(0, part, 512):
-        at = slice(lo, min(lo + 512, part))
+    for at in pieces:
         gate = dot_f32(x, w_ref[0, :, at])
         up = dot_f32(x, w_ref[1, :, at])
-        d_act = dot_f32(cot, down_ref[at, :], ((1,), (1,)))
+        d_act = d_act_ref[:, at]
         sig = jax.nn.sigmoid(gate)
         silu = gate * sig
         act_ref[:, at] = (silu * up).astype(bf16)
@@ -1811,6 +1824,7 @@
         scratch_shapes=[
             pltpu.VMEM((2, width, part), bf16),
             pltpu.VMEM((part, width), bf16),
+            pltpu.VMEM((tile, part), jnp.float32),
             pltpu.SemaphoreType.DMA((3 + wgu.shape[0] * wgu.shape[1] * wgu.shape[2] * wgu.shape[3],)),
         ],
         compiler_params=pltpu.CompilerParams(vmem_limit_bytes=62 * 2**20),
@@ -2204,9 +2218,8 @@
     part = ff_width // shard_count
     shard_rows = model_width // shard_count
     thin = shard_rows // 2 // line
-    halves = jnp.arange(0, HDIM, 2).astype(jnp.float32) / HDIM
-    inverse = rope_base ** (-halves)
-    inverse = jnp.broadcast_to(jnp.concatenate([inverse, inverse])[None], (8, HDIM))
+    inverse = rope_base ** (-np.arange(0, HDIM, 2) / HDIM)
+    inverse = np.tile(np.concatenate([inverse, inverse]).astype(np.float32)[None], (8, 1))
 
     def spread(vector, first, size):
         zeros = jnp.zeros((1, size), jnp.float32)

time: 578 us -> 576 us (level)
  no operation moved by 1% of the time
where the time goes in v6:
time: 576 us; the launch traced here: 569 us
  Pallas kernels  550 us (95%)
  other arithmetic  11 us (2%)
  local copies, waits for them, and re-layouts  6.94 us (1%)
    pallas_call x1, Pallas kernels, epilogue(): pl.pallas_call(epilogue_kernel, name='epilogue', out_shape=tuple(outs), i...  334 us
    pallas_call x1, Pallas kernels, prologue(): pl.pallas_call(prologue_kernel, name='prologue', out_shape=(shape((shards...  157 us
    pallas_call x1, Pallas kernels, feed_forward(): pl.pallas_call(feed_forward_kernel, name='feed_forward', grid=(rows // ti...  39.9 us

profile of v6, /device:TPU:0, one launch (start us, length us, event | category | flops | bytes accessed | tf_op | source)
XLA Modules:
  0.0 568.9 jit_solution(7433173841544708421)
XLA Ops:
  0.7 0.7 bitcast_convert_fusion
  1.3 0.7 broadcast_in_dim.44
  2.0 0.7 broadcast_in_dim.45
  2.7 0.7 broadcast_in_dim.46
  3.4 0.2 dynamic_update_slice.20
  3.6 0.7 fusion.2
  4.3 0.1 add.42
  4.4 0.7 concatenate.6.vec_ref
  5.1 2.9 pad_maximum_fusion.wqkv_ref
  8.0 157.0 %prologue.1 = (bf16[4,320,1536]{2,1,0:T(8,128)(2,1)}, bf16[4,320,1536]{2,1,0:T(8,128)(2,1)}, bf16[2,4,3,2,48,2240]{5,4,3,2,1,0:T(8,128)(2,1)}, bf16[2,384,2240]{...) custom-call(s32[1,8]{1,0:T(1,128)} %lengths_ref.3, ...), custom_call_target="tpu_custom_call" | custom-call | tf_op jit(solution)/shard_map/prologue/pallas_call | solution.py:638
  165.0 39.9 %feed_forward.1 = (bf16[1280,2240]{1,0:T(8,128)(2,1)}, bf16[1280,2240]{1,0:T(8,128)(2,1)}, bf16[1280,2240]{1,0:T(8,128)(2,1)}, bf16[2,1536,2240]{2,1,0:T(8,128)(2,1)}) custom-call(bf16[1280,1536]{1,0:T(8,128)(2,1)} %bitcast.25, bf16[1280,1536]{1,0:T(8,128)(2,1)} %bitcast.27, bf16[2,4,3,2,48,2240]{5,4,3,2,1,0:T(8,128)(2,1)} %get-tuple-element.59.wgu, ...), custom_call_target="tpu_custom_call" | custom-call | flops 26424115200 | bytes 34406400 | tf_op jit(solution)/shard_map/feed_forward/pallas_call | solution.py:1817
  204.9 334.3 %epilogue.1 = (f32[320,1536]{1,0:T(8,128)}, f32[8,1536]{1,0:T(8,128)}, bf16[2,2240,768]{2,1,0:T(8,128)(2,1)}, bf16[2,4,192,2240]{3,2,1,0:T(8,128)(2,1)}, bf16[2,...) custom-call(s32[1,8]{1,0:T(1,128)} %lengths_ref.3, ...), custom_call_target="tpu_custom_call" | custom-call | tf_op jit(solution)/shard_map/epilogue/pallas_call | solution.py:1679
  539.2 0.0 copy-start
  539.2 0.0 slice-start
  539.2 0.0 slice-start.2
  539.3 4.7 convert_add_fusion
  544.0 2.1 fusion.1
  546.0 1.5 dynamic-slice_reduce_fusion
  547.5 0.0 copy-done
  547.5 0.0 slice-start.1
  547.5 0.0 slice-start.3
  547.5 0.0 copy-start.1
  547.5 0.0 copy-start.2
  547.6 7.0 %join.1 = f32[2240,1536]{1,0:T(8,128)} custom-call(bf16[2,2240,768]{2,1,0:T(8,128)(2,1)S(1)} %copy-done), custom_call_target="tpu_custom_call" | custom-call | tf_op jit(solution)/shard_map/join/pallas_call | solution.py:1881
  554.6 0.0 slice-done
  554.6 0.0 slice-done.2
  554.6 0.0 slice-done.1
  554.6 0.0 slice-done.3
  554.6 0.5 copy-done.1
  555.1 0.6 copy-done.2
  555.7 0.0 copy-start.3
  555.7 11.4 %unfold.1 = (f32[384,8960]{1,0:T(8,128)}, f32[384,8960]{1,0:T(8,128)}, f32[384,1536]{1,0:T(8,128)}, f32[384,1536]{1,0:T(8,128)}, f32[384,256]{1,0:T(8,128)}, /*index=5*/f32[384,256]{1,0:T(8,128)}) custom-call(bf16[2,4,192,2240]{3,2,1,0:T(8,128)(2,1)S(1)} %bitcast.22, bf16[2,4,192,2240]{3,2,1,0:T(8,128)(2,1)S(1)} %bitcast.24, ...), custom_call_target="tpu_custom_call" | custom-call | tf_op jit(solution)/shard_map/unfold/pallas_call | solution.py:1861
  567.1 0.0 copy-done.3
  567.1 1.3 copy.37
  (10 shorter events, 0.1 us)
Async XLA Ops:
  539.2 8.3 %copy-start = (bf16[2,2240,768]{2,1,0:T(8,128)(2,1)S(1)}, bf16[2,2240,768]{2,1,0:T(8,128)(2,1)}, u32[]{:S(2)}) copy-start(bf16[2,2240,768]{2,1,0:T(8,128)(2,1)} %get-tuple-element.79.down_ref) | copy-start | bytes 20643844
  539.2 15.3 %slice-start = ((s8[7077888]{0:T(1024)(128)(4,1)}), s8[4194304]{0:T(1024)(128)(4,1)S(1)}, s32[]{:S(2)}) async-start(s8[7077888]{0:T(1024)(128)(4,1)} %bitcast.21), calls=%async_computation | async-start | bytes 8388608
  539.2 15.3 %slice-start.2 = ((s8[7077888]{0:T(1024)(128)(4,1)}), s8[4194304]{0:T(1024)(128)(4,1)S(1)}, s32[]{:S(2)}) async-start(s8[7077888]{0:T(1024)(128)(4,1)} %bitcast.23), calls=%async_computation.2 | async-start | bytes 8388608
  547.5 7.1 %slice-start.1 = ((s8[7077888]{0:T(1024)(128)(4,1)}), s8[2883584]{0:T(1024)(128)(4,1)S(1)}, s32[]{:S(2)}) async-start(s8[7077888]{0:T(1024)(128)(4,1)} %bitcast.21), calls=%async_computation.1 | async-start | bytes 5767168
  547.5 7.1 %slice-start.3 = ((s8[7077888]{0:T(1024)(128)(4,1)}), s8[2883584]{0:T(1024)(128)(4,1)S(1)}, s32[]{:S(2)}) async-start(s8[7077888]{0:T(1024)(128)(4,1)} %bitcast.23), calls=%async_computation.3 | async-start | bytes 5767168
  547.5 7.5 %copy-start.1 = (bf16[2,192,2048]{2,1,0:T(8,128)(2,1)S(1)}, bf16[2,192,2048]{2,1,0:T(8,128)(2,1)}, u32[]{:S(2)}) copy-start(bf16[2,192,2048]{2,1,0:T(8,128)(2,1)} %get-tuple-element.71.qkv_ref) | copy-start | bytes 4718596
  547.5 8.2 %copy-start.2 = (bf16[2,192,1536]{2,1,0:T(8,128)(2,1)S(1)}, bf16[2,192,1536]{2,1,0:T(8,128)(2,1)}, u32[]{:S(2)}) copy-start(bf16[2,192,1536]{2,1,0:T(8,128)(2,1)} %get-tuple-element.70.out_ref) | copy-start | bytes 3538948
  555.7 11.4 %copy-start.3 = (f32[320,1536]{1,0:T(8,128)S(1)}, f32[320,1536]{1,0:T(8,128)}, u32[]{:S(2)}) copy-start(f32[320,1536]{1,0:T(8,128)} %get-tuple-element.100) | copy-start | bytes 5898244
